TPU v7x, 32 devices: a whole 2x2x4 slice. The times are simulated.
32 devices in a mesh: grp: 4 (over y, x), fsdp: 8 (over z, core).
Axes of the slice: x: 2, y: 2, z: 4, core: 2. Of those that a mesh axis runs over, the one named last changes fastest.
Arguments:
- prompt_in: bfloat16 [3, 16384, 768], P(None, ('grp', 'fsdp')), may hold values from -6 to 6
- cont_in: bfloat16 [3, 8192, 768], P(None, ('grp', 'fsdp')), may hold values from -6 to 6
- prompt_cot: bfloat16 [3, 16384, 768], P(None, ('grp', 'fsdp')), may hold values from -6 to 6
- cont_cot: bfloat16 [3, 8192, 768], P(None, ('grp', 'fsdp')), may hold values from -6 to 6
- cont_prompt: int32 [3, 4, 8], P(None, 'grp', 'fsdp'), may hold values from 0 to 1
- cont_len: int32 [3, 4, 8], P(None, 'grp', 'fsdp'), may hold values from 1 to 256, 1280 in all within a row
- ln1_gain: float32 [768], P(('grp', 'fsdp')), may hold values from 0.5 to 1.5
- ln1_bias: float32 [768], P(('grp', 'fsdp')), may hold values from -1 to 1
- attn_weight: float32 [768, 2304], P(('grp', 'fsdp')), may hold values from -0.3125 to 0.3125
- attn_bias: float32 [2, 768], P(None, ('grp', 'fsdp')), may hold values from -1 to 1
- proj_weight: float32 [768, 768], P(('grp', 'fsdp')), may hold values from -0.875 to 0.875
- proj_bias: float32 [768], P(('grp', 'fsdp')), may hold values from -1 to 1
- ln2_gain: float32 [768], P(('grp', 'fsdp')), may hold values from 0.5 to 1.5
- ln2_bias: float32 [768], P(('grp', 'fsdp')), may hold values from -1 to 1
- fc_weight: float32 [768, 3072], P(('grp', 'fsdp')), may hold values from -0.21875 to 0.21875
- fc_bias: float32 [3072], P(('grp', 'fsdp')), may hold values from -1 to 1
- out_weight: float32 [3072, 768], P(('grp', 'fsdp')), may hold values from -0.109375 to 0.109375
- out_bias: float32 [768], P(('grp', 'fsdp')), may hold values from -2 to 2
Outputs:
- prompt_out: bfloat16 [3, 16384, 768], P(None, ('grp', 'fsdp'))
- cont_out: bfloat16 [3, 8192, 768], P(None, ('grp', 'fsdp'))
- prompt_grad: bfloat16 [3, 16384, 768], P(None, ('grp', 'fsdp'))
- cont_grad: bfloat16 [3, 8192, 768], P(None, ('grp', 'fsdp'))
- ln1_gain_grad: float32 [768], P(('grp', 'fsdp'))
- ln1_bias_grad: float32 [768], P(('grp', 'fsdp'))
- attn_weight_grad: float32 [768, 2304], P(('grp', 'fsdp'))
- attn_bias_grad: float32 [2, 768], P(None, ('grp', 'fsdp'))
- proj_weight_grad: float32 [768, 768], P(('grp', 'fsdp'))
- proj_bias_grad: float32 [768], P(('grp', 'fsdp'))
- ln2_gain_grad: float32 [768], P(('grp', 'fsdp'))
- ln2_bias_grad: float32 [768], P(('grp', 'fsdp'))
- fc_weight_grad: float32 [768, 3072], P(('grp', 'fsdp'))
- fc_bias_grad: float32 [3072], P(('grp', 'fsdp'))
- out_weight_grad: float32 [3072, 768], P(('grp', 'fsdp'))
- out_bias_grad: float32 [768], P(('grp', 'fsdp'))
Inputs may be any that keep to these rules, and one draw needn't show every extreme that they name: `cont_len`: in each micro-batch and group the longest continuation has 256 live rows.
All inputs are finite; a program needn't handle non-finite values.
Results may differ from a plain program's by a relative error of at most 0.039.
Values may be sent and summed in bfloat16 or wider, within the bound.
A program may use at most 1 GiB of HBM per device.

v0:
```python
import jax
import jax.numpy as jnp
from jax import lax
from jax.sharding import PartitionSpec as P

D = 768
HEADS = 12
HEAD_DIM = 64
MB = 3
NPR = 2
PLEN = 2048


EPSILON = 1e-05
MASKED = -1e30


def layer_norm(value, gain, shift):
    center = value - jnp.mean(value, axis=-1, keepdims=True)
    spread = jnp.mean(center * center, axis=-1, keepdims=True)
    return center * lax.rsqrt(spread + EPSILON) * gain + shift


def gelu_tanh(value):
    return jax.nn.gelu(value, approximate=True)


def split_heads(value):
    return value.reshape(value.shape[0], value.shape[1], HEADS, HEAD_DIM)


def scores_of(query, keys, allowed):
    raw = jnp.einsum(
        "bqhd,bkhd->bhqk", split_heads(query), split_heads(keys), preferred_element_type=jnp.float32
    )
    return jnp.where(allowed[:, None], raw * HEAD_DIM ** (-0.5), MASKED)


def attend_forward(query, keys, values, allowed):
    scores = scores_of(query, keys, allowed)
    ceiling = jnp.max(scores, axis=-1, keepdims=True)
    powers = jnp.exp(scores - ceiling)
    total = jnp.sum(powers, axis=-1, keepdims=True)
    probs = (powers / total).astype(jnp.bfloat16)
    mixed = jnp.einsum(
        "bhqk,bkhd->bqhd", probs, split_heads(values), preferred_element_type=jnp.float32
    )
    return (mixed.reshape(query.shape[0], query.shape[1], D), ceiling + jnp.log(total))


def attend_backward(query, keys, values, allowed, log_total, grad_mixed, key_from):
    scores = scores_of(query, keys, allowed)
    probs = jnp.exp(scores - log_total)
    heads_query = split_heads(query)
    heads_keys = split_heads(keys)
    heads_grad = split_heads(grad_mixed)
    grad_probs = jnp.einsum(
        "bqhd,bkhd->bhqk", heads_grad, split_heads(values), preferred_element_type=jnp.float32
    )
    inner = jnp.sum(probs * grad_probs, axis=-1, keepdims=True)
    grad_scores = (probs * (grad_probs - inner)).astype(jnp.bfloat16)
    scale = HEAD_DIM ** (-0.5)
    grad_query = (
        jnp.einsum("bhqk,bkhd->bqhd", grad_scores, heads_keys, preferred_element_type=jnp.float32)
        * scale
    )
    grad_keys = (
        jnp.einsum("bhqk,bqhd->bkhd", grad_scores, heads_query, preferred_element_type=jnp.float32)
        * scale
    )
    grad_values = jnp.einsum(
        "bhqk,bqhd->bkhd",
        probs.astype(jnp.bfloat16),
        heads_grad,
        preferred_element_type=jnp.float32,
    )
    batch, rows, count = (query.shape[0], query.shape[1], keys.shape[1] - key_from)
    return (
        grad_query.reshape(batch, rows, D),
        grad_keys.reshape(batch, count, D),
        grad_values.reshape(batch, count, D),
        inner,
    )


def fetch_weights(masters):
    gain_a, shift_a, w_attn, b_attn, w_proj, b_proj, gain_b, shift_b, w_fc, b_fc, w_out, b_out = (
        masters
    )
    return (
        lax.all_gather(gain_a.astype(jnp.bfloat16), ("grp", "fsdp"), axis=0, tiled=True),
        lax.all_gather(shift_a.astype(jnp.bfloat16), ("grp", "fsdp"), axis=0, tiled=True),
        lax.all_gather(w_attn.astype(jnp.bfloat16), ("grp", "fsdp"), axis=0, tiled=True),
        lax.all_gather(b_attn.astype(jnp.bfloat16), ("grp", "fsdp"), axis=1, tiled=True),
        lax.all_gather(w_proj.astype(jnp.bfloat16), ("grp", "fsdp"), axis=0, tiled=True),
        lax.all_gather(b_proj.astype(jnp.bfloat16), ("grp", "fsdp"), axis=0, tiled=True),
        lax.all_gather(gain_b.astype(jnp.bfloat16), ("grp", "fsdp"), axis=0, tiled=True),
        lax.all_gather(shift_b.astype(jnp.bfloat16), ("grp", "fsdp"), axis=0, tiled=True),
        lax.all_gather(w_fc.astype(jnp.bfloat16), ("grp", "fsdp"), axis=0, tiled=True),
        lax.all_gather(b_fc.astype(jnp.bfloat16), ("grp", "fsdp"), axis=0, tiled=True),
        lax.all_gather(w_out.astype(jnp.bfloat16), ("grp", "fsdp"), axis=0, tiled=True),
        lax.all_gather(b_out.astype(jnp.bfloat16), ("grp", "fsdp"), axis=0, tiled=True),
    )


def fetch_again(masters):
    gain_a, shift_a, w_attn, b_attn, w_proj, b_proj, gain_b, shift_b, w_fc, b_fc, w_out, b_out = (
        masters
    )
    return (
        lax.all_gather(gain_a.astype(jnp.bfloat16), ("grp", "fsdp"), axis=0, tiled=True),
        lax.all_gather(shift_a.astype(jnp.bfloat16), ("grp", "fsdp"), axis=0, tiled=True),
        lax.all_gather(w_attn.astype(jnp.bfloat16), ("grp", "fsdp"), axis=0, tiled=True),
        lax.all_gather(b_attn.astype(jnp.bfloat16), ("grp", "fsdp"), axis=1, tiled=True),
        lax.all_gather(w_proj.astype(jnp.bfloat16), ("grp", "fsdp"), axis=0, tiled=True),
        lax.all_gather(b_proj.astype(jnp.bfloat16), ("grp", "fsdp"), axis=0, tiled=True),
        lax.all_gather(gain_b.astype(jnp.bfloat16), ("grp", "fsdp"), axis=0, tiled=True),
        lax.all_gather(shift_b.astype(jnp.bfloat16), ("grp", "fsdp"), axis=0, tiled=True),
        lax.all_gather(w_fc.astype(jnp.bfloat16), ("grp", "fsdp"), axis=0, tiled=True),
        lax.all_gather(b_fc.astype(jnp.bfloat16), ("grp", "fsdp"), axis=0, tiled=True),
        lax.all_gather(w_out.astype(jnp.bfloat16), ("grp", "fsdp"), axis=0, tiled=True),
        lax.all_gather(b_out.astype(jnp.bfloat16), ("grp", "fsdp"), axis=0, tiled=True),
    )


def sum_end(grads):
    return (
        lax.psum_scatter(grads[0], ("grp", "fsdp"), scatter_dimension=0, tiled=True),
        lax.psum_scatter(grads[1], ("grp", "fsdp"), scatter_dimension=0, tiled=True),
        lax.psum_scatter(grads[2], ("grp", "fsdp"), scatter_dimension=0, tiled=True),
        lax.psum_scatter(grads[3], ("grp", "fsdp"), scatter_dimension=1, tiled=True),
        lax.psum_scatter(grads[4], ("grp", "fsdp"), scatter_dimension=0, tiled=True),
        lax.psum_scatter(grads[5], ("grp", "fsdp"), scatter_dimension=0, tiled=True),
        lax.psum_scatter(grads[6], ("grp", "fsdp"), scatter_dimension=0, tiled=True),
        lax.psum_scatter(grads[7], ("grp", "fsdp"), scatter_dimension=0, tiled=True),
        lax.psum_scatter(grads[8], ("grp", "fsdp"), scatter_dimension=0, tiled=True),
        lax.psum_scatter(grads[9], ("grp", "fsdp"), scatter_dimension=0, tiled=True),
        lax.psum_scatter(grads[10], ("grp", "fsdp"), scatter_dimension=0, tiled=True),
        lax.psum_scatter(grads[11], ("grp", "fsdp"), scatter_dimension=0, tiled=True),
    )


def row_sum(value):
    return jnp.sum(value.astype(jnp.float32), axis=0)


def run_batch(
    masters, prompt_rows, cont_rows, prompt_seed, cont_seed, follows, lengths, prompt_index, offset
):
    used = fetch_weights(masters)
    gain_first = used[0].astype(jnp.float32)
    shift_first = used[1].astype(jnp.float32)
    w_attn, b_attn, w_proj, b_proj = (
        used[2],
        used[3].astype(jnp.float32),
        used[4],
        used[5].astype(jnp.float32),
    )
    gain_second = used[6].astype(jnp.float32)
    shift_second = used[7].astype(jnp.float32)
    w_fc, b_fc, w_out, b_out = (
        used[8],
        used[9].astype(jnp.float32),
        used[10],
        used[11].astype(jnp.float32),
    )
    prow = prompt_rows.shape[0]
    crow = cont_rows.shape[0]
    conts = follows.shape[0]
    clen = crow // conts
    inputs = jnp.concatenate([prompt_rows, cont_rows], axis=0).astype(jnp.float32)
    live = (jnp.arange(clen)[None, :] < lengths[:, None]).astype(jnp.float32).reshape(crow)
    valid = jnp.concatenate([jnp.ones((prow,), jnp.float32), live])[:, None]
    normed_first, pull_first = jax.vjp(layer_norm, inputs, gain_first, shift_first)
    normed = normed_first.astype(jnp.bfloat16)
    projected = jnp.dot(normed, w_attn, preferred_element_type=jnp.float32)
    query = (projected[:, :D] + b_attn[0]).astype(jnp.bfloat16)
    keys = projected[:, D : 2 * D].astype(jnp.bfloat16)
    values = (projected[:, 2 * D :] + b_attn[1]).astype(jnp.bfloat16)
    all_keys, all_values = (
        lax.all_gather(keys[:prow], "fsdp", axis=0, tiled=True),
        lax.all_gather(values[:prow], "fsdp", axis=0, tiled=True),
    )
    own_keys = lax.dynamic_slice_in_dim(all_keys, prompt_index * PLEN, PLEN, 0)[None]
    own_values = lax.dynamic_slice_in_dim(all_values, prompt_index * PLEN, PLEN, 0)[None]
    places = offset + jnp.arange(prow)
    prompt_allowed = (jnp.arange(PLEN)[None, :] <= places[:, None])[None]
    prompt_query = query[None, :prow]
    prompt_mix, prompt_total = attend_forward(prompt_query, own_keys, own_values, prompt_allowed)
    chosen_keys = jnp.take(all_keys.reshape(NPR, PLEN, D), follows, axis=0)
    chosen_values = jnp.take(all_values.reshape(NPR, PLEN, D), follows, axis=0)
    cont_keys = jnp.concatenate([chosen_keys, keys[prow:].reshape(conts, clen, D)], axis=1)
    cont_values = jnp.concatenate([chosen_values, values[prow:].reshape(conts, clen, D)], axis=1)
    causal = jnp.arange(clen)[None, :] <= jnp.arange(clen)[:, None]
    cont_allowed = jnp.concatenate([jnp.ones((clen, PLEN), jnp.bool_), causal], axis=1)[None]
    cont_query = query[prow:].reshape(conts, clen, D)
    cont_mix, cont_total = attend_forward(cont_query, cont_keys, cont_values, cont_allowed)
    mixed = jnp.concatenate([prompt_mix[0], cont_mix.reshape(crow, D)], axis=0).astype(jnp.bfloat16)
    branch = jnp.dot(mixed, w_proj, preferred_element_type=jnp.float32) + b_proj
    hidden = inputs + valid * branch
    normed_second, pull_second = jax.vjp(layer_norm, hidden, gain_second, shift_second)
    second = normed_second.astype(jnp.bfloat16)
    inner = jnp.dot(second, w_fc, preferred_element_type=jnp.float32) + b_fc
    active_full, pull_gelu = jax.vjp(gelu_tanh, inner)
    active = active_full.astype(jnp.bfloat16)
    result = jnp.dot(active, w_out, preferred_element_type=jnp.float32) + b_out
    final = (hidden + valid * result).astype(jnp.bfloat16)
    back = fetch_again(masters)
    w_attn, w_proj, w_fc, w_out = (back[2], back[4], back[8], back[10])
    grad_out = jnp.concatenate([prompt_seed, cont_seed], axis=0).astype(jnp.float32)
    grad_result = (valid * grad_out).astype(jnp.bfloat16)
    grad_out_bias = row_sum(grad_result)
    grad_out_weight = jnp.einsum(
        "rf,rd->fd", active, grad_result, preferred_element_type=jnp.float32
    )
    grad_active = jnp.einsum("rd,fd->rf", grad_result, w_out, preferred_element_type=jnp.float32)
    grad_inner = pull_gelu(grad_active)[0].astype(jnp.bfloat16)
    grad_fc_bias = row_sum(grad_inner)
    grad_fc_weight = jnp.einsum("rd,rf->df", second, grad_inner, preferred_element_type=jnp.float32)
    grad_second = jnp.einsum("rf,df->rd", grad_inner, w_fc, preferred_element_type=jnp.float32)
    grad_hidden_norm, grad_gain_second, grad_shift_second = pull_second(grad_second)
    grad_hidden = grad_out + grad_hidden_norm
    grad_branch = (valid * grad_hidden).astype(jnp.bfloat16)
    grad_proj_bias = row_sum(grad_branch)
    grad_proj_weight = jnp.einsum(
        "rd,re->de", mixed, grad_branch, preferred_element_type=jnp.float32
    )
    grad_mixed = jnp.einsum(
        "re,de->rd", grad_branch, w_proj, preferred_element_type=jnp.float32
    ).astype(jnp.bfloat16)
    prompt_dq, prompt_dk, prompt_dv, prompt_inner = attend_backward(
        prompt_query, own_keys, own_values, prompt_allowed, prompt_total, grad_mixed[None, :prow], 0
    )
    cont_dq, cont_dk, cont_dv, cont_inner = attend_backward(
        cont_query,
        cont_keys,
        cont_values,
        cont_allowed,
        cont_total,
        grad_mixed[prow:].reshape(conts, clen, D),
        0,
    )
    picks = (jnp.arange(NPR)[None, :] == follows[:, None]).astype(jnp.float32)
    mine = (jnp.arange(NPR) == prompt_index).astype(jnp.float32)
    key_table = (
        jnp.sum(picks[:, :, None, None] * cont_dk[:, None, :PLEN], axis=0)
        + mine[:, None, None] * prompt_dk
    )
    value_table = (
        jnp.sum(picks[:, :, None, None] * cont_dv[:, None, :PLEN], axis=0)
        + mine[:, None, None] * prompt_dv
    )
    summed_keys, summed_values = (
        lax.psum_scatter(
            key_table.reshape(NPR * PLEN, D).astype(jnp.bfloat16),
            "fsdp",
            scatter_dimension=0,
            tiled=True,
        ).astype(jnp.float32),
        lax.psum_scatter(
            value_table.reshape(NPR * PLEN, D).astype(jnp.bfloat16),
            "fsdp",
            scatter_dimension=0,
            tiled=True,
        ).astype(jnp.float32),
    )
    cont_own_dk = cont_dk[:, PLEN:]
    cont_own_dv = cont_dv[:, PLEN:]
    grad_query = jnp.concatenate([prompt_dq[0], cont_dq.reshape(crow, D)], axis=0).astype(
        jnp.bfloat16
    )
    grad_keys = jnp.concatenate([summed_keys, cont_own_dk.reshape(crow, D)], axis=0).astype(
        jnp.bfloat16
    )
    grad_values = jnp.concatenate([summed_values, cont_own_dv.reshape(crow, D)], axis=0).astype(
        jnp.bfloat16
    )
    grad_projected = jnp.concatenate([grad_query, grad_keys, grad_values], axis=1)
    grad_attn_bias = jnp.stack([row_sum(grad_query), row_sum(grad_values)])
    grad_attn_weight = jnp.einsum(
        "rd,re->de", normed, grad_projected, preferred_element_type=jnp.float32
    )
    grad_normed = jnp.einsum(
        "re,de->rd", grad_projected, w_attn, preferred_element_type=jnp.float32
    )
    grad_inputs_norm, grad_gain_first, grad_shift_first = pull_first(grad_normed)
    grad_inputs = (grad_hidden + grad_inputs_norm).astype(jnp.bfloat16)
    grads = (
        grad_gain_first,
        grad_shift_first,
        grad_attn_weight,
        grad_attn_bias,
        grad_proj_weight,
        grad_proj_bias,
        grad_gain_second,
        grad_shift_second,
        grad_fc_weight,
        grad_fc_bias,
        grad_out_weight,
        grad_out_bias,
    )
    return (final[:prow], final[prow:], grad_inputs[:prow], grad_inputs[prow:], grads)


def body(
    prompt_in,
    cont_in,
    prompt_cot,
    cont_cot,
    cont_prompt,
    cont_len,
    ln1_gain,
    ln1_bias,
    attn_weight,
    attn_bias,
    proj_weight,
    proj_bias,
    ln2_gain,
    ln2_bias,
    fc_weight,
    fc_bias,
    out_weight,
    out_bias,
):
    masters = (
        ln1_gain,
        ln1_bias,
        attn_weight,
        attn_bias,
        proj_weight,
        proj_bias,
        ln2_gain,
        ln2_bias,
        fc_weight,
        fc_bias,
        out_weight,
        out_bias,
    )
    prow = prompt_in.shape[1]
    per_prompt = lax.axis_size("fsdp") // NPR
    place = lax.axis_index("fsdp")
    prompt_index = place // per_prompt
    offset = place % per_prompt * prow
    prompt_outs, cont_outs, prompt_grads, cont_grads = ([], [], [], [])
    totals = None
    for batch_index in range(MB):
        first, later, grad_first, grad_later, grads = run_batch(
            masters,
            prompt_in[batch_index],
            cont_in[batch_index],
            prompt_cot[batch_index],
            cont_cot[batch_index],
            cont_prompt[batch_index, 0],
            cont_len[batch_index, 0],
            prompt_index,
            offset,
        )
        prompt_outs.append(first)
        cont_outs.append(later)
        prompt_grads.append(grad_first)
        cont_grads.append(grad_later)
        if totals is None:
            totals = grads
        else:
            totals = jax.tree.map(lambda left, right: left + right, totals, grads)
    shares = sum_end(totals)
    return (
        jnp.stack(prompt_outs),
        jnp.stack(cont_outs),
        jnp.stack(prompt_grads),
        jnp.stack(cont_grads),
        shares[0],
        shares[1],
        shares[2],
        shares[3],
        shares[4],
        shares[5],
        shares[6],
        shares[7],
        shares[8],
        shares[9],
        shares[10],
        shares[11],
    )


def solution(mesh):
    return jax.shard_map(
        body,
        mesh=mesh,
        in_specs=(
            P(None, ("grp", "fsdp"), None),
            P(None, ("grp", "fsdp"), None),
            P(None, ("grp", "fsdp"), None),
            P(None, ("grp", "fsdp"), None),
            P(None, "grp", "fsdp"),
            P(None, "grp", "fsdp"),
            P(("grp", "fsdp")),
            P(("grp", "fsdp")),
            P(("grp", "fsdp"), None),
            P(None, ("grp", "fsdp")),
            P(("grp", "fsdp"), None),
            P(("grp", "fsdp")),
            P(("grp", "fsdp")),
            P(("grp", "fsdp")),
            P(("grp", "fsdp"), None),
            P(("grp", "fsdp")),
            P(("grp", "fsdp"), None),
            P(("grp", "fsdp")),
        ),
        out_specs=(
            P(None, ("grp", "fsdp"), None),
            P(None, ("grp", "fsdp"), None),
            P(None, ("grp", "fsdp"), None),
            P(None, ("grp", "fsdp"), None),
            P(("grp", "fsdp")),
            P(("grp", "fsdp")),
            P(("grp", "fsdp"), None),
            P(None, ("grp", "fsdp")),
            P(("grp", "fsdp"), None),
            P(("grp", "fsdp")),
            P(("grp", "fsdp")),
            P(("grp", "fsdp")),
            P(("grp", "fsdp"), None),
            P(("grp", "fsdp")),
            P(("grp", "fsdp"), None),
            P(("grp", "fsdp")),
        ),
        check_vma=False,
    )
```

profile of v0, /device:TPU:0, one launch (start us, length us, event | category | flops | bytes accessed | tf_op | source)
XLA Modules:
  0.0 2887.3 jit_solution(1538382989458644103)
XLA Ops:
  14.9 42.7 %all-reduce.20 = (bf16[768]{0:T(1024)(128)(2,1)}, bf16[768]{0:T(1024)(128)(2,1)S(1)}, bf16[768]{0:T(1024)(128)(2,1)S(1)}, bf16[768]{0:T(1024)(128)(2,1)}, bf16[7...) all-reduce(bf16[768]{0:T(1024)(128)(2,1)S(1)} %dynamic-update-slice, ...), channel_id=1, replica_groups=mesh['grp'=4,'fsdp'=8] {'grp','fsdp'}, use_global_device_ids=true, to_apply=%add.6 | all-reduce | flops 7680 | bytes 30720
  85.0 40.3 %all-gather = bf16[32,24,2]{1,2,0:T(2,128)(2,1)S(1)} all-gather(bf16[1,24,2]{1,2,0:T(2,128)(2,1)S(1)} %convert_bitcast_fusion), channel_id=1, replica_groups=mesh['grp'=4,'fsdp'=8] {'grp','fsdp'}, dimensions={0}, use_global_device_ids=true | all-gather | bytes 3168 | tf_op jit(solution)/shard_map/all_gather | solution.py:94
  242.6 36.1 %all-gather.24.cloned.1.call-done = bf16[4096,768]{1,0:T(8,128)(2,1)} async-done(((bf16[512,768]{1,0:T(8,128)(2,1)}), bf16[4096,768]{1,0:T(8,128)(2,1)}) %all-gather.24.cloned.1.call-update) | async-done | bytes 6291472 | tf_op jit(solution)/shard_map/all_gather | solution.py:182
  278.7 64.9 %all-gather.26.cloned.1.call-done = bf16[4096,768]{1,0:T(8,128)(2,1)} async-done(((bf16[512,768]{1,0:T(8,128)(2,1)}), bf16[4096,768]{1,0:T(8,128)(2,1)}) %all-gather.26.cloned.1.call-update) | async-done | bytes 6291472 | tf_op jit(solution)/shard_map/all_gather | solution.py:181
  354.4 54.1 %all-gather.30.cloned.1.call-done = bf16[4096,768]{1,0:T(8,128)(2,1)} async-done(((bf16[512,768]{1,0:T(8,128)(2,1)}), bf16[4096,768]{1,0:T(8,128)(2,1)}) %all-gather.30.cloned.1.call-update) | async-done | bytes 6291472 | tf_op jit(solution)/shard_map/all_gather | solution.py:181
  408.6 65.1 %all-gather.28.cloned.1.call-done = bf16[4096,768]{1,0:T(8,128)(2,1)} async-done(((bf16[512,768]{1,0:T(8,128)(2,1)}), bf16[4096,768]{1,0:T(8,128)(2,1)}) %all-gather.28.cloned.1.call-update) | async-done | bytes 6291472 | tf_op jit(solution)/shard_map/all_gather | solution.py:182
  526.1 21.4 fusion.243
  561.0 23.4 fusion.24
  584.5 54.4 %fusion = (f32[12,512]{1,0:T(8,128)S(1)}, f32[12,512]{1,0:T(8,128)}, f32[12,512]{1,0:T(8,128)}, f32[12,512,2048]{2,1,0:T(8,128)}) fusion(f32[12,512]{1,0:T(8,128)S(1)} %get-tuple-element.201, f32[12,512,2048]{2,1,0:T(8,128)} %get-tuple-element.202, pred[512,2048]{1,0:T(8,128)(4,1)S(1)} %iota_compare_fusion, f32[12,512,2048]{2,1,0:T(8,128)} %fusion.243, ...), kind=kOutput, calls=%fused_computation.18 | convolution fusion | flops 1736423424 | bytes 156073984 | tf_op jit(solution)/shard_map/bqhd,bkhd->bhqk/dot_general | solution.py:33
  638.9 22.7 fusion.125
  798.5 22.9 fusion.10
  821.5 69.2 %multiply_reduce_fusion.2 = (f32[12,512]{1,0:T(8,128)}, f32[12,512]{1,0:T(8,128)S(1)}, f32[12,512]{1,0:T(8,128)S(1)}, f32[12,512,2048]{2,1,0:T(8,128)}) fusion(f32[12,512]{1,0:T(8,128)S(1)} %log_add_fusion.2, f32[12,512,2048]{2,1,0:T(8,128)} %get-tuple-element.202, pred[512,2048]{1,0:T(8,128)(4,1)S(1)} %iota_compare_fusion, f32[12,512]{1,0:T(8,128)S(1)} %copy-done.220, ...), kind=kOutput, calls=%fused_computation.7 | convolution fusion | flops 1774172160 | bytes 206454784 | tf_op jit(solution)/shard_map/bqhd,bkhd->bhqk/dot_general | solution.py:57
  891.9 21.8 fusion.124
  913.8 21.0 fusion.123
  1051.0 21.8 copy.304
  1098.7 21.9 copy.303
  1120.6 21.9 multiply_reduce_fusion.5
  1142.5 18.3 multiply_convert_fusion.5
  1177.3 21.7 copy.300
  1199.1 20.5 fusion.8
  1227.8 21.9 copy.309
  1249.7 21.2 fusion.244
  1270.9 20.4 fusion.6
  1299.7 22.1 copy.314
  1321.8 14.6 fusion.29
  1347.9 21.8 copy.308
  1395.6 21.9 copy.313
  1417.5 21.9 multiply_reduce_fusion.3
  1439.3 18.3 multiply_convert_fusion.3
  1474.2 21.9 copy.311
  1496.1 21.9 multiply_reduce_fusion.4
  1518.0 18.3 multiply_convert_fusion.4
  1552.4 22.1 copy.306
  1574.5 66.3 %multiply_reduce_fusion.1 = (f32[12,512]{1,0:T(8,128)S(1)}, f32[12,512]{1,0:T(8,128)S(1)}, f32[12,512,2048]{2,1,0:T(8,128)}) fusion(f32[12,512]{1,0:T(8,128)S(1)} %copy-done.139, f32[12,512,2048]{2,1,0:T(8,128)} %get-tuple-element.205, pred[512,2048]{1,0:T(8,128)(4,1)S(1)} %copy-done.7, f32[12,512,2048]{2,1,0:T(8,128)} %fusion.244, ...), kind=kOutput, calls=%fused_computation.4 | convolution fusion | flops 1736429568 | bytes 206405632 | tf_op jit(solution)/shard_map/bqhd,bkhd->bhqk/dot_general | solution.py:57
  1640.7 117.6 %multiply_convert_fusion.1 = (bf16[12,512,2048]{2,1,0:T(8,128)(2,1)}, bf16[12,512,2048]{2,1,0:T(8,128)(2,1)}, bf16[12,512,2048]{2,1,0:T(8,128)(2,1)}) fusion(f32[12,512,2048]{2,1,0:T(8,128)} %get-tuple-element.215, f32[12,512]{1,0:T(8,128)S(1)} %get-tuple-element.107, f32[12,512]{1,0:T(8,128)S(1)} %copy-done.139, f32[12,512,2048]{2,1,0:T(8,128)} %get-tuple-element.205, ...), kind=kLoop, calls=%fused_computation.3 | loop fusion | flops 226492416 | bytes 378683392 | tf_op jit(solution)/shard_map/convert_element_type | solution.py:61
  1769.1 15.4 convolution_multiply_fusion.5
  1803.4 22.0 copy.312
  1835.5 21.8 copy.302
  1865.4 21.9 copy.307
  1887.4 61.1 %add_convert_fusion.3 = (bf16[4096,768]{0,1:T(8,128)(2,1)}, bf16[4096,768]{0,1:T(8,128)(2,1)}, bf16[4096,768]{0,1:T(8,128)(2,1)}, bf16[4096,768]{0,1:T(8,128)(2,...) fusion(f32[4096,768]{0,1:T(8,128)} %bitcast.464, f32[4096,768]{0,1:T(8,128)} %bitcast.461, ...), kind=kLoop, calls=%fused_computation.78 | loop fusion | flops 75497472 | bytes 188809216 | tf_op jit(solution)/shard_map/convert_element_type | solution.py:255
  1986.5 15.1 add_add_fusion
  2183.4 44.8 %reduce-scatter.16.cloned.1.call-done = bf16[512,768]{0,1:T(8,128)(2,1)} async-done(((bf16[4096,768]{0,1:T(8,128)(2,1)}), bf16[512,768]{0,1:T(8,128)(2,1)}) %reduce-scatter.16.cloned.1.call-update) | async-done | bytes 786448 | tf_op jit(solution)/shard_map/reduce_scatter | solution.py:254
  2236.0 62.6 %reduce-scatter.12.cloned.1.call-done = bf16[512,768]{0,1:T(8,128)(2,1)} async-done(((bf16[4096,768]{0,1:T(8,128)(2,1)}), bf16[512,768]{0,1:T(8,128)(2,1)}) %reduce-scatter.12.cloned.1.call-update) | async-done | bytes 786448 | tf_op jit(solution)/shard_map/reduce_scatter | solution.py:254
  2306.7 62.3 %reduce-scatter.20.cloned.1.call-done = bf16[512,768]{0,1:T(8,128)(2,1)} async-done(((bf16[4096,768]{0,1:T(8,128)(2,1)}), bf16[512,768]{0,1:T(8,128)(2,1)}) %reduce-scatter.20.cloned.1.call-update) | async-done | bytes 786448 | tf_op jit(solution)/shard_map/reduce_scatter | solution.py:254
  2429.8 40.3 %all-reduce.19 = (f32[768]{0:T(1024)}, f32[768]{0:T(1024)}, f32[2,768]{1,0:T(2,128)}, f32[768]{0:T(1024)}, f32[768]{0:T(1024)}, /*index=5*/f32[768]{0:T(1024)}, f32[3072]{0:T(1024)}, f32[768]{0:T(1024)}) all-reduce(f32[768]{0:T(1024)S(1)} %add_add_fusion.16, ...), channel_id=8, replica_groups=mesh['grp'=4,'fsdp'=8] {'grp','fsdp'}, use_global_device_ids=true, to_apply=%region_51.53.clone | all-reduce | flops 9216 | bytes 73728
  2492.0 121.9 %reduce-scatter.30.cloned.1.call-done = f32[96,768]{1,0:T(8,128)} async-done(((f32[3072,768]{1,0:T(8,128)}), f32[96,768]{1,0:T(8,128)}) %reduce-scatter.30.cloned.1.call-update) | async-done | bytes 294928 | tf_op jit(solution)/shard_map/reduce_scatter | solution.py:138
  2613.9 141.2 %reduce-scatter.28.cloned.1.call-done = f32[24,3072]{1,0:T(8,128)} async-done(((f32[768,3072]{1,0:T(8,128)}), f32[24,3072]{1,0:T(8,128)}) %reduce-scatter.28.cloned.1.call-update) | async-done | bytes 294928 | tf_op jit(solution)/shard_map/reduce_scatter | solution.py:136
  2755.1 125.2 %reduce-scatter.24.cloned.1.call-done = f32[24,2304]{1,0:T(8,128)} async-done(((f32[768,2304]{1,0:T(8,128)}), f32[24,2304]{1,0:T(8,128)}) %reduce-scatter.24.cloned.1.call-update) | async-done | bytes 221200 | tf_op jit(solution)/shard_map/reduce_scatter | solution.py:130
  (937 shorter events, 969.7 us)
Async XLA Ops:
  7.2 67.7 %all-gather.12.cloned.1.call-start = ((), (), s32[]{:S(2)}) async-start(), calls=%async_computation.10 | async-start | bytes 3649536 | tf_op jit(solution)/shard_map/all_gather | solution.py:93
  8.8 217.8 %all-gather.16.cloned.1.call-start = ((), (), s32[]{:S(2)}) async-start(), calls=%async_computation.12 | async-start | bytes 7077888 | tf_op jit(solution)/shard_map/all_gather | solution.py:181
  57.7 76.2 %copy-start.172 = (f32[768]{0:T(1024)}, f32[768]{0:T(1024)S(1)}, u32[]{:S(2)}) copy-start(f32[768]{0:T(1024)S(1)} %convert_element_type.435) | copy-start | bytes 9220
  57.7 76.2 %copy-start.242 = (f32[768]{0:T(1024)}, f32[768]{0:T(1024)S(1)}, u32[]{:S(2)}) copy-start(f32[768]{0:T(1024)S(1)} %convert_element_type.437) | copy-start | bytes 9220
  82.2 43.8 %copy-start.97 = (bf16[1,512,768]{2,1,0:T(8,128)(2,1)S(1)}, bf16[1,512,768]{2,1,0:T(8,128)(2,1)}, u32[]{:S(2)}) copy-start(bf16[1,512,768]{2,1,0:T(8,128)(2,1)} %get-tuple-element.152) | copy-start | bytes 2359300
  84.9 141.7 %all-gather.14.cloned.1.call-start = ((), (), s32[]{:S(2)}) async-start(), calls=%async_computation.11 | async-start | bytes 7077888 | tf_op jit(solution)/shard_map/all_gather | solution.py:182
  142.8 135.9 %all-gather.24.cloned.1.call-start = ((), (), s32[]{:S(2)}) async-start(), calls=%async_computation.16 | async-start | bytes 7077888 | tf_op jit(solution)/shard_map/all_gather | solution.py:182
  144.9 198.7 %all-gather.26.cloned.1.call-start = ((), (), s32[]{:S(2)}) async-start(), calls=%async_computation.17 | async-start | bytes 7077888 | tf_op jit(solution)/shard_map/all_gather | solution.py:181
  147.2 261.3 %all-gather.30.cloned.1.call-start = ((), (), s32[]{:S(2)}) async-start(), calls=%async_computation.19 | async-start | bytes 7077888 | tf_op jit(solution)/shard_map/all_gather | solution.py:181
  149.4 324.2 %all-gather.28.cloned.1.call-start = ((), (), s32[]{:S(2)}) async-start(), calls=%async_computation.18 | async-start | bytes 7077888 | tf_op jit(solution)/shard_map/all_gather | solution.py:182
  151.6 510.1 %all-gather.18.cloned.1.call-start = ((), (), s32[]{:S(2)}) async-start(), calls=%async_computation.13 | async-start | bytes 1216512 | tf_op jit(solution)/shard_map/all_gather | solution.py:95
  152.4 513.9 %all-gather.20.cloned.1.call-start = ((), (), s32[]{:S(2)}) async-start(), calls=%async_computation.14 | async-start | bytes 4866048 | tf_op jit(solution)/shard_map/all_gather | solution.py:99
  153.1 522.1 %all-gather.22.cloned.1.call-start = ((), (), s32[]{:S(2)}) async-start(), calls=%async_computation.15 | async-start | bytes 4866048 | tf_op jit(solution)/shard_map/all_gather | solution.py:101
  153.9 2023.6 %reduce-scatter.14.cloned.1.call-start = ((), (), s32[]{:S(2)}) async-start(), calls=%async_computation.21 | async-start | bytes 7077888 | tf_op jit(solution)/shard_map/reduce_scatter | solution.py:260
  172.7 741.0 %copy-start.5 = (pred[512,2048]{1,0:T(8,128)(4,1)}, pred[512,2048]{1,0:T(8,128)(4,1)S(1)}, u32[]{:S(2)}) copy-start(pred[512,2048]{1,0:T(8,128)(4,1)S(1)} %iota_compare_fusion) | copy-start | bytes 3145732
  215.2 310.9 %copy-start.58 = (bf16[512,768]{0,1:T(8,128)(2,1)}, bf16[512,768]{0,1:T(8,128)(2,1)S(1)}, u32[]{:S(2)}) copy-start(bf16[512,768]{0,1:T(8,128)(2,1)S(1)} %copy.246) | copy-start | bytes 2359300
  222.9 338.1 %copy-start.60 = (bf16[512,768]{0,1:T(8,128)(2,1)}, bf16[512,768]{0,1:T(8,128)(2,1)S(1)}, u32[]{:S(2)}) copy-start(bf16[512,768]{0,1:T(8,128)(2,1)S(1)} %copy.224) | copy-start | bytes 2359300
  223.1 276.4 %copy-start.113 = (bf16[256,768]{0,1:T(8,128)(2,1)}, bf16[256,768]{0,1:T(8,128)(2,1)S(1)}, u32[]{:S(2)}) copy-start(bf16[256,768]{0,1:T(8,128)(2,1)S(1)} %copy.228) | copy-start | bytes 1179652
  224.6 323.0 %copy-start.118 = (bf16[256,768]{0,1:T(8,128)(2,1)}, bf16[256,768]{0,1:T(8,128)(2,1)S(1)}, u32[]{:S(2)}) copy-start(bf16[256,768]{0,1:T(8,128)(2,1)S(1)} %copy.227) | copy-start | bytes 1179652
  666.2 155.2 %copy-start.174 = (f32[12,512]{1,0:T(8,128)}, f32[12,512]{1,0:T(8,128)S(1)}, u32[]{:S(2)}) copy-start(f32[12,512]{1,0:T(8,128)S(1)} %log_add_fusion.2) | copy-start | bytes 73732
  951.6 80.1 %copy-start.3 = (f32[768,768]{0,1:T(8,128)}, f32[768,768]{0,1:T(8,128)S(1)}, u32[]{:S(2)}) copy-start(f32[768,768]{0,1:T(8,128)S(1)} %get-tuple-element.210) | copy-start | bytes 7077892
  951.6 80.0 %copy-start.154 = (f32[768]{0:T(1024)}, f32[768]{0:T(1024)S(1)}, u32[]{:S(2)}) copy-start(f32[768]{0:T(1024)S(1)} %broadcast_multiply_fusion) | copy-start | bytes 9220
  951.9 79.7 %copy-start.156 = (f32[768]{0:T(1024)}, f32[768]{0:T(1024)S(1)}, u32[]{:S(2)}) copy-start(f32[768]{0:T(1024)S(1)} %fusion.169) | copy-start | bytes 9220
  1040.6 158.4 %copy-start.95 = (bf16[512,768]{0,1:T(8,128)(2,1)}, bf16[512,768]{0,1:T(8,128)(2,1)S(1)}, u32[]{:S(2)}) copy-start(bf16[512,768]{0,1:T(8,128)(2,1)S(1)} %slice.366) | copy-start | bytes 2359300
  1574.4 66.3 %copy-start.175 = (f32[12,512]{1,0:T(8,128)S(1)}, f32[12,512]{1,0:T(8,128)}, u32[]{:S(2)}) copy-start(f32[12,512]{1,0:T(8,128)} %copy-done.174) | copy-start | bytes 73732
  1574.4 66.3 %copy-start.219 = (f32[12,512]{1,0:T(8,128)S(1)}, f32[12,512]{1,0:T(8,128)}, u32[]{:S(2)}) copy-start(f32[12,512]{1,0:T(8,128)} %get-tuple-element.104) | copy-start | bytes 73732
  1948.5 230.9 %reduce-scatter.22.cloned.1.call-start = ((), (), s32[]{:S(2)}) async-start(), calls=%async_computation.25 | async-start | bytes 7077888 | tf_op jit(solution)/shard_map/reduce_scatter | solution.py:260
  1949.1 232.3 %reduce-scatter.18.cloned.1.call-start = ((), (), s32[]{:S(2)}) async-start(), calls=%async_computation.23 | async-start | bytes 7077888 | tf_op jit(solution)/shard_map/reduce_scatter | solution.py:260
  1949.9 278.4 %reduce-scatter.16.cloned.1.call-start = ((), (), s32[]{:S(2)}) async-start(), calls=%async_computation.22 | async-start | bytes 7077888 | tf_op jit(solution)/shard_map/reduce_scatter | solution.py:254
  1950.4 348.1 %reduce-scatter.12.cloned.1.call-start = ((), (), s32[]{:S(2)}) async-start(), calls=%async_computation.20 | async-start | bytes 7077888 | tf_op jit(solution)/shard_map/reduce_scatter | solution.py:254
  1951.1 417.9 %reduce-scatter.20.cloned.1.call-start = ((), (), s32[]{:S(2)}) async-start(), calls=%async_computation.24 | async-start | bytes 7077888 | tf_op jit(solution)/shard_map/reduce_scatter | solution.py:254
  1951.6 540.4 %reduce-scatter.26.cloned.1.call-start = ((), (), s32[]{:S(2)}) async-start(), calls=%async_computation.27 | async-start | bytes 2433024 | tf_op jit(solution)/shard_map/reduce_scatter | solution.py:132
  1972.3 641.6 %reduce-scatter.30.cloned.1.call-start = ((), (), s32[]{:S(2)}) async-start(), calls=%async_computation.29 | async-start | bytes 9732096 | tf_op jit(solution)/shard_map/reduce_scatter | solution.py:138
  2001.7 753.5 %reduce-scatter.28.cloned.1.call-start = ((), (), s32[]{:S(2)}) async-start(), calls=%async_computation.28 | async-start | bytes 9732096 | tf_op jit(solution)/shard_map/reduce_scatter | solution.py:136
  2081.7 798.5 %reduce-scatter.24.cloned.1.call-start = ((), (), s32[]{:S(2)}) async-start(), calls=%async_computation.26 | async-start | bytes 7299072 | tf_op jit(solution)/shard_map/reduce_scatter | solution.py:130
  2170.8 57.5 %copy-start.23 = (bf16[1,512,768]{1,2,0:T(8,128)(2,1)S(1)}, bf16[1,512,768]{1,2,0:T(8,128)(2,1)}, u32[]{:S(2)}) copy-start(bf16[1,512,768]{1,2,0:T(8,128)(2,1)} %copy-done.21) | copy-start | bytes 2359300
  2170.8 57.5 %copy-start.43 = (bf16[1,256,768]{1,2,0:T(8,128)(2,1)S(1)}, bf16[1,256,768]{1,2,0:T(8,128)(2,1)}, u32[]{:S(2)}) copy-start(bf16[1,256,768]{1,2,0:T(8,128)(2,1)} %copy-done.41) | copy-start | bytes 1179652
  2170.8 57.5 %copy-start.83 = (bf16[12,64,512]{2,1,0:T(8,128)(2,1)S(1)}, bf16[12,64,512]{2,1,0:T(8,128)(2,1)}, u32[]{:S(2)}) copy-start(bf16[12,64,512]{2,1,0:T(8,128)(2,1)} %multiply_convert_fusion.13) | copy-start | bytes 2359300
  2170.8 57.5 %copy-start.173 = (f32[768]{0:T(1024)S(1)}, f32[768]{0:T(1024)}, u32[]{:S(2)}) copy-start(f32[768]{0:T(1024)} %copy-done.172) | copy-start | bytes 9220
  2170.8 57.5 %copy-start.177 = (f32[768]{0:T(1024)S(1)}, f32[768]{0:T(1024)}, u32[]{:S(2)}) copy-start(f32[768]{0:T(1024)} %copy-done.176) | copy-start | bytes 9220
  2170.8 57.5 %copy-start.200 = (f32[768]{0:T(1024)S(1)}, f32[768]{0:T(1024)}, u32[]{:S(2)}) copy-start(f32[768]{0:T(1024)} %copy-done.199) | copy-start | bytes 9220
  2172.1 56.1 %copy-start.122 = (bf16[256,768]{0,1:T(8,128)(2,1)}, bf16[256,768]{0,1:T(8,128)(2,1)S(1)}, u32[]{:S(2)}) copy-start(bf16[256,768]{0,1:T(8,128)(2,1)S(1)} %fusion.157) | copy-start | bytes 1179652
  2183.4 115.2 %copy-start.25 = (bf16[1,512,768]{1,2,0:T(8,128)(2,1)S(1)}, bf16[1,512,768]{1,2,0:T(8,128)(2,1)}, u32[]{:S(2)}) copy-start(bf16[1,512,768]{1,2,0:T(8,128)(2,1)} %copy-done.24) | copy-start | bytes 2359300
  2183.4 115.2 %copy-start.45 = (bf16[1,256,768]{1,2,0:T(8,128)(2,1)S(1)}, bf16[1,256,768]{1,2,0:T(8,128)(2,1)}, u32[]{:S(2)}) copy-start(bf16[1,256,768]{1,2,0:T(8,128)(2,1)} %copy-done.44) | copy-start | bytes 1179652
  2183.4 115.2 %copy-start.179 = (f32[768]{0:T(1024)S(1)}, f32[768]{0:T(1024)}, u32[]{:S(2)}) copy-start(f32[768]{0:T(1024)} %copy-done.178) | copy-start | bytes 9220
  2236.0 132.9 %copy-start.29 = (bf16[1,512,768]{1,2,0:T(8,128)(2,1)S(1)}, bf16[1,512,768]{1,2,0:T(8,128)(2,1)}, u32[]{:S(2)}) copy-start(bf16[1,512,768]{1,2,0:T(8,128)(2,1)} %copy-done.27) | copy-start | bytes 2359300
  2236.0 132.9 %copy-start.49 = (bf16[1,256,768]{1,2,0:T(8,128)(2,1)S(1)}, bf16[1,256,768]{1,2,0:T(8,128)(2,1)}, u32[]{:S(2)}) copy-start(bf16[1,256,768]{1,2,0:T(8,128)(2,1)} %copy-done.47) | copy-start | bytes 1179652
  2236.0 132.9 %copy-start.181 = (f32[768]{0:T(1024)S(1)}, f32[768]{0:T(1024)}, u32[]{:S(2)}) copy-start(f32[768]{0:T(1024)} %copy-done.180) | copy-start | bytes 9220
  (252 other events, 2402.7 us)
Sparse Core Ops, SparseCore 0:
  11.6 63.1 all-gather.11
  85.1 63.6 all-gather.15
  150.4 63.3 all-gather.13
  215.3 63.3 all-gather.23
  280.2 63.3 all-gather.25
  345.1 63.3 all-gather.29
  410.2 63.3 all-gather.27
  477.2 52.8 all-gather.17
  533.7 62.6 all-gather.19
  599.8 62.4 all-gather.21
  1948.6 68.3 reduce-scatter.13
  2019.2 68.1 reduce-scatter.21
  2089.7 68.1 reduce-scatter.17
  2160.0 68.1 reduce-scatter.15
  2230.4 68.1 reduce-scatter.11
  2300.7 68.1 reduce-scatter.19
  2374.6 97.2 reduce-scatter.25
  2479.3 134.5 reduce-scatter.29
  2620.3 134.7 reduce-scatter.27
  2762.2 118.0 reduce-scatter.23
where the time goes:
time: 2900 us; the launch traced here: 2890 us
  matrix products  955 us (33%)
  waiting for transfers between devices  793 us (27%)
  local copies, waits for them, and re-layouts  626 us (22%)
  other arithmetic  365 us (13%)
  blocking collectives  123 us (4%)
    unnamed x618, local copies, waits for them, and re-layouts  335 us
    dot_general x6, matrix products, attend_backward(): jnp.einsum('bqhd,bkhd->bhqk', heads_grad, split_heads(values), preferred_...  222 us
    convert_element_type x4, other arithmetic, attend_backward(): grad_scores = (probs * (grad_probs - inner)).astype(jnp.bfloat16)  173 us
    reduce_scatter x3, waiting for transfers between devices, run_batch(): lax.psum_scatter(key_table.reshape(NPR * PLEN, D).astype(jnp.bfloat16), '...  170 us
    reduce_scatter x1, waiting for transfers between devices, sum_end(): lax.psum_scatter(grads[8], ('grp', 'fsdp'), scatter_dimension=0, tiled=True)  141 us
    dot_general x6, matrix products, scores_of(): jnp.einsum('bqhd,bkhd->bhqk', split_heads(query), split_heads(keys), pref...  140 us
    reduce_scatter x1, waiting for transfers between devices, sum_end(): lax.psum_scatter(grads[2], ('grp', 'fsdp'), scatter_dimension=0, tiled=True)  125 us
    reduce_scatter x1, waiting for transfers between devices, sum_end(): lax.psum_scatter(grads[10], ('grp', 'fsdp'), scatter_dimension=0, tiled=T...  122 us
  transfers between devices with their start and end apart: 20, of which 11 were waited for; matrix products, arithmetic and copies ran while one was open for 23% of the time, Pallas kernels for 0%

commit v1 on v0

v1 whole, which is shorter than its diff:
```python
import functools
import math

import jax
import jax.numpy as jnp
from jax import lax
from jax.experimental import pallas as pl
from jax.experimental.pallas import tpu as pltpu
from jax.sharding import PartitionSpec as P

D = 768
HEADS = 12
HEAD_DIM = 64
FF = 3072
MB = 3
NPR = 2
PLEN = 2048
ALL = ("grp", "fsdp")

EPSILON = 1e-05
MASKED = -1e30
BF = jnp.bfloat16
F32 = jnp.float32

HALF = D // 2
NH = HEADS // 2
PAIRS = NH // 2
TQ = 256
TK = 512
LOG2E = math.log2(math.e)
QSCALE = HEAD_DIM ** (-0.5) * LOG2E


def dot_nt(a, b):
    return lax.dot_general(a, b, (((1,), (1,)), ((), ())), preferred_element_type=F32)


def dot_nn(a, b):
    return lax.dot_general(a, b, (((1,), (0,)), ((), ())), preferred_element_type=F32)


def half_masks():
    lane = lax.broadcasted_iota(jnp.int32, (TQ, 128), 1)
    return (lane < HEAD_DIM, lane >= HEAD_DIM)


def attend_forward_kernel(
    info, q_ref, kvp_hbm, kvc_hbm, o_ref, lse_ref, kv, qm, s_ref, mx, acc, sems
):
    block = pl.program_id(0)
    prompt_rows = kvp_hbm.shape[0]
    cont_rows = kvc_hbm.shape[0]

    @pl.when(block == 0)
    def _():
        one = pltpu.make_async_copy(kvp_hbm, kv.at[pl.ds(0, prompt_rows)], sems.at[0])
        two = pltpu.make_async_copy(kvc_hbm, kv.at[pl.ds(prompt_rows, cont_rows)], sems.at[1])
        one.start()
        two.start()
        one.wait()
        two.wait()

    base = pl.multiple_of(info[block, 0], TQ)
    tiles = info[block, 1]
    extra = info[block, 2]
    diag = pl.multiple_of(info[block, 3], TQ)
    extra_row = pl.multiple_of(base + tiles * TK, TQ)
    low, high = half_masks()
    zero = jnp.zeros((TQ, 128), BF)
    for pair in range(PAIRS):
        part = q_ref[:, pair * 128 : (pair + 1) * 128]
        qm[2 * pair] = jnp.where(low, part, zero)
        qm[2 * pair + 1] = jnp.where(high, part, zero)

    def score(pair, row, size, column, first, masked):
        keys = kv[pl.ds(row, size), pair * 128 : (pair + 1) * 128]
        for side in (0, 1):
            raw = dot_nt(qm[2 * pair + side], keys)
            if masked:
                across = lax.broadcasted_iota(jnp.int32, (TQ, size), 1)
                down = lax.broadcasted_iota(jnp.int32, (TQ, size), 0)
                raw = jnp.where(across <= down, raw, MASKED)
            slot = 2 * (pair % 2) + side
            s_ref[slot, :, pl.ds(column, size)] = raw
            top = raw[:, :128]
            for piece in range(1, size // 128):
                top = jnp.maximum(top, raw[:, piece * 128 : (piece + 1) * 128])
            if not first:
                top = jnp.maximum(top, mx[slot])
            mx[slot] = top

    def settle(pair):
        for side in (0, 1):
            slot = 2 * (pair % 2) + side
            top = jnp.max(mx[slot], axis=1, keepdims=True)
            mx[slot] = jnp.broadcast_to(top, (TQ, 128))

    def blend(pair, row, size, column, first):
        vals = kv[pl.ds(row, size), HALF + pair * 128 : HALF + (pair + 1) * 128]
        wide = jnp.concatenate([vals, jnp.ones((size, 128), BF)], axis=1)
        for side in (0, 1):
            slot = 2 * (pair % 2) + side
            top = jnp.concatenate([mx[slot]] * (size // 128), axis=1)
            power = jnp.exp2(s_ref[slot, :, pl.ds(column, size)] - top).astype(BF)
            new = dot_nn(power, wide)
            if first:
                acc[side] = new
            else:
                acc[side] += new

    def sweep(step):
        step(diag, TQ, 0, True)

        @pl.when(extra > 0)
        def _():
            step(extra_row, TQ, TQ, False)

        def one(index, carry):
            row = pl.multiple_of(base + index * TK, TQ)
            step(row, TK, pl.multiple_of(2 * TQ + index * TK, TQ), False)
            return carry

        lax.fori_loop(0, tiles, one, 0)

    sweep(lambda row, size, column, first: score(0, row, size, column, first, first))
    for pair in range(PAIRS):
        settle(pair)

        def both(row, size, column, first):
            if pair + 1 < PAIRS:
                score(pair + 1, row, size, column, first, first)
            blend(pair, row, size, column, first)

        sweep(both)
        sides = []
        for side in (0, 1):
            total = acc[side][:, 128:]
            sides.append(acc[side][:, :128] / total)
            tall = jnp.transpose(mx[2 * (pair % 2) + side] + jnp.log2(total))
            lse_ref[0, 2 * pair + side] = tall[0]
        o_ref[:, pair * 128 : (pair + 1) * 128] = jnp.where(low, sides[0], sides[1]).astype(BF)


def attend_forward(info, q, kvp, kvc):
    rows = q.shape[0]
    keys = kvp.shape[0] + kvc.shape[0]
    blocks = rows // TQ
    return pl.pallas_call(
        attend_forward_kernel,
        grid_spec=pltpu.PrefetchScalarGridSpec(
            num_scalar_prefetch=1,
            grid=(blocks,),
            in_specs=[
                pl.BlockSpec((TQ, HALF), lambda i, s: (i, 0)),
                pl.BlockSpec(memory_space=pl.ANY),
                pl.BlockSpec(memory_space=pl.ANY),
            ],
            out_specs=[
                pl.BlockSpec((TQ, HALF), lambda i, s: (i, 0)),
                pl.BlockSpec((1, 8, TQ), lambda i, s: (i, 0, 0)),
            ],
            scratch_shapes=[
                pltpu.VMEM((keys, D), BF),
                pltpu.VMEM((NH, TQ, 128), BF),
                pltpu.VMEM((4, TQ, PLEN + 2 * TQ), F32),
                pltpu.VMEM((4, TQ, 128), F32),
                pltpu.VMEM((2, TQ, 256), F32),
                pltpu.SemaphoreType.DMA((2,)),
            ],
        ),
        out_shape=(
            jax.ShapeDtypeStruct((rows, HALF), BF),
            jax.ShapeDtypeStruct((blocks, 8, TQ), F32),
        ),
        compiler_params=pltpu.CompilerParams(
            dimension_semantics=("arbitrary",), vmem_limit_bytes=50 << 20
        ),
        cost_estimate=pl.CostEstimate(
            flops=int(4 * rows * PLEN * HALF * 4), bytes_accessed=20 << 20, transcendentals=0
        ),
        name="attend_forward",
    )(info, q, kvp, kvc)


def attend_backward_kernel(
    info,
    q_ref,
    do_ref,
    o_ref,
    lse_ref,
    kvp_hbm,
    kvc_hbm,
    dq_ref,
    dkvp_hbm,
    dkvc_hbm,
    kv,
    kt,
    dkv,
    qm,
    dom,
    dqt,
    drow,
    sems,
):
    block = pl.program_id(0)
    prompt_rows = kvp_hbm.shape[0]
    cont_rows = kvc_hbm.shape[0]
    keys_all = prompt_rows + cont_rows

    @pl.when(block == 0)
    def _():
        one = pltpu.make_async_copy(kvp_hbm, kv.at[pl.ds(0, prompt_rows)], sems.at[0])
        two = pltpu.make_async_copy(kvc_hbm, kv.at[pl.ds(prompt_rows, cont_rows)], sems.at[1])
        one.start()
        two.start()
        one.wait()
        two.wait()

        def prepare(index, carry):
            row = pl.multiple_of(index * TQ, TQ)
            dkv[pl.ds(row, TQ), :] = jnp.zeros((TQ, D), F32)
            for pair in range(PAIRS):
                piece = kv[pl.ds(row, TQ), pair * 128 : (pair + 1) * 128]
                kt[pair * 128 : (pair + 1) * 128, pl.ds(row, TQ)] = jnp.transpose(
                    piece.astype(F32)
                ).astype(BF)
            return carry

        lax.fori_loop(0, keys_all // TQ, prepare, 0)

    base = pl.multiple_of(info[block, 0], TQ)
    tiles = info[block, 1]
    extra = info[block, 2]
    diag = pl.multiple_of(info[block, 3], TQ)
    extra_row = pl.multiple_of(base + tiles * TK, TQ)
    low, high = half_masks()
    zero = jnp.zeros((TQ, 128), BF)
    for pair in range(PAIRS):
        lanes = slice(pair * 128, (pair + 1) * 128)
        part = q_ref[:, lanes]
        qm[2 * pair] = jnp.where(low, part, zero)
        qm[2 * pair + 1] = jnp.where(high, part, zero)
        part = do_ref[:, lanes]
        dom[2 * pair] = jnp.where(low, part, zero)
        dom[2 * pair + 1] = jnp.where(high, part, zero)
        product = jnp.transpose(part.astype(F32) * o_ref[:, lanes].astype(F32))
        drow[2 * pair] = jnp.sum(product[:HEAD_DIM], axis=0)
        drow[2 * pair + 1] = jnp.sum(product[HEAD_DIM:], axis=0)

    def step(row, size, first):
        for pair in range(PAIRS):
            lanes = slice(pair * 128, (pair + 1) * 128)
            more = slice(HALF + pair * 128, HALF + (pair + 1) * 128)
            keys = kv[pl.ds(row, size), lanes]
            vals = kv[pl.ds(row, size), more]
            dk = None
            dv = None
            for side in (0, 1):
                head = 2 * pair + side
                raw = dot_nt(keys, qm[head])
                if first:
                    across = lax.broadcasted_iota(jnp.int32, (size, TQ), 1)
                    down = lax.broadcasted_iota(jnp.int32, (size, TQ), 0)
                    raw = jnp.where(down <= across, raw, MASKED)
                probs = jnp.exp2(raw - lse_ref[0, head : head + 1, :])
                grad = dot_nt(vals, dom[head])
                slope = (probs * (grad - drow[head : head + 1, :])).astype(BF)
                probs = probs.astype(BF)
                part_v = dot_nn(probs, dom[head])
                part_k = dot_nn(slope, qm[head])
                dv = part_v if dv is None else dv + part_v
                dk = part_k if dk is None else dk + part_k
                spot = slice(head * HEAD_DIM, (head + 1) * HEAD_DIM)
                new = dot_nn(kt[spot, pl.ds(row, size)], slope)
                if first:
                    dqt[spot, :] = new
                else:
                    dqt[spot, :] += new
            dkv[pl.ds(row, size), lanes] += dk
            dkv[pl.ds(row, size), more] += dv

    step(diag, TQ, True)

    @pl.when(extra > 0)
    def _():
        step(extra_row, TQ, False)

    def one(index, carry):
        step(pl.multiple_of(base + index * TK, TQ), TK, False)
        return carry

    lax.fori_loop(0, tiles, one, 0)
    for pair in range(PAIRS):
        lanes = slice(pair * 128, (pair + 1) * 128)
        dq_ref[:, lanes] = (jnp.transpose(dqt[lanes, :]) * HEAD_DIM ** (-0.5)).astype(BF)

    @pl.when(block == pl.num_programs(0) - 1)
    def _():
        def finish(index, carry):
            row = pl.multiple_of(index * TQ, TQ)
            kv[pl.ds(row, TQ), :HALF] = (dkv[pl.ds(row, TQ), :HALF] * (1.0 / LOG2E)).astype(BF)
            kv[pl.ds(row, TQ), HALF:] = dkv[pl.ds(row, TQ), HALF:].astype(BF)
            return carry

        lax.fori_loop(0, keys_all // TQ, finish, 0)
        one = pltpu.make_async_copy(kv.at[pl.ds(0, prompt_rows)], dkvp_hbm, sems.at[0])
        two = pltpu.make_async_copy(kv.at[pl.ds(prompt_rows, cont_rows)], dkvc_hbm, sems.at[1])
        one.start()
        two.start()
        one.wait()
        two.wait()


def attend_backward(info, q, do, o, lse, kvp, kvc):
    rows = q.shape[0]
    keys = kvp.shape[0] + kvc.shape[0]
    blocks = rows // TQ
    tile = pl.BlockSpec((TQ, HALF), lambda i, s: (i, 0))
    whole = pl.BlockSpec(memory_space=pl.ANY)
    return pl.pallas_call(
        attend_backward_kernel,
        grid_spec=pltpu.PrefetchScalarGridSpec(
            num_scalar_prefetch=1,
            grid=(blocks,),
            in_specs=[
                tile,
                tile,
                tile,
                pl.BlockSpec((1, 8, TQ), lambda i, s: (i, 0, 0)),
                whole,
                whole,
            ],
            out_specs=[tile, whole, whole],
            scratch_shapes=[
                pltpu.VMEM((keys, D), BF),
                pltpu.VMEM((HALF, keys), BF),
                pltpu.VMEM((keys, D), F32),
                pltpu.VMEM((NH, TQ, 128), BF),
                pltpu.VMEM((NH, TQ, 128), BF),
                pltpu.VMEM((HALF, TQ), F32),
                pltpu.VMEM((8, TQ), F32),
                pltpu.SemaphoreType.DMA((2,)),
            ],
        ),
        out_shape=(
            jax.ShapeDtypeStruct((rows, HALF), BF),
            jax.ShapeDtypeStruct(kvp.shape, BF),
            jax.ShapeDtypeStruct(kvc.shape, BF),
        ),
        compiler_params=pltpu.CompilerParams(
            dimension_semantics=("arbitrary",), vmem_limit_bytes=56 << 20
        ),
        cost_estimate=pl.CostEstimate(
            flops=int(10 * rows * PLEN * HALF * 4), bytes_accessed=30 << 20, transcendentals=0
        ),
        name="attend_backward",
    )(info, q, do, o, lse, kvp, kvc)


def normal_form(value):
    center = value - jnp.mean(value, axis=-1, keepdims=True)
    spread = jnp.mean(center * center, axis=-1, keepdims=True)
    return center * lax.rsqrt(spread + EPSILON)


def layer_norm(value, gain, shift):
    return normal_form(value) * gain + shift


def gelu_tanh(value):
    return jax.nn.gelu(value, approximate=True)


def row_sum(value):
    return jnp.sum(value.astype(F32), axis=0)


def body(
    prompt_in,
    cont_in,
    prompt_cot,
    cont_cot,
    cont_prompt,
    cont_len,
    ln1_gain,
    ln1_bias,
    attn_weight,
    attn_bias,
    proj_weight,
    proj_bias,
    ln2_gain,
    ln2_bias,
    fc_weight,
    fc_bias,
    out_weight,
    out_bias,
):
    fsdp = lax.axis_size("fsdp")
    devices = fsdp * lax.axis_size("grp")
    prow = prompt_in.shape[1]
    crow = cont_in.shape[1]
    conts = cont_prompt.shape[2]
    clen = crow // conts
    mine = prow + crow
    prompt_rows = NPR * PLEN
    place = lax.axis_index("fsdp")
    core = place % 2
    mate = [(i, i ^ 1) for i in range(fsdp)]
    chip_row = place // 2 * (2 * prow)
    share = D // devices
    wide = FF // D

    def swap(value):
        return lax.ppermute(value, "fsdp", mate)

    prompt_all = [lax.all_gather(prompt_in[m], "fsdp", axis=0, tiled=True) for m in range(MB)]
    cont_mate = swap(cont_in)
    plan_mate = swap(cont_prompt[:, 0, :].astype(F32)).astype(jnp.int32)

    vectors = (ln1_gain, ln1_bias, attn_bias[0], attn_bias[1], proj_bias, ln2_gain, ln2_bias, out_bias)
    columns = jnp.concatenate(
        [v[:, None] for v in vectors] + [fc_bias.reshape(share, wide)], axis=1
    )
    columns = jnp.pad(columns, ((0, 0), (0, 128 - columns.shape[1])))
    first = jnp.concatenate([attn_weight, columns], axis=1).astype(BF)
    first = lax.all_gather(first, ALL, axis=0, tiled=True)
    rest = jnp.concatenate([proj_weight, fc_weight, out_weight.reshape(share, FF)], axis=1).astype(BF)
    rest = lax.all_gather(rest, ALL, axis=0, tiled=True)
    small = first[:, 3 * D :].astype(F32)
    gain_a, shift_a, bias_q, bias_v, b_proj, gain_b, shift_b, b_out = (small[:, i] for i in range(8))
    b_fc = small[:, 8 : 8 + wide].reshape(FF)
    w_heads = lax.dynamic_index_in_dim(
        first[:, : 3 * D].reshape(D, 3, 2, HALF), core, axis=2, keepdims=False
    )
    w_q = w_heads[:, 0]
    w_kv = w_heads[:, 1:].reshape(D, D)
    bias_q = lax.dynamic_slice_in_dim(bias_q, core * HALF, HALF)
    bias_v = lax.dynamic_slice_in_dim(bias_v, core * HALF, HALF)
    bias_kv = jnp.concatenate([jnp.zeros((HALF,), F32), bias_v])
    w_proj = rest[:, :D]
    w_fc = rest[:, D : D + FF]
    w_out = rest[:, D + FF :].reshape(FF, D)

    first_place = chip_row % PLEN
    block_place = first_place + TQ * jnp.arange(2 * prow // TQ)
    prompt_plan = jnp.stack(
        [
            jnp.broadcast_to(chip_row - first_place, block_place.shape),
            block_place // TK,
            block_place % TK // TQ,
            chip_row + TQ * jnp.arange(2 * prow // TQ),
        ],
        axis=1,
    )

    def plan_of(m):
        follows = jnp.concatenate([cont_prompt[m, 0], plan_mate[m]])
        count = follows.shape[0]
        cont_plan = jnp.stack(
            [
                follows * PLEN,
                jnp.full((count,), PLEN // TK),
                jnp.zeros((count,), jnp.int32),
                prompt_rows + clen * jnp.arange(count),
            ],
            axis=1,
        )
        return jnp.concatenate([prompt_plan, cont_plan], axis=0).astype(jnp.int32)

    def split_rows(value):
        own = lax.dynamic_slice_in_dim(value, core * prow, prow, 0)
        other = lax.dynamic_slice_in_dim(value, (1 - core) * prow, prow, 0)
        return (
            jnp.concatenate([own, value[2 * prow : 2 * prow + crow]], axis=0),
            jnp.concatenate([other, value[2 * prow + crow :]], axis=0),
        )

    saved = []
    mixed = []
    for m in range(MB):
        a_prompt = layer_norm(prompt_all[m].astype(F32), gain_a, shift_a).astype(BF)
        cont_pair = jnp.concatenate([cont_in[m], cont_mate[m]], axis=0)
        a_cont = layer_norm(cont_pair.astype(F32), gain_a, shift_a).astype(BF)
        a_chip = jnp.concatenate(
            [lax.dynamic_slice_in_dim(a_prompt, chip_row, 2 * prow, 0), a_cont], axis=0
        )
        kvp = (jnp.dot(a_prompt, w_kv, preferred_element_type=F32) + bias_kv).astype(BF)
        kvc = (jnp.dot(a_cont, w_kv, preferred_element_type=F32) + bias_kv).astype(BF)
        query = ((jnp.dot(a_chip, w_q, preferred_element_type=F32) + bias_q) * QSCALE).astype(BF)
        plan = plan_of(m)
        o, lse = attend_forward(plan, query, kvp, kvc)
        own, other = split_rows(o)
        back = swap(other)
        mixed.append(
            jnp.where(
                core == 0,
                jnp.concatenate([own, back], axis=1),
                jnp.concatenate([back, own], axis=1),
            )
        )
        saved.append((a_prompt, a_cont, a_chip, kvp, kvc, query, plan, o, lse))

    inputs = jnp.concatenate([prompt_in, cont_in], axis=1).astype(F32).reshape(MB * mine, D)
    live = (jnp.arange(clen)[None, None, :] < cont_len[:, 0, :, None]).astype(F32)
    valid = jnp.concatenate(
        [jnp.ones((MB, prow), F32), live.reshape(MB, crow)], axis=1
    ).reshape(MB * mine)[:, None]
    ob = jnp.concatenate(mixed, axis=0)
    hidden = inputs + valid * (jnp.dot(ob, w_proj, preferred_element_type=F32) + b_proj)
    normed_second, pull_second = jax.vjp(layer_norm, hidden, gain_b, shift_b)
    second = normed_second.astype(BF)
    inner = jnp.dot(second, w_fc, preferred_element_type=F32) + b_fc
    active_full, pull_gelu = jax.vjp(gelu_tanh, inner)
    active = active_full.astype(BF)
    result = jnp.dot(active, w_out, preferred_element_type=F32) + b_out
    final = (hidden + valid * result).astype(BF).reshape(MB, mine, D)

    grad_out = jnp.concatenate([prompt_cot, cont_cot], axis=1).astype(F32).reshape(MB * mine, D)
    dz = (valid * grad_out).astype(BF)
    g_out_bias = row_sum(dz)
    g_out = jnp.einsum("rf,rd->fd", active, dz, preferred_element_type=F32)
    d_active = jnp.einsum("rd,fd->rf", dz, w_out, preferred_element_type=F32)
    du = pull_gelu(d_active)[0].astype(BF)
    g_fc_bias = row_sum(du)
    g_fc = jnp.einsum("rd,rf->df", second, du, preferred_element_type=F32)
    d_second = jnp.einsum("rf,df->rd", du, w_fc, preferred_element_type=F32)
    d_norm, g_gain_b, g_shift_b = pull_second(d_second)
    dh = grad_out + d_norm
    dy = (valid * dh).astype(BF)
    g_proj_bias = row_sum(dy)
    g_proj = jnp.einsum("rd,re->de", ob, dy, preferred_element_type=F32)
    dob = jnp.einsum("re,de->rd", dy, w_proj, preferred_element_type=F32).astype(BF)
    dob = dob.reshape(MB, mine, D)

    early = jnp.concatenate(
        [
            g_proj.astype(BF),
            g_fc.astype(BF),
            g_out.astype(BF).reshape(D, FF),
        ],
        axis=1,
    )
    early = lax.psum_scatter(early, ALL, scatter_dimension=0, tiled=True).astype(F32)

    g_q = g_kv = g_bias_q = g_bias_v = None
    d_rows = []
    for m in range(MB):
        a_prompt, a_cont, a_chip, kvp, kvc, query, plan, o, lse = saved[m]
        own = lax.dynamic_slice_in_dim(dob[m], core * HALF, HALF, 1)
        other = lax.dynamic_slice_in_dim(dob[m], (1 - core) * HALF, HALF, 1)
        back = swap(other)
        do = jnp.concatenate(
            [
                jnp.where(
                    core == 0,
                    jnp.concatenate([own[:prow], back[:prow]], axis=0),
                    jnp.concatenate([back[:prow], own[:prow]], axis=0),
                ),
                own[prow:],
                back[prow:],
            ],
            axis=0,
        )
        dq, dkvp, dkvc = attend_backward(plan, query, do, o, lse, kvp, kvc)
        table = jnp.einsum("re,de->rd", dkvp, w_kv, preferred_element_type=F32).astype(BF)
        table = lax.psum_scatter(table, "fsdp", scatter_dimension=0, tiled=True).astype(F32)
        part_q = jnp.einsum("rd,re->de", a_chip, dq, preferred_element_type=F32)
        part_kv = jnp.einsum(
            "rd,re->de", a_prompt, dkvp, preferred_element_type=F32
        ) + jnp.einsum("rd,re->de", a_cont, dkvc, preferred_element_type=F32)
        sum_q = row_sum(dq)
        sum_v = row_sum(dkvp[:, HALF:]) + row_sum(dkvc[:, HALF:])
        if g_q is None:
            g_q, g_kv, g_bias_q, g_bias_v = part_q, part_kv, sum_q, sum_v
        else:
            g_q, g_kv = g_q + part_q, g_kv + part_kv
            g_bias_q, g_bias_v = g_bias_q + sum_q, g_bias_v + sum_v
        chip = jnp.einsum("re,de->rd", dq, w_q, preferred_element_type=F32)
        cont = jnp.einsum("re,de->rd", dkvc, w_kv, preferred_element_type=F32)
        chip = jnp.concatenate([chip[: 2 * prow], chip[2 * prow :] + cont], axis=0)
        own, other = split_rows(chip)
        back = swap(other.astype(BF)).astype(F32)
        d_rows.append(
            own + back + jnp.concatenate([table, jnp.zeros((crow, D), F32)], axis=0)
        )

    heads = jnp.concatenate([g_q[:, None, None], g_kv.reshape(D, 2, 1, HALF)], axis=1)
    late = jnp.where(
        (jnp.arange(2) == core)[None, None, :, None], heads, 0.0
    ).reshape(D, 3 * D)
    late = lax.psum_scatter(late.astype(BF), ALL, scatter_dimension=0, tiled=True).astype(F32)

    d_first = jnp.concatenate(d_rows, axis=0)
    _, pull_first = jax.vjp(layer_norm, inputs, gain_a, shift_a)
    d_inputs, g_gain_a, g_shift_a = pull_first(d_first)
    d_inputs = (dh + d_inputs).astype(BF).reshape(MB, mine, D)

    def spread(value):
        return jnp.where((jnp.arange(2) == core)[:, None], value[None, :], 0.0).reshape(D)

    sums = jnp.stack(
        [
            g_gain_a,
            g_shift_a,
            spread(g_bias_q),
            spread(g_bias_v),
            g_proj_bias,
            g_gain_b,
            g_shift_b,
            g_out_bias,
        ]
        + [g_fc_bias.reshape(D, wide)[:, i] for i in range(wide)],
        axis=0,
    )
    sums = lax.psum(sums, ALL)
    index = lax.axis_index("grp") * fsdp + place
    sums = lax.dynamic_slice_in_dim(sums, index * share, share, 1)
    return (
        final[:, :prow],
        final[:, prow:],
        d_inputs[:, :prow],
        d_inputs[:, prow:],
        sums[0],
        sums[1],
        late,
        sums[2:4],
        early[:, :D],
        sums[4],
        sums[5],
        sums[6],
        early[:, D : D + FF],
        sums[8:].T.reshape(share * wide),
        early[:, D + FF :].reshape(share * wide, D),
        sums[7],
    )


def solution(mesh):
    rows = P(None, ALL, None)
    conts = P(None, "grp", "fsdp")
    vector = P(ALL)
    matrix = P(ALL, None)
    pair = P(None, ALL)
    params = (
        vector,
        vector,
        matrix,
        pair,
        matrix,
        vector,
        vector,
        vector,
        matrix,
        vector,
        matrix,
        vector,
    )
    return jax.shard_map(
        body,
        mesh=mesh,
        in_specs=(rows, rows, rows, rows, conts, conts) + params,
        out_specs=(rows, rows, rows, rows) + params,
        check_vma=False,
    )
```

time: 2900 us -> 1350 us (0.47)
  matrix products: 955 us -> 253 us
  local copies, waits for them, and re-layouts: 626 us -> 137 us
  waiting for transfers between devices: 793 us -> 494 us
  Pallas kernels: 0 us -> 241 us
  other arithmetic: 365 us -> 154 us
  blocking collectives: 123 us -> 39.6 us
    dot_general x72 -> x36, matrix products: 955 us -> 253 us  [the longest x1 38 us: body(): d_active = jnp.einsum('rd,fd->rf', dz, w_out, preferred_element_type=F32)]
    unnamed x618 -> x281, local copies, waits for them, and re-layouts: 335 us -> 29 us
    reduce_scatter x10 -> x5, waiting for transfers between devices: 558 us -> 305 us  [the longest x3 201 us: body(): lax.psum_scatter(table, 'fsdp', scatter_dimension=0, tiled=True).astype(F32)]
    pallas_call x0 -> x6, Pallas kernels: none -> 241 us  [the longest x3 155 us: attend_backward(): pl.pallas_call(attend_backward_kernel, grid_spec=pltpu.PrefetchScalarGrid...]
    convert_element_type x29 -> x8, other arithmetic: 252 us -> 29.1 us  [the longest x1 11.5 us: body(): a_prompt = layer_norm(prompt_all[m].astype(F32), gain_a, shift_a).astype(BF)]
    mul x18 -> x2, local copies, waits for them, and re-layouts: 114 us -> 1.92 us  [the longest x1 1.32 us: normal_form(): return center * lax.rsqrt(spread + EPSILON)]
    unnamed x2 -> x0, blocking collectives: 83.1 us -> none
    all_gather x10 -> x5, waiting for transfers between devices: 232 us -> 187 us  [the longest x3 152 us: body(): lax.all_gather(prompt_in[m], 'fsdp', axis=0, tiled=True)]
  transfers between devices with their start and end apart: 20 -> 21, of which waited for: 11 -> 10; matrix products, arithmetic and copies ran while one was open for 23% -> 25% of each run, Pallas kernels for 0% -> 14%
where the time goes in v1:
time: 1350 us; the launch traced here: 1340 us
  waiting for transfers between devices  494 us (37%)
  matrix products  253 us (19%)
  Pallas kernels  241 us (18%)
  other arithmetic  154 us (11%)
  local copies, waits for them, and re-layouts  137 us (10%)
  blocking collectives  39.6 us (3%)
  between operations  16.7 us (1%)
    reduce_scatter x3, waiting for transfers between devices, body(): lax.psum_scatter(table, 'fsdp', scatter_dimension=0, tiled=True).astype(F32)  201 us
    pallas_call x3, Pallas kernels, attend_backward(): pl.pallas_call(attend_backward_kernel, grid_spec=pltpu.PrefetchScalarGrid...  155 us
    all_gather x3, waiting for transfers between devices, body(): lax.all_gather(prompt_in[m], 'fsdp', axis=0, tiled=True)  152 us
    pallas_call x3, Pallas kernels, attend_forward(): pl.pallas_call(attend_forward_kernel, grid_spec=pltpu.PrefetchScalarGridS...  85.8 us
    reduce_scatter x1, waiting for transfers between devices, body(): lax.psum_scatter(early, ALL, scatter_dimension=0, tiled=True).astype(F32)  68.3 us
    psum x1, blocking collectives, body(): sums = lax.psum(sums, ALL)  39.6 us
    dot_general x1, matrix products, body(): d_active = jnp.einsum('rd,fd->rf', dz, w_out, preferred_element_type=F32)  38 us
    reduce_scatter x1, waiting for transfers between devices, body(): lax.psum_scatter(late.astype(BF), ALL, scatter_dimension=0, tiled=True)  35.2 us
  transfers between devices with their start and end apart: 21, of which 10 were waited for; matrix products, arithmetic and copies ran while one was open for 25% of the time, Pallas kernels for 14%

profile of v1, /device:TPU:0, one launch (start us, length us, event | category | flops | bytes accessed | tf_op | source)
XLA Modules:
  0.0 1338.3 jit_solution(9266293456691272614)
XLA Ops:
  43.7 35.1 %all-gather.9.cloned.1.call-done = bf16[768,2432]{1,0:T(8,128)(2,1)} async-done(((bf16[24,2432]{1,0:T(8,128)(2,1)}), bf16[768,2432]{1,0:T(8,128)(2,1)}) %all-gather.9.cloned.1.call-update) | async-done | bytes 3735568 | tf_op jit(solution)/shard_map/all_gather | solution.py:426
  82.8 5.8 copy.107
  110.3 34.4 %all-gather.17.cloned.1.call-done = bf16[1,4096,768]{2,1,0:T(8,128)(2,1)} async-done(((bf16[1,512,768]{2,1,0:T(8,128)(2,1)}), bf16[1,4096,768]{2,1,0:T(8,128)(2,1)}) %all-gather.17.cloned.1.call-update) | async-done | bytes 6291472 | tf_op jit(solution)/shard_map/all_gather | solution.py:416
  151.2 58.6 %all-gather.15.cloned.1.call-done = bf16[1,4096,768]{2,1,0:T(8,128)(2,1)} async-done(((bf16[1,512,768]{2,1,0:T(8,128)(2,1)}), bf16[1,4096,768]{2,1,0:T(8,128)(2,1)}) %all-gather.15.cloned.1.call-update) | async-done | bytes 6291472 | tf_op jit(solution)/shard_map/all_gather | solution.py:416
  216.2 59.0 %all-gather.13.cloned.1.call-done = bf16[1,4096,768]{2,1,0:T(8,128)(2,1)} async-done(((bf16[1,512,768]{2,1,0:T(8,128)(2,1)}), bf16[1,4096,768]{2,1,0:T(8,128)(2,1)}) %all-gather.13.cloned.1.call-update) | async-done | bytes 6291472 | tf_op jit(solution)/shard_map/all_gather | solution.py:416
  281.8 11.5 fusion.13
  298.4 7.2 add_convert_fusion.2.kvp_hbm
  305.5 28.5 %attend_forward.3 = (bf16[1536,384]{1,0:T(8,128)(2,1)S(1)}, f32[6,8,256]{2,1,0:T(8,128)S(1)}) custom-call(s32[6,4]{1,0:T(8,128)S(1)} %fusion.97.info, bf16[1536,384]{1,0:T(8,128)(2,1)S(1)} %fusion.50.q_ref, bf16[4096,768]{1,0:T(8,128)(2,1)} %add_convert_fusion.2.kvp_hbm, bf16[512,768]{1,0:T(8,128)(2,1)S(1)} %add_convert_fusion.7.kvc_hbm), custom_call_target="tpu_custom_call" | custom-call | flops 19327352832 | bytes 20971520 | tf_op jit(solution)/shard_map/attend_forward/pallas_call | solution.py:148
  342.3 7.2 add_convert_fusion.1.kvp_hbm
  349.5 28.8 %attend_forward.4 = (bf16[1536,384]{1,0:T(8,128)(2,1)S(1)}, f32[6,8,256]{2,1,0:T(8,128)S(1)}) custom-call(s32[6,4]{1,0:T(8,128)S(1)} %fusion.98.info, bf16[1536,384]{1,0:T(8,128)(2,1)S(1)} %fusion.51.q_ref, bf16[4096,768]{1,0:T(8,128)(2,1)} %add_convert_fusion.1.kvp_hbm, bf16[512,768]{1,0:T(8,128)(2,1)S(1)} %add_convert_fusion.6.kvc_hbm), custom_call_target="tpu_custom_call" | custom-call | flops 19327352832 | bytes 20971520 | tf_op jit(solution)/shard_map/attend_forward/pallas_call | solution.py:148
  382.7 7.2 add_convert_fusion.kvp_hbm
  389.8 28.5 %attend_forward.5 = (bf16[1536,384]{1,0:T(8,128)(2,1)S(1)}, f32[6,8,256]{2,1,0:T(8,128)S(1)}) custom-call(s32[6,4]{1,0:T(8,128)S(1)} %fusion.99.info, bf16[1536,384]{1,0:T(8,128)(2,1)S(1)} %fusion.52.q_ref, bf16[4096,768]{1,0:T(8,128)(2,1)} %add_convert_fusion.kvp_hbm, bf16[512,768]{1,0:T(8,128)(2,1)S(1)} %add_convert_fusion.5.kvc_hbm), custom_call_target="tpu_custom_call" | custom-call | flops 19327352832 | bytes 20971520 | tf_op jit(solution)/shard_map/attend_forward/pallas_call | solution.py:148
  435.6 7.3 fusion.135
  445.8 4.8 slice.401
  450.6 8.5 reshape.767
  459.1 26.0 %multiply_convert_fusion = (bf16[2304,3072]{1,0:T(8,128)(2,1)}, f32[2304,3072]{1,0:T(8,128)}) fusion(f32[3072]{0:T(1024)S(1)} %copy-done.106, bf16[768,6912]{1,0:T(8,128)(2,1)} %all-gather.11.cloned.1.call-done, f32[2304,768]{1,0:T(8,128)} %copy-done.32, f32[768]{0:T(1024)S(1)} %copy-done.121, f32[768]{0:T(1024)S(1)} %copy-done.99, f32[2304]{0:T(1024)S(1)} %fusion.96, ...), kind=kOutput, calls=%fused_computation.10 | convolution fusion | flops 10951262208 | bytes 54300672 | tf_op jit(solution)/shard_map/dot_general | solution.py:512
  485.1 38.0 %convert_reduce_fusion = (f32[3072]{0:T(1024)}, bf16[2304,3072]{1,0:T(8,128)(2,1)}) fusion(f32[2304,3072]{1,0:T(8,128)} %get-tuple-element.138, f32[3072]{0:T(1024)S(1)} %copy-done.106, bf16[2304,768]{1,0:T(8,128)(2,1)} %bitcast.245, bf16[3072,768]{1,0:T(8,128)(2,1)} %reshape.767), kind=kOutput, calls=%fused_computation.9 | convolution fusion | flops 11034424320 | bytes 50749440 | tf_op jit(solution)/shard_map/rd,fd->rf/dot_general | solution.py:522
  523.1 18.7 %multiply_reduce_fusion = (f32[768]{0:T(1024)}, f32[2304]{0:T(1024)S(1)}, f32[768]{0:T(1024)}, f32[2304,768]{1,0:T(8,128)}) fusion(f32[2304,768]{1,0:T(8,128)S(1)} %bitcast.213, f32[2304]{0:T(1024)S(1)} %fusion.96, f32[2304]{0:T(1024)S(1)} %broadcast_multiply_fusion.4, f32[768]{0:T(1024)S(1)} %copy-done.99, bf16[2304,3072]{1,0:T(8,128)(2,1)} %get-tuple-element.141, ...), kind=kOutput, calls=%fused_computation.70 | convolution fusion | flops 10885787648 | bytes 33067008 | tf_op jit(solution)/shard_map/rf,df->rd/dot_general | solution.py:526
  541.9 5.6 fusion.124
  547.6 4.6 convert_reduce_fusion.6
  552.2 5.4 convolution_convert_fusion.4
  561.5 51.5 %attend_backward.4 = (bf16[1536,384]{1,0:T(8,128)(2,1)}, bf16[4096,768]{1,0:T(8,128)(2,1)}, bf16[512,768]{1,0:T(8,128)(2,1)}) custom-call(s32[6,4]{1,0:T(8,128)} %copy-done.5, bf16[1536,384]{1,0:T(8,128)(2,1)} %copy-done.11, bf16[1536,384]{1,0:T(8,128)(2,1)} %pad_maximum_fusion.24.do_ref, bf16[1536,384]{1,0:T(8,128)(2,1)} %copy-done.2, ...), custom_call_target="tpu_custom_call" | custom-call | flops 48318382080 | bytes 31457280 | tf_op jit(solution)/shard_map/attend_backward/pallas_call | solution.py:320
  614.5 52.0 %attend_backward.3 = (bf16[1536,384]{1,0:T(8,128)(2,1)}, bf16[4096,768]{1,0:T(8,128)(2,1)}, bf16[512,768]{1,0:T(8,128)(2,1)}) custom-call(s32[6,4]{1,0:T(8,128)} %copy-done.4, bf16[1536,384]{1,0:T(8,128)(2,1)} %copy-done.9, bf16[1536,384]{1,0:T(8,128)(2,1)} %pad_maximum_fusion.22.do_ref, bf16[1536,384]{1,0:T(8,128)(2,1)} %copy-done, ...), custom_call_target="tpu_custom_call" | custom-call | flops 48318382080 | bytes 31457280 | tf_op jit(solution)/shard_map/attend_backward/pallas_call | solution.py:320
  671.6 51.5 %attend_backward.5 = (bf16[1536,384]{1,0:T(8,128)(2,1)}, bf16[4096,768]{1,0:T(8,128)(2,1)}, bf16[512,768]{1,0:T(8,128)(2,1)}) custom-call(s32[6,4]{1,0:T(8,128)} %copy-done.3, bf16[1536,384]{1,0:T(8,128)(2,1)} %copy-done.10, bf16[1536,384]{1,0:T(8,128)(2,1)} %pad_maximum_fusion.26.do_ref, bf16[1536,384]{1,0:T(8,128)(2,1)} %copy-done.1, ...), custom_call_target="tpu_custom_call" | custom-call | flops 48318382080 | bytes 31457280 | tf_op jit(solution)/shard_map/attend_backward/pallas_call | solution.py:320
  728.1 9.2 fusion.136
  738.3 7.8 fusion.138
  747.0 5.8 fusion.140
  759.4 4.6 broadcast_in_dim.154
  764.0 7.5 broadcast_in_dim.155
  775.2 9.9 convolution_convert_fusion.2
  785.2 9.7 convolution_convert_fusion.1
  794.9 9.7 convolution_convert_fusion
  813.3 6.1 convolution_convert_fusion.6
  821.7 17.0 %convolution_convert_fusion.5 = bf16[3072,768]{1,0:T(8,128)(2,1)} fusion(bf16[2304,3072]{1,0:T(8,128)(2,1)} %get-tuple-element.137, bf16[2304,768]{1,0:T(8,128)(2,1)} %get-tuple-element.73), kind=kOutput, calls=%fused_computation.97 | convolution fusion | flops 10873995264 | bytes 22413312 | tf_op jit(solution)/shard_map/rf,rd->fd/dot_general | solution.py:521
  838.7 8.5 reshape.775
  847.2 18.5 %convolution_convert_fusion.3 = bf16[768,3072]{1,0:T(8,128)(2,1)S(1)} fusion(bf16[2304,3072]{1,0:T(8,128)(2,1)} %get-tuple-element.141, f32[2304,768]{1,0:T(8,128)} %copy-done.32, f32[768]{0:T(1024)} %get-tuple-element.104, f32[768]{0:T(1024)S(1)} %copy-done.100, f32[2304]{0:T(1024)} %copy-done.95, f32[2304]{0:T(1024)} %copy-done.89), kind=kOutput, calls=%fused_computation.95 | convolution fusion | flops 10882842624 | bytes 25976832 | tf_op jit(solution)/shard_map/rd,rf->df/dot_general | solution.py:525
  865.8 4.7 pad_maximum_fusion
  871.2 17.5 %add_convert_fusion.3 = bf16[2304,768]{1,0:T(8,128)(2,1)S(1)} fusion(f32[2304,768]{1,0:T(8,128)} %copy-done.32, bf16[2304,3072]{1,0:T(8,128)(2,1)} %get-tuple-element.137, bf16[3072,768]{1,0:T(8,128)(2,1)} %reshape.767, f32[768]{0:T(1024)S(1)} %copy-done.120, f32[2304]{0:T(1024)} %mul.454), kind=kOutput, calls=%fused_computation.74 | convolution fusion | flops 10878713856 | bytes 29503488 | tf_op jit(solution)/shard_map/dot_general | solution.py:515
  933.3 35.2 %reduce-scatter.12.cloned.1.call-done = bf16[24,2304]{1,0:T(8,128)(2,1)} async-done(((bf16[768,2304]{1,0:T(8,128)(2,1)}), bf16[24,2304]{1,0:T(8,128)(2,1)}) %reduce-scatter.12.cloned.1.call-update) | async-done | bytes 110608 | tf_op jit(solution)/shard_map/reduce_scatter | solution.py:591
  970.1 69.4 %reduce-scatter.6.cloned.1.call-done = bf16[512,768]{1,0:T(8,128)(2,1)} async-done(((bf16[4096,768]{1,0:T(8,128)(2,1)}), bf16[512,768]{1,0:T(8,128)(2,1)}) %reduce-scatter.6.cloned.1.call-update) | async-done | bytes 786448 | tf_op jit(solution)/shard_map/reduce_scatter | solution.py:566
  1044.1 65.9 %reduce-scatter.8.cloned.1.call-done = bf16[512,768]{1,0:T(8,128)(2,1)} async-done(((bf16[4096,768]{1,0:T(8,128)(2,1)}), bf16[512,768]{1,0:T(8,128)(2,1)}) %reduce-scatter.8.cloned.1.call-update) | async-done | bytes 786448 | tf_op jit(solution)/shard_map/reduce_scatter | solution.py:566
  1110.0 4.6 fusion.118
  1114.6 65.9 %reduce-scatter.10.cloned.1.call-done = bf16[512,768]{1,0:T(8,128)(2,1)} async-done(((bf16[4096,768]{1,0:T(8,128)(2,1)}), bf16[512,768]{1,0:T(8,128)(2,1)}) %reduce-scatter.10.cloned.1.call-update) | async-done | bytes 786448 | tf_op jit(solution)/shard_map/reduce_scatter | solution.py:566
  1185.4 4.9 fusion.38
  1196.9 8.6 fusion.40
  1205.6 8.5 fusion.30
  1217.1 39.6 %psum.7 = f32[12,768]{1,0:T(8,128)S(1)} all-reduce(f32[12,768]{1,0:T(8,128)S(1)} %stack.40), channel_id=1, replica_groups=mesh['grp'=4,'fsdp'=8] {'grp','fsdp'}, use_global_device_ids=true, to_apply=%region_41.42 | all-reduce | flops 9216 | bytes 73728 | tf_op jit(solution)/shard_map/psum | solution.py:615
  1258.8 68.3 %reduce-scatter.14.cloned.1.call-done = bf16[24,6912]{1,0:T(8,128)(2,1)} async-done(((bf16[768,6912]{1,0:T(8,128)(2,1)}), bf16[24,6912]{1,0:T(8,128)(2,1)}) %reduce-scatter.14.cloned.1.call-update) | async-done | bytes 331792 | tf_op jit(solution)/shard_map/reduce_scatter | solution.py:543
  (552 shorter events, 228.6 us)
Async XLA Ops:
  7.2 71.6 %all-gather.9.cloned.1.call-start = ((), (), s32[]{:S(2)}) async-start(), calls=%async_computation.5 | async-start | bytes 3852288 | tf_op jit(solution)/shard_map/all_gather | solution.py:426
  15.2 129.5 %all-gather.17.cloned.1.call-start = ((), (), s32[]{:S(2)}) async-start(), calls=%async_computation.14 | async-start | bytes 7077888 | tf_op jit(solution)/shard_map/all_gather | solution.py:416
  18.3 191.4 %all-gather.15.cloned.1.call-start = ((), (), s32[]{:S(2)}) async-start(), calls=%async_computation.13 | async-start | bytes 7077888 | tf_op jit(solution)/shard_map/all_gather | solution.py:416
  19.1 256.2 %all-gather.13.cloned.1.call-start = ((), (), s32[]{:S(2)}) async-start(), calls=%async_computation.12 | async-start | bytes 7077888 | tf_op jit(solution)/shard_map/all_gather | solution.py:416
  19.7 416.0 %all-gather.11.cloned.1.call-start = ((), (), s32[]{:S(2)}) async-start(), calls=%async_computation.6 | async-start | bytes 10948608 | tf_op jit(solution)/shard_map/all_gather | solution.py:428
  19.7 20.9 %collective-permute-start.1 = (bf16[3,256,768]{2,1,0:T(8,128)(2,1)S(1)}, bf16[3,256,768]{2,1,0:T(8,128)(2,1)}, u32[]{:S(2)}, u32[]{:S(2)}) collective-permute-start(bf16[3,256,768]{2,1,0:T(8,128)(2,1)S(1)} %copy-done.18), channel_id=1, source_target_pairs={{0,1},{1,0},{2,3},{3,2},{4,5},{5,4},{6,7},{7,6},{8,9},{9,8},{10,11... | collective-permute-start | bytes 3538952 | tf_op jit(solution)/shard_map/ppermute | solution.py:414
  20.3 10.8 copy-start.33
  20.3 14.8 %collective-permute-start = (f32[3,1]{1,0:T(4,128)S(1)}, f32[3,1]{1,0:T(4,128)}, u32[]{:S(2)}, u32[]{:S(2)}) collective-permute-start(f32[3,1]{1,0:T(4,128)S(1)} %copy.88), channel_id=1, source_target_pairs={{0,1},{1,0},{2,3},{3,2},{4,5},{5,4},{6,7},{7,6},{8,9},{9,8},{10,11... | collective-permute-start | bytes 44 | tf_op jit(solution)/shard_map/ppermute | solution.py:414
  27.4 941.1 %reduce-scatter.12.cloned.1.call-start = ((), (), s32[]{:S(2)}) async-start(), calls=%async_computation.10 | async-start | bytes 3649536 | tf_op jit(solution)/shard_map/reduce_scatter | solution.py:591
  40.4 265.1 %copy-start.4 = (s32[6,4]{1,0:T(8,128)}, s32[6,4]{1,0:T(8,128)S(1)}, u32[]{:S(2)}) copy-start(s32[6,4]{1,0:T(8,128)S(1)} %fusion.97.info) | copy-start | bytes 292
  40.5 309.0 %copy-start.5 = (s32[6,4]{1,0:T(8,128)}, s32[6,4]{1,0:T(8,128)S(1)}, u32[]{:S(2)}) copy-start(s32[6,4]{1,0:T(8,128)S(1)} %fusion.98.info) | copy-start | bytes 292
  40.6 349.2 %copy-start.3 = (s32[6,4]{1,0:T(8,128)}, s32[6,4]{1,0:T(8,128)S(1)}, u32[]{:S(2)}) copy-start(s32[6,4]{1,0:T(8,128)S(1)} %fusion.99.info) | copy-start | bytes 292
  94.3 11.9 copy-start.41
  98.7 183.1 %copy-start.87 = (f32[768]{0:T(1024)}, f32[768]{0:T(1024)S(1)}, u32[]{:S(2)}) copy-start(f32[768]{0:T(1024)S(1)} %get-tuple-element.100) | copy-start | bytes 9220
  107.0 198.5 %copy-start.7 = (bf16[512,768]{1,0:T(8,128)(2,1)}, bf16[512,768]{1,0:T(8,128)(2,1)S(1)}, u32[]{:S(2)}) copy-start(bf16[512,768]{1,0:T(8,128)(2,1)S(1)} %add_convert_fusion.7.kvc_hbm) | copy-start | bytes 2359300
  107.9 241.6 %copy-start.8 = (bf16[512,768]{1,0:T(8,128)(2,1)}, bf16[512,768]{1,0:T(8,128)(2,1)S(1)}, u32[]{:S(2)}) copy-start(bf16[512,768]{1,0:T(8,128)(2,1)S(1)} %add_convert_fusion.6.kvc_hbm) | copy-start | bytes 2359300
  110.3 279.6 %copy-start.6 = (bf16[512,768]{1,0:T(8,128)(2,1)}, bf16[512,768]{1,0:T(8,128)(2,1)S(1)}, u32[]{:S(2)}) copy-start(bf16[512,768]{1,0:T(8,128)(2,1)S(1)} %add_convert_fusion.5.kvc_hbm) | copy-start | bytes 2359300
  336.6 90.3 %collective-permute-start.2 = (bf16[768,384]{1,0:T(8,128)(2,1)}, bf16[768,384]{1,0:T(8,128)(2,1)}, u32[]{:S(2)}, u32[]{:S(2)}) collective-permute-start(bf16[768,384]{1,0:T(8,128)(2,1)} %pad_maximum_fusion.31), channel_id=1, source_target_pairs={{0,1},{1,0},{2,3},{3,2},{4,5},{5,4},{6,7},{7,6},{8,9},{9,8},{10,11... | collective-permute-start | bytes 1769480 | tf_op jit(solution)/shard_map/ppermute | solution.py:414
  339.2 41.7 %copy-start.80 = (bf16[1024,768]{1,0:T(8,128)(2,1)}, bf16[1024,768]{1,0:T(8,128)(2,1)S(1)}, u32[]{:S(2)}) copy-start(bf16[1024,768]{1,0:T(8,128)(2,1)S(1)} %get-tuple-element.152) | copy-start | bytes 4718596
  380.8 49.2 %collective-permute-start.3 = (bf16[768,384]{1,0:T(8,128)(2,1)}, bf16[768,384]{1,0:T(8,128)(2,1)}, u32[]{:S(2)}, u32[]{:S(2)}) collective-permute-start(bf16[768,384]{1,0:T(8,128)(2,1)} %pad_maximum_fusion.32), channel_id=1, source_target_pairs={{0,1},{1,0},{2,3},{3,2},{4,5},{5,4},{6,7},{7,6},{8,9},{9,8},{10,11... | collective-permute-start | bytes 1769480 | tf_op jit(solution)/shard_map/ppermute | solution.py:414
  389.8 32.1 %copy-start.91 = (f32[3,768]{1,0:T(4,128)S(1)}, f32[3,768]{1,0:T(4,128)}, u32[]{:S(2)}) copy-start(f32[3,768]{1,0:T(4,128)} %copy-done.90) | copy-start | bytes 27652
  421.1 11.9 collective-permute-start.4
  443.0 98.9 %copy-start.89 = (f32[2304]{0:T(1024)}, f32[2304]{0:T(1024)S(1)}, u32[]{:S(2)}) copy-start(f32[2304]{0:T(1024)S(1)} %broadcast_multiply_fusion.4) | copy-start | bytes 27652
  445.8 96.1 %copy-start.95 = (f32[2304]{0:T(1024)}, f32[2304]{0:T(1024)S(1)}, u32[]{:S(2)}) copy-start(f32[2304]{0:T(1024)S(1)} %fusion.96) | copy-start | bytes 27652
  459.1 64.0 %slice-start = ((s8[7077888]{0:T(1024)(128)(4,1)}), s8[4194304]{0:T(1024)(128)(4,1)S(1)}, s32[]{:S(2)}) async-start(s8[7077888]{0:T(1024)(128)(4,1)} %bitcast.212), calls=%async_computation.15 | async-start | bytes 8388608
  485.1 38.0 %slice-start.1 = ((s8[7077888]{0:T(1024)(128)(4,1)}), s8[2883584]{0:T(1024)(128)(4,1)S(1)}, s32[]{:S(2)}) async-start(s8[7077888]{0:T(1024)(128)(4,1)} %bitcast.212), calls=%async_computation.16 | async-start | bytes 5767168
  557.9 2.1 collective-permute-start.7
  558.2 54.8 %collective-permute-start.5 = (bf16[768,384]{1,0:T(8,128)(2,1)S(1)}, bf16[768,384]{1,0:T(8,128)(2,1)S(1)}, u32[]{:S(2)}, u32[]{:S(2)}) collective-permute-start(bf16[768,384]{1,0:T(8,128)(2,1)S(1)} %constant_dynamic-slice_fusion.6), channel_id=1, source_target_pairs={{0,1},{1,0},{2,3},{3,2},{4,5},{5,4},{6,7},{7,6},{8,9},{9,8},{10,11... | collective-permute-start | bytes 1769480 | tf_op jit(solution)/shard_map/ppermute | solution.py:414
  558.7 111.3 %collective-permute-start.9 = (bf16[768,384]{1,0:T(8,128)(2,1)S(1)}, bf16[768,384]{1,0:T(8,128)(2,1)S(1)}, u32[]{:S(2)}, u32[]{:S(2)}) collective-permute-start(bf16[768,384]{1,0:T(8,128)(2,1)S(1)} %constant_dynamic-slice_fusion.3), channel_id=1, source_target_pairs={{0,1},{1,0},{2,3},{3,2},{4,5},{5,4},{6,7},{7,6},{8,9},{9,8},{10,11... | collective-permute-start | bytes 1769480 | tf_op jit(solution)/shard_map/ppermute | solution.py:414
  614.5 52.1 %copy-start.47 = (bf16[1536,384]{1,0:T(8,128)(2,1)S(1)}, bf16[1536,384]{1,0:T(8,128)(2,1)}, u32[]{:S(2)}) copy-start(bf16[1536,384]{1,0:T(8,128)(2,1)} %get-tuple-element.39) | copy-start | bytes 3538948
  614.5 52.1 %copy-start.60 = (bf16[512,768]{1,0:T(8,128)(2,1)S(1)}, bf16[512,768]{1,0:T(8,128)(2,1)}, u32[]{:S(2)}) copy-start(bf16[512,768]{1,0:T(8,128)(2,1)} %copy-done.58) | copy-start | bytes 2359300
  614.5 52.1 %copy-start.85 = (bf16[1024,768]{1,0:T(8,128)(2,1)S(1)}, bf16[1024,768]{1,0:T(8,128)(2,1)}, u32[]{:S(2)}) copy-start(bf16[1024,768]{1,0:T(8,128)(2,1)} %copy-done.84) | copy-start | bytes 4718596
  671.6 51.5 %copy-start.77 = (bf16[512,768]{1,0:T(8,128)(2,1)S(1)}, bf16[512,768]{1,0:T(8,128)(2,1)}, u32[]{:S(2)}) copy-start(bf16[512,768]{1,0:T(8,128)(2,1)} %copy-done.75) | copy-start | bytes 2359300
  671.6 51.5 %copy-start.81 = (bf16[1024,768]{1,0:T(8,128)(2,1)S(1)}, bf16[1024,768]{1,0:T(8,128)(2,1)}, u32[]{:S(2)}) copy-start(bf16[1024,768]{1,0:T(8,128)(2,1)} %copy-done.80) | copy-start | bytes 4718596
  723.1 15.1 %slice-start.8 = ((s8[6291456]{0:T(1024)(128)(4,1)}), s8[2097152]{0:T(1024)(128)(4,1)S(1)}, s32[]{:S(2)}) async-start(s8[6291456]{0:T(1024)(128)(4,1)} %bitcast.241), calls=%async_computation.23 | async-start | bytes 4194304
  728.1 10.1 slice-start.9
  737.4 9.6 slice-start.4
  737.4 9.6 slice-start.14
  774.0 265.6 %reduce-scatter.6.cloned.1.call-start = ((), (), s32[]{:S(2)}) async-start(), calls=%async_computation.7 | async-start | bytes 7077888 | tf_op jit(solution)/shard_map/reduce_scatter | solution.py:566
  785.1 324.9 %reduce-scatter.8.cloned.1.call-start = ((), (), s32[]{:S(2)}) async-start(), calls=%async_computation.8 | async-start | bytes 7077888 | tf_op jit(solution)/shard_map/reduce_scatter | solution.py:566
  794.9 385.6 %reduce-scatter.10.cloned.1.call-start = ((), (), s32[]{:S(2)}) async-start(), calls=%async_computation.9 | async-start | bytes 7077888 | tf_op jit(solution)/shard_map/reduce_scatter | solution.py:566
  804.7 522.4 %reduce-scatter.14.cloned.1.call-start = ((), (), s32[]{:S(2)}) async-start(), calls=%async_computation.11 | async-start | bytes 10948608 | tf_op jit(solution)/shard_map/reduce_scatter | solution.py:543
  847.2 18.6 %copy-start.40 = (bf16[768,3072]{1,0:T(8,128)(2,1)S(1)}, bf16[768,3072]{1,0:T(8,128)(2,1)}, u32[]{:S(2)}) copy-start(bf16[768,3072]{1,0:T(8,128)(2,1)} %reshape.775) | copy-start | bytes 14155780
  847.2 18.6 %copy-start.71 = (bf16[768,768]{1,0:T(8,128)(2,1)S(1)}, bf16[768,768]{1,0:T(8,128)(2,1)}, u32[]{:S(2)}) copy-start(bf16[768,768]{1,0:T(8,128)(2,1)} %copy.104) | copy-start | bytes 3538948
  906.2 63.9 %collective-permute-start.6 = (bf16[768,768]{1,0:T(8,128)(2,1)}, bf16[768,768]{1,0:T(8,128)(2,1)}, u32[]{:S(2)}, u32[]{:S(2)}) collective-permute-start(bf16[768,768]{1,0:T(8,128)(2,1)} %pad_maximum_fusion.23), channel_id=1, source_target_pairs={{0,1},{1,0},{2,3},{3,2},{4,5},{5,4},{6,7},{7,6},{8,9},{9,8},{10,11... | collective-permute-start | bytes 3538952 | tf_op jit(solution)/shard_map/ppermute | solution.py:414
  912.2 131.9 %collective-permute-start.8 = (bf16[768,768]{1,0:T(8,128)(2,1)}, bf16[768,768]{1,0:T(8,128)(2,1)}, u32[]{:S(2)}, u32[]{:S(2)}) collective-permute-start(bf16[768,768]{1,0:T(8,128)(2,1)} %pad_maximum_fusion.25), channel_id=1, source_target_pairs={{0,1},{1,0},{2,3},{3,2},{4,5},{5,4},{6,7},{7,6},{8,9},{9,8},{10,11... | collective-permute-start | bytes 3538952 | tf_op jit(solution)/shard_map/ppermute | solution.py:414
  923.7 190.9 %collective-permute-start.10 = (bf16[768,768]{1,0:T(8,128)(2,1)}, bf16[768,768]{1,0:T(8,128)(2,1)}, u32[]{:S(2)}, u32[]{:S(2)}) collective-permute-start(bf16[768,768]{1,0:T(8,128)(2,1)} %pad_maximum_fusion.27), channel_id=1, source_target_pairs={{0,1},{1,0},{2,3},{3,2},{4,5},{5,4},{6,7},{7,6},{8,9},{9,8},{10,11... | collective-permute-start | bytes 3538952 | tf_op jit(solution)/shard_map/ppermute | solution.py:414
  1114.6 70.8 %copy-start.88 = (f32[768]{0:T(1024)S(1)}, f32[768]{0:T(1024)}, u32[]{:S(2)}) copy-start(f32[768]{0:T(1024)} %copy-done.87) | copy-start | bytes 9220
  (112 other events, 447.1 us)
Sparse Core Ops, SparseCore 0:
  15.3 63.4 all-gather.8
  81.0 63.5 all-gather.16
  146.3 63.3 all-gather.14
  211.8 63.3 all-gather.12
  278.1 86.1 all-gather.10
  774.1 194.3 reduce-scatter.11
  970.8 68.6 reduce-scatter.5
  1041.8 68.1 reduce-scatter.7
  1112.4 68.1 reduce-scatter.9
  1186.5 140.5 reduce-scatter.13

commit v2 on v1

v2 whole, which is shorter than its diff:
```python
import functools
import math

import jax
import jax.numpy as jnp
from jax import lax
from jax.experimental import pallas as pl
from jax.experimental.pallas import tpu as pltpu
from jax.sharding import PartitionSpec as P

D = 768
HEADS = 12
HEAD_DIM = 64
FF = 3072
MB = 3
NPR = 2
PLEN = 2048
ALL = ("grp", "fsdp")

EPSILON = 1e-05
MASKED = -1e30
BF = jnp.bfloat16
F32 = jnp.float32

HALF = D // 2
NH = HEADS // 2
PAIRS = NH // 2
TK = 512
LOG2E = math.log2(math.e)
QSCALE = HEAD_DIM ** (-0.5) * LOG2E


def dot_nt(a, b):
    return lax.dot_general(a, b, (((1,), (1,)), ((), ())), preferred_element_type=F32)


def dot_nn(a, b):
    return lax.dot_general(a, b, (((1,), (0,)), ((), ())), preferred_element_type=F32)


def half_masks(rows):
    lane = lax.broadcasted_iota(jnp.int32, (rows, 128), 1)
    return (lane < HEAD_DIM, lane >= HEAD_DIM)


def attend_forward_kernel(
    info, q_ref, kvp_hbm, kvc_hbm, o_ref, lse_ref, kv, qm, s_ref, mx, acc, sems
):
    block = pl.program_id(0)
    prompt_rows = kvp_hbm.shape[0]
    cont_rows = kvc_hbm.shape[0]

    @pl.when(block == 0)
    def _():
        one = pltpu.make_async_copy(kvp_hbm, kv.at[pl.ds(0, prompt_rows)], sems.at[0])
        two = pltpu.make_async_copy(kvc_hbm, kv.at[pl.ds(prompt_rows, cont_rows)], sems.at[1])
        one.start()
        two.start()
        one.wait()
        two.wait()

    TQ = q_ref.shape[0]
    base = pl.multiple_of(info[block, 0], TQ)
    tiles = info[block, 1]
    extra = info[block, 2]
    extra_row = pl.multiple_of(info[block, 3], TQ)
    diag = pl.multiple_of(info[block, 4], TQ)
    low, high = half_masks(TQ)
    zero = jnp.zeros((TQ, 128), BF)
    for pair in range(PAIRS):
        part = q_ref[:, pair * 128 : (pair + 1) * 128]
        qm[2 * pair] = jnp.where(low, part, zero)
        qm[2 * pair + 1] = jnp.where(high, part, zero)

    def score(pair, row, size, column, first, masked):
        keys = kv[pl.ds(row, size), pair * 128 : (pair + 1) * 128]
        for side in (0, 1):
            raw = dot_nt(qm[2 * pair + side], keys)
            if masked:
                across = lax.broadcasted_iota(jnp.int32, (TQ, size), 1)
                down = lax.broadcasted_iota(jnp.int32, (TQ, size), 0)
                raw = jnp.where(across <= down, raw, MASKED)
            slot = 2 * (pair % 2) + side
            s_ref[slot, :, pl.ds(column, size)] = raw
            top = raw[:, :128]
            for piece in range(1, size // 128):
                top = jnp.maximum(top, raw[:, piece * 128 : (piece + 1) * 128])
            if not first:
                top = jnp.maximum(top, mx[slot])
            mx[slot] = top

    def settle(pair):
        for side in (0, 1):
            slot = 2 * (pair % 2) + side
            top = jnp.max(mx[slot], axis=1, keepdims=True)
            mx[slot] = jnp.broadcast_to(top, (TQ, 128))

    def blend(pair, row, size, column, first):
        vals = kv[pl.ds(row, size), HALF + pair * 128 : HALF + (pair + 1) * 128]
        wide = jnp.concatenate([vals, jnp.ones((size, 128), BF)], axis=1)
        for side in (0, 1):
            slot = 2 * (pair % 2) + side
            top = jnp.concatenate([mx[slot]] * (size // 128), axis=1)
            power = jnp.exp2(s_ref[slot, :, pl.ds(column, size)] - top).astype(BF)
            new = dot_nn(power, wide)
            if first:
                acc[side] = new
            else:
                acc[side] += new

    def sweep(step):
        step(diag, TQ, 0, True)

        def some(index, carry):
            row = pl.multiple_of(extra_row + index * TQ, TQ)
            step(row, TQ, pl.multiple_of(TQ + index * TQ, TQ), False)
            return carry

        lax.fori_loop(0, extra, some, 0)

        def one(index, carry):
            row = pl.multiple_of(base + index * TK, TQ)
            step(row, TK, pl.multiple_of(TK + index * TK, TQ), False)
            return carry

        lax.fori_loop(0, tiles, one, 0)

    sweep(lambda row, size, column, first: score(0, row, size, column, first, first))
    for pair in range(PAIRS):
        settle(pair)

        def both(row, size, column, first):
            if pair + 1 < PAIRS:
                score(pair + 1, row, size, column, first, first)
            blend(pair, row, size, column, first)

        sweep(both)
        sides = []
        for side in (0, 1):
            total = acc[side][:, 128:]
            sides.append(acc[side][:, :128] / total)
            tall = jnp.transpose(mx[2 * (pair % 2) + side] + jnp.log2(total))
            lse_ref[0, 2 * pair + side] = tall[0]
        o_ref[:, pair * 128 : (pair + 1) * 128] = jnp.where(low, sides[0], sides[1]).astype(BF)


def attend_forward(info, q, kvp, kvc, TQ):
    rows = q.shape[0]
    keys = kvp.shape[0] + kvc.shape[0]
    blocks = rows // TQ
    return pl.pallas_call(
        attend_forward_kernel,
        grid_spec=pltpu.PrefetchScalarGridSpec(
            num_scalar_prefetch=1,
            grid=(blocks,),
            in_specs=[
                pl.BlockSpec((TQ, HALF), lambda i, s: (i, 0)),
                pl.BlockSpec(memory_space=pl.ANY),
                pl.BlockSpec(memory_space=pl.ANY),
            ],
            out_specs=[
                pl.BlockSpec((TQ, HALF), lambda i, s: (i, 0)),
                pl.BlockSpec((1, 8, TQ), lambda i, s: (i, 0, 0)),
            ],
            scratch_shapes=[
                pltpu.VMEM((keys, D), BF),
                pltpu.VMEM((NH, TQ, 128), BF),
                pltpu.VMEM((4, TQ, PLEN + TK), F32),
                pltpu.VMEM((4, TQ, 128), F32),
                pltpu.VMEM((2, TQ, 256), F32),
                pltpu.SemaphoreType.DMA((2,)),
            ],
        ),
        out_shape=(
            jax.ShapeDtypeStruct((rows, HALF), BF),
            jax.ShapeDtypeStruct((blocks, 8, TQ), F32),
        ),
        compiler_params=pltpu.CompilerParams(
            dimension_semantics=("arbitrary",), vmem_limit_bytes=50 << 20
        ),
        cost_estimate=pl.CostEstimate(
            flops=int(4 * rows * PLEN * HALF * 4), bytes_accessed=20 << 20, transcendentals=0
        ),
        name="attend_forward",
    )(info, q, kvp, kvc)


def attend_backward_kernel(
    info,
    q_ref,
    do_ref,
    o_ref,
    lse_ref,
    kvp_hbm,
    kvc_hbm,
    dq_ref,
    dkvp_hbm,
    dkvc_hbm,
    kv,
    kt,
    dkv,
    qm,
    dom,
    dqt,
    drow,
    sems,
):
    TQ = q_ref.shape[0]
    block = pl.program_id(0)
    prompt_rows = kvp_hbm.shape[0]
    cont_rows = kvc_hbm.shape[0]
    keys_all = prompt_rows + cont_rows

    @pl.when(block == 0)
    def _():
        one = pltpu.make_async_copy(kvp_hbm, kv.at[pl.ds(0, prompt_rows)], sems.at[0])
        two = pltpu.make_async_copy(kvc_hbm, kv.at[pl.ds(prompt_rows, cont_rows)], sems.at[1])
        one.start()
        two.start()
        one.wait()
        two.wait()

        def prepare(index, carry):
            row = pl.multiple_of(index * TQ, TQ)
            dkv[pl.ds(row, TQ), :] = jnp.zeros((TQ, D), F32)
            for pair in range(PAIRS):
                piece = kv[pl.ds(row, TQ), pair * 128 : (pair + 1) * 128]
                kt[pair * 128 : (pair + 1) * 128, pl.ds(row, TQ)] = jnp.transpose(
                    piece.astype(F32)
                ).astype(BF)
            return carry

        lax.fori_loop(0, keys_all // TQ, prepare, 0)

    base = pl.multiple_of(info[block, 0], TQ)
    tiles = info[block, 1]
    extra = info[block, 2]
    extra_row = pl.multiple_of(info[block, 3], TQ)
    diag = pl.multiple_of(info[block, 4], TQ)
    low, high = half_masks(TQ)
    zero = jnp.zeros((TQ, 128), BF)
    for pair in range(PAIRS):
        lanes = slice(pair * 128, (pair + 1) * 128)
        part = q_ref[:, lanes]
        qm[2 * pair] = jnp.where(low, part, zero)
        qm[2 * pair + 1] = jnp.where(high, part, zero)
        part = do_ref[:, lanes]
        dom[2 * pair] = jnp.where(low, part, zero)
        dom[2 * pair + 1] = jnp.where(high, part, zero)
        product = jnp.transpose(part.astype(F32) * o_ref[:, lanes].astype(F32))
        drow[2 * pair] = jnp.sum(product[:HEAD_DIM], axis=0)
        drow[2 * pair + 1] = jnp.sum(product[HEAD_DIM:], axis=0)

    def step(row, size, first):
        for pair in range(PAIRS):
            lanes = slice(pair * 128, (pair + 1) * 128)
            more = slice(HALF + pair * 128, HALF + (pair + 1) * 128)
            keys = kv[pl.ds(row, size), lanes]
            vals = kv[pl.ds(row, size), more]
            dk = None
            dv = None
            for side in (0, 1):
                head = 2 * pair + side
                raw = dot_nt(keys, qm[head])
                if first:
                    across = lax.broadcasted_iota(jnp.int32, (size, TQ), 1)
                    down = lax.broadcasted_iota(jnp.int32, (size, TQ), 0)
                    raw = jnp.where(down <= across, raw, MASKED)
                probs = jnp.exp2(raw - lse_ref[0, head : head + 1, :])
                grad = dot_nt(vals, dom[head])
                slope = (probs * (grad - drow[head : head + 1, :])).astype(BF)
                probs = probs.astype(BF)
                part_v = dot_nn(probs, dom[head])
                part_k = dot_nn(slope, qm[head])
                dv = part_v if dv is None else dv + part_v
                dk = part_k if dk is None else dk + part_k
                spot = slice(head * HEAD_DIM, (head + 1) * HEAD_DIM)
                new = dot_nn(kt[spot, pl.ds(row, size)], slope)
                if first:
                    dqt[spot, :] = new
                else:
                    dqt[spot, :] += new
            dkv[pl.ds(row, size), lanes] += dk
            dkv[pl.ds(row, size), more] += dv

    step(diag, TQ, True)

    def some(index, carry):
        step(pl.multiple_of(extra_row + index * TQ, TQ), TQ, False)
        return carry

    lax.fori_loop(0, extra, some, 0)

    def one(index, carry):
        step(pl.multiple_of(base + index * TK, TQ), TK, False)
        return carry

    lax.fori_loop(0, tiles, one, 0)
    for pair in range(PAIRS):
        lanes = slice(pair * 128, (pair + 1) * 128)
        dq_ref[:, lanes] = (jnp.transpose(dqt[lanes, :]) * HEAD_DIM ** (-0.5)).astype(BF)

    @pl.when(block == pl.num_programs(0) - 1)
    def _():
        def finish(index, carry):
            row = pl.multiple_of(index * TQ, TQ)
            kv[pl.ds(row, TQ), :HALF] = (dkv[pl.ds(row, TQ), :HALF] * (1.0 / LOG2E)).astype(BF)
            kv[pl.ds(row, TQ), HALF:] = dkv[pl.ds(row, TQ), HALF:].astype(BF)
            return carry

        lax.fori_loop(0, keys_all // TQ, finish, 0)
        one = pltpu.make_async_copy(kv.at[pl.ds(0, prompt_rows)], dkvp_hbm, sems.at[0])
        two = pltpu.make_async_copy(kv.at[pl.ds(prompt_rows, cont_rows)], dkvc_hbm, sems.at[1])
        one.start()
        two.start()
        one.wait()
        two.wait()


def attend_backward(info, q, do, o, lse, kvp, kvc, TQ):
    rows = q.shape[0]
    keys = kvp.shape[0] + kvc.shape[0]
    blocks = rows // TQ
    tile = pl.BlockSpec((TQ, HALF), lambda i, s: (i, 0))
    whole = pl.BlockSpec(memory_space=pl.ANY)
    return pl.pallas_call(
        attend_backward_kernel,
        grid_spec=pltpu.PrefetchScalarGridSpec(
            num_scalar_prefetch=1,
            grid=(blocks,),
            in_specs=[
                tile,
                tile,
                tile,
                pl.BlockSpec((1, 8, TQ), lambda i, s: (i, 0, 0)),
                whole,
                whole,
            ],
            out_specs=[tile, whole, whole],
            scratch_shapes=[
                pltpu.VMEM((keys, D), BF),
                pltpu.VMEM((HALF, keys), BF),
                pltpu.VMEM((keys, D), F32),
                pltpu.VMEM((NH, TQ, 128), BF),
                pltpu.VMEM((NH, TQ, 128), BF),
                pltpu.VMEM((HALF, TQ), F32),
                pltpu.VMEM((8, TQ), F32),
                pltpu.SemaphoreType.DMA((2,)),
            ],
        ),
        out_shape=(
            jax.ShapeDtypeStruct((rows, HALF), BF),
            jax.ShapeDtypeStruct(kvp.shape, BF),
            jax.ShapeDtypeStruct(kvc.shape, BF),
        ),
        compiler_params=pltpu.CompilerParams(
            dimension_semantics=("arbitrary",), vmem_limit_bytes=56 << 20
        ),
        cost_estimate=pl.CostEstimate(
            flops=int(10 * rows * PLEN * HALF * 4), bytes_accessed=30 << 20, transcendentals=0
        ),
        name="attend_backward",
    )(info, q, do, o, lse, kvp, kvc)


def normal_form(value):
    center = value - jnp.mean(value, axis=1, keepdims=True)
    return center * lax.rsqrt(jnp.mean(center * center, axis=1, keepdims=True) + EPSILON)


def flip(value):
    return jnp.transpose(value.astype(F32)).astype(BF)


def project_kernel(prompt_tiles, has, spot, xp_ref, xc_ref, w_ref, vec_ref, kvp_ref, kvc_ref, q_ref):
    step = pl.program_id(0)
    is_cont = step >= prompt_tiles
    x = jnp.where(is_cont, xc_ref[...].astype(F32), xp_ref[...].astype(F32))
    normed = (normal_form(x) * vec_ref[0:1, :] + vec_ref[1:2, :]).astype(BF)
    kv = (dot_nn(normed, w_ref[:, HALF : 3 * HALF]) + vec_ref[2:3, :]).astype(BF)

    @pl.when(jnp.logical_not(is_cont))
    def _():
        kvp_ref[...] = kv

    @pl.when(is_cont)
    def _():
        kvc_ref[...] = kv

    @pl.when(has[step] > 0)
    def _():
        query = dot_nn(normed, w_ref[:, :HALF]) + vec_ref[3:4, :HALF]
        q_ref[...] = (query * QSCALE).astype(BF)


def tile_specs(tile, prompt_tiles):
    prompts = pl.BlockSpec((tile, D), lambda i, h, s: (jnp.minimum(i, prompt_tiles - 1), 0))
    conts = pl.BlockSpec((tile, D), lambda i, h, s: (jnp.maximum(i - prompt_tiles, 0), 0))
    heads = pl.BlockSpec((tile, HALF), lambda i, h, s: (s[i], 0))
    return prompts, conts, heads


def project(has, spot, xp, xc, weight, vec, rows, tile):
    prompt_tiles = xp.shape[0] // tile
    steps = prompt_tiles + xc.shape[0] // tile
    prompts, conts, heads = tile_specs(tile, prompt_tiles)
    total = xp.shape[0] + xc.shape[0]
    return pl.pallas_call(
        functools.partial(project_kernel, prompt_tiles),
        grid_spec=pltpu.PrefetchScalarGridSpec(
            num_scalar_prefetch=2,
            grid=(steps,),
            in_specs=[
                prompts,
                conts,
                pl.BlockSpec(weight.shape, lambda i, h, s: (0, 0)),
                pl.BlockSpec(vec.shape, lambda i, h, s: (0, 0)),
            ],
            out_specs=[prompts, conts, heads],
        ),
        out_shape=(
            jax.ShapeDtypeStruct(xp.shape, BF),
            jax.ShapeDtypeStruct(xc.shape, BF),
            jax.ShapeDtypeStruct((rows, HALF), BF),
        ),
        compiler_params=pltpu.CompilerParams(
            dimension_semantics=("arbitrary",), vmem_limit_bytes=32 << 20
        ),
        cost_estimate=pl.CostEstimate(
            flops=2 * D * (total * D + rows * HALF), bytes_accessed=20 << 20, transcendentals=0
        ),
        name="project",
    )(has, spot, xp, xc, weight, vec)


def unproject_kernel(
    prompt_tiles,
    chained,
    has,
    spot,
    xp_ref,
    xc_ref,
    dkvp_ref,
    dkvc_ref,
    dq_ref,
    w_ref,
    vec_ref,
    *refs,
):
    if chained:
        old_w, old_vec, old_bias = refs[:3]
        refs = refs[3:]
    tp_ref, tc_ref, gw_ref, gvec_ref, gbias_ref = refs
    step = pl.program_id(0)
    is_cont = step >= prompt_tiles

    @pl.when(step == 0)
    def _():
        if chained:
            gw_ref[...] = old_w[...]
            gvec_ref[...] = old_vec[...]
            gbias_ref[...] = old_bias[...]
        else:
            gw_ref[...] = jnp.zeros_like(gw_ref)
            gvec_ref[...] = jnp.zeros_like(gvec_ref)
            gbias_ref[...] = jnp.zeros_like(gbias_ref)

    x = jnp.where(is_cont, xc_ref[...].astype(F32), xp_ref[...].astype(F32))
    hat = normal_form(x)
    normed_t = flip(hat * vec_ref[0:1, :] + vec_ref[1:2, :])
    dkv = jnp.where(is_cont, dkvc_ref[...].astype(F32), dkvp_ref[...].astype(F32)).astype(BF)
    gw_ref[:, HALF : 3 * HALF] += dot_nn(normed_t, dkv)
    gbias_ref[0:1, HALF : 3 * HALF] += jnp.sum(dkv.astype(F32), axis=0, keepdims=True)
    table = dot_nt(dkv, w_ref[:, HALF : 3 * HALF])

    def finish(value):
        gvec_ref[0:1, :] += jnp.sum(value * hat, axis=0, keepdims=True)
        gvec_ref[1:2, :] += jnp.sum(value, axis=0, keepdims=True)
        value = value.astype(BF)

        @pl.when(jnp.logical_not(is_cont))
        def _():
            tp_ref[...] = value

        @pl.when(is_cont)
        def _():
            tc_ref[...] = value

    @pl.when(has[step] == 0)
    def _():
        finish(table)

    @pl.when(has[step] > 0)
    def _():
        dq = dq_ref[...]
        gw_ref[:, :HALF] += dot_nn(normed_t, dq)
        gbias_ref[0:1, :HALF] += jnp.sum(dq.astype(F32), axis=0, keepdims=True)
        finish(table + dot_nt(dq, w_ref[:, :HALF]))


def unproject(has, spot, xp, xc, dkvp, dkvc, dq, weight, vec, totals, tile):
    prompt_tiles = xp.shape[0] // tile
    steps = prompt_tiles + xc.shape[0] // tile
    prompts, conts, heads = tile_specs(tile, prompt_tiles)
    total = xp.shape[0] + xc.shape[0]
    shapes = ((D, 3 * HALF), (8, D), (8, 3 * HALF))
    fixed = [pl.BlockSpec(shape, lambda i, h, s: (0, 0)) for shape in shapes]
    extra = () if totals is None else tuple(totals)
    return pl.pallas_call(
        functools.partial(unproject_kernel, prompt_tiles, totals is not None),
        grid_spec=pltpu.PrefetchScalarGridSpec(
            num_scalar_prefetch=2,
            grid=(steps,),
            in_specs=[
                prompts,
                conts,
                prompts,
                conts,
                heads,
                pl.BlockSpec(weight.shape, lambda i, h, s: (0, 0)),
                pl.BlockSpec(vec.shape, lambda i, h, s: (0, 0)),
            ]
            + (fixed if extra else []),
            out_specs=[prompts, conts] + fixed,
        ),
        out_shape=(
            jax.ShapeDtypeStruct(xp.shape, BF),
            jax.ShapeDtypeStruct(xc.shape, BF),
        )
        + tuple(jax.ShapeDtypeStruct(shape, F32) for shape in shapes),
        compiler_params=pltpu.CompilerParams(
            dimension_semantics=("arbitrary",), vmem_limit_bytes=40 << 20
        ),
        cost_estimate=pl.CostEstimate(
            flops=4 * D * (total * D + dq.shape[0] * HALF), bytes_accessed=30 << 20, transcendentals=0
        ),
        name="unproject",
    )(has, spot, xp, xc, dkvp, dkvc, dq, weight, vec, *extra)


def gelu_parts(value):
    rate = math.sqrt(2.0 / math.pi)
    square = value * value
    half = 0.5 + 0.5 * jnp.tanh(value * (rate + (rate * 0.044715) * square))
    slope = half + value * (half * (1.0 - half)) * (2.0 * rate + (6.0 * rate * 0.044715) * square)
    return value * half, slope


def feed_forward_kernel(
    prompt_parts,
    clen,
    count,
    groups,
    lens,
    places,
    xp_ref,
    xc_ref,
    gp_ref,
    gc_ref,
    mine_ref,
    mate_ref,
    vec_ref,
    bfc_ref,
    *refs,
):
    pieces = refs[:count]
    (
        fp_ref,
        fc_ref,
        hp_ref,
        hc_ref,
        dmine_ref,
        dmate_ref,
        gvec_ref,
        gbfc_ref,
        grads_hbm,
        wp,
        wfc,
        wout,
        ap,
        afc,
        aout,
        stage,
        sems,
    ) = refs[count:]
    core = places[0]
    batch = pl.program_id(0)
    part = pl.program_id(1)
    tile = mine_ref.shape[1]
    is_cont = part >= prompt_parts
    begin = (batch == 0) & (part == 0)

    @pl.when(begin)
    def _():
        loads = []
        for index, piece in enumerate(pieces):
            size = piece.shape[1]
            for inner in range(piece.shape[0]):
                row = pl.multiple_of(places[1 + index * piece.shape[0] + inner], 16)
                turned = pl.multiple_of(lax.rem(row + core * HALF, D), 16)
                source = piece.at[inner]
                moves = [
                    (source.at[:, pl.ds(0, D)], wp.at[pl.ds(turned, size), :]),
                    (source.at[:, pl.ds(D, FF)], wfc.at[pl.ds(row, size), :]),
                ]
                for block in range(FF // D):
                    moves.append(
                        (
                            source.at[:, pl.ds(D + FF + block * D, D)],
                            wout.at[pl.ds(block * D + row, size), :],
                        )
                    )
                for one, two in moves:
                    loads.append(pltpu.make_async_copy(one, two, sems.at[len(loads)]))
        for load in loads:
            load.start()
        ap[...] = jnp.zeros_like(ap)
        gvec_ref[...] = jnp.zeros_like(gvec_ref)
        gbfc_ref[...] = jnp.zeros_like(gbfc_ref)

        def clear(index, carry):
            row = pl.multiple_of(index * 64, 64)
            afc[pl.ds(row, 64), :] = jnp.zeros((64, FF), F32)
            aout[pl.ds(row, 64), :] = jnp.zeros((64, FF), F32)
            return carry

        lax.fori_loop(0, D // 64, clear, 0)
        for load in loads:
            load.wait()

    b_proj = vec_ref[0:1, :]
    gain = vec_ref[1:2, :]
    shift = vec_ref[2:3, :]
    b_out = vec_ref[3:4, :]
    x = jnp.where(is_cont, xc_ref[0].astype(F32), xp_ref[0].astype(F32))
    gy = jnp.where(is_cont, gc_ref[0].astype(F32), gp_ref[0].astype(F32))
    start = jnp.maximum(part - prompt_parts, 0) * tile
    length = lens[batch, start // clen]
    place = lax.broadcasted_iota(jnp.int32, (tile, 1), 0) + start % clen
    valid = jnp.where(jnp.logical_not(is_cont) | (place < length), 1.0, 0.0)

    mine = mine_ref[0]
    mate = mate_ref[0]
    h = x + valid * (dot_nn(mine, wp[:HALF, :]) + dot_nn(mate, wp[HALF:, :]) + b_proj)
    center = h - jnp.mean(h, axis=1, keepdims=True)
    rate = lax.rsqrt(jnp.mean(center * center, axis=1, keepdims=True) + EPSILON)
    hat = center * rate
    second = (hat * gain + shift).astype(BF)
    dz_full = valid * gy
    dz = dz_full.astype(BF)
    second_t = flip(second)
    dz_t = flip(dz)
    result = None
    back = None
    for index in range(FF // D):
        cols = slice(index * D, (index + 1) * D)
        inner = dot_nn(second, wfc[:, cols]) + bfc_ref[:, cols]
        act, slope = gelu_parts(inner)
        act = act.astype(BF)
        du_full = dot_nt(dz, wout[cols, :]) * slope
        du = du_full.astype(BF)
        gbfc_ref[0:1, cols] += jnp.sum(du_full, axis=0, keepdims=True)
        new = dot_nn(act, wout[cols, :])
        result = new if result is None else result + new
        new = dot_nt(du, wfc[:, cols])
        back = new if back is None else back + new
        aout[:, cols] += dot_nn(dz_t, act)
        afc[:, cols] += dot_nn(second_t, du)
    final = (h + valid * (result + b_out)).astype(BF)
    e2 = back * gain
    dh = gy + rate * (
        e2
        - jnp.mean(e2, axis=1, keepdims=True)
        - hat * jnp.mean(e2 * hat, axis=1, keepdims=True)
    )
    dy_full = valid * dh
    dy = dy_full.astype(BF)
    gvec_ref[0:1, :] += jnp.sum(dy_full, axis=0, keepdims=True)
    gvec_ref[1:2, :] += jnp.sum(back * hat, axis=0, keepdims=True)
    gvec_ref[2:3, :] += jnp.sum(back, axis=0, keepdims=True)
    gvec_ref[3:4, :] += jnp.sum(dz.astype(F32), axis=0, keepdims=True)
    ap[:HALF, :] += dot_nn(flip(mine), dy)
    ap[HALF:, :] += dot_nn(flip(mate), dy)
    dmine_ref[0] = dot_nt(dy, wp[:HALF, :]).astype(BF)
    dmate_ref[0] = dot_nt(dy, wp[HALF:, :]).astype(BF)
    dh = dh.astype(BF)

    @pl.when(jnp.logical_not(is_cont))
    def _():
        fp_ref[0] = final
        hp_ref[0] = dh

    @pl.when(is_cont)
    def _():
        fc_ref[0] = final
        hc_ref[0] = dh

    @pl.when((batch == pl.num_programs(0) - 1) & (part == pl.num_programs(1) - 1))
    def _():
        blocks, share = stage.shape[1], stage.shape[2]
        sends = []

        def send(column, fetch):
            slot = len(sends) % 2
            if len(sends) >= 2:
                sends[-2].wait()
            for block in range(blocks):
                stage[slot, block] = fetch(block).astype(BF)
            sends.append(
                pltpu.make_async_copy(
                    stage.at[slot], grads_hbm.at[:, :, pl.ds(column, D)], sems.at[slot]
                )
            )
            sends[-1].start()

        def first_row(block):
            return (block % groups * (blocks // groups) + block // groups) * share

        def proj_rows(block):
            row = lax.rem(first_row(block) + core * HALF, D)
            return ap[pl.ds(pl.multiple_of(row, math.gcd(share, HALF)), share), :]

        send(0, proj_rows)
        for part_of in range(FF // D):
            cols = slice(part_of * D, (part_of + 1) * D)
            send(D + part_of * D, lambda block: afc[first_row(block) : first_row(block) + share, cols])
        for part_of in range(FF // D):
            cols = slice(part_of * D, (part_of + 1) * D)
            ap[...] = jnp.transpose(aout[:, cols])
            send(
                D + FF + part_of * D,
                lambda block: ap[first_row(block) : first_row(block) + share, :],
            )
        for copy in sends[-2:]:
            copy.wait()


def feed_forward(lens, places, prompt_in, cont_in, prompt_cot, cont_cot, mine, mate, vec, bfc, pieces, groups, share):
    prow = prompt_in.shape[1]
    crow = cont_in.shape[1]
    clen = crow // lens.shape[1]
    tile = min(256, prow, clen)
    prompt_parts = prow // tile
    parts = prompt_parts + crow // tile
    prompts = pl.BlockSpec((1, tile, D), lambda m, i, s, t: (m, jnp.minimum(i, prompt_parts - 1), 0))
    conts = pl.BlockSpec((1, tile, D), lambda m, i, s, t: (m, jnp.maximum(i - prompt_parts, 0), 0))
    heads = pl.BlockSpec((1, tile, HALF), lambda m, i, s, t: (m, i, 0))
    whole = pl.BlockSpec(memory_space=pl.ANY)
    fixed = pl.BlockSpec((8, D), lambda m, i, s, t: (0, 0))
    long = pl.BlockSpec((8, FF), lambda m, i, s, t: (0, 0))
    shape = jax.ShapeDtypeStruct
    rows = MB * (prow + crow)
    return pl.pallas_call(
        functools.partial(feed_forward_kernel, prompt_parts, clen, len(pieces), groups),
        grid_spec=pltpu.PrefetchScalarGridSpec(
            num_scalar_prefetch=2,
            grid=(MB, parts),
            in_specs=[
                prompts,
                conts,
                prompts,
                conts,
                heads,
                heads,
                fixed,
                pl.BlockSpec((1, FF), lambda m, i, s, t: (0, 0)),
            ]
            + [whole] * len(pieces),
            out_specs=[prompts, conts, prompts, conts, heads, heads, fixed, long, whole],
            scratch_shapes=[
                pltpu.VMEM((D, D), BF),
                pltpu.VMEM((D, FF), BF),
                pltpu.VMEM((FF, D), BF),
                pltpu.VMEM((D, D), F32),
                pltpu.VMEM((D, FF), F32),
                pltpu.VMEM((D, FF), F32),
                pltpu.VMEM((2, D // share, share, D), BF),
                pltpu.SemaphoreType.DMA(
                    (max(16, (2 + FF // D) * sum(piece.shape[0] for piece in pieces)),)
                ),
            ],
        ),
        out_shape=(
            shape(prompt_in.shape, BF),
            shape(cont_in.shape, BF),
            shape(prompt_in.shape, BF),
            shape(cont_in.shape, BF),
            shape(mine.shape, BF),
            shape(mate.shape, BF),
            shape((8, D), F32),
            shape((8, FF), F32),
            shape((D // share, share, D + 2 * FF), BF),
        ),
        compiler_params=pltpu.CompilerParams(
            dimension_semantics=("arbitrary", "arbitrary"), vmem_limit_bytes=63 << 20
        ),
        cost_estimate=pl.CostEstimate(
            flops=6 * rows * (D * D + 2 * D * FF), bytes_accessed=50 << 20, transcendentals=0
        ),
        name="feed_forward",
    )(lens, places, prompt_in, cont_in, prompt_cot, cont_cot, mine, mate, vec, bfc, *pieces)


HEAD_COLS = 3 * HALF
SMALL_COLS = 128


def neighbour(value, axis, distance):
    pairs = [(i, i ^ distance) for i in range(lax.axis_size(axis))]
    return lax.ppermute(value, axis, pairs)


def swap(value):
    return neighbour(value, "fsdp", 1)


def is_square():
    return lax.axis_size("grp") == 4 and lax.axis_size("fsdp") == 8


def square_halves(block):
    half = block.shape[0] // 2
    pieces = []
    for index, (one, two) in enumerate(((1, 2), (2, 1))):
        piece = block[index * half : (index + 1) * half]
        both = jnp.stack([piece, neighbour(piece, "grp", one)])
        far = neighbour(both, "grp", two)
        pieces.append((both, (0, one), index))
        pieces.append((far, (two, 3), index))
    return pieces


def gather_parameters(packed, core):
    own = lax.axis_index("grp")
    cut = 3 * D + SMALL_COLS
    if not is_square():
        whole = lax.all_gather(packed, ALL, axis=0, tiled=True)
        heads = lax.dynamic_slice_in_dim(whole[:, : 3 * D], core * HEAD_COLS, HEAD_COLS, 1)
        front = jnp.concatenate([heads, whole[:, 3 * D : cut]], axis=1)
        return front, [whole[:, cut:].reshape(2, HALF, -1)], [0, HALF], whole
    zone = lax.all_gather(packed, "fsdp", axis=0, tiled=True)
    group_rows = zone.shape[0]
    heads = lax.dynamic_slice_in_dim(zone[:, : 3 * D], core * HEAD_COLS, HEAD_COLS, 1)
    parts = {}
    for both, offsets, index in square_halves(
        jnp.concatenate([heads, zone[:, 3 * D : cut]], axis=1)
    ):
        for which, offset in enumerate(offsets):
            parts[offset, index] = both[which]
    table = jnp.stack([jnp.concatenate([parts[k, 0], parts[k, 1]], axis=0) for k in range(4)])
    front = jnp.concatenate(
        [lax.dynamic_index_in_dim(table, own ^ k, 0, keepdims=False) for k in range(4)], axis=0
    )
    half = group_rows // 2
    rest = lax.dynamic_slice(zone, (core * half, cut), (half, zone.shape[1] - cut))
    pieces, rows = [], []
    for both, offsets, index in square_halves(rest):
        for source, side in ((both, core), (swap(both), 1 - core)):
            pieces.append(source)
            for offset in offsets:
                rows.append((own ^ offset) * group_rows + side * half + index * (half // 2))
    return front, pieces, rows, zone


def pick(array, index, axis):
    return lax.dynamic_index_in_dim(array, index, axis, keepdims=False)


def meet(array, index, axis, name, distance):
    other = neighbour(pick(array, 1 - index, axis), name, distance)
    return (pick(array, index, axis).astype(F32) + other.astype(F32)).astype(BF)


def reduce_steps():
    if not is_square():
        groups = [list(range(c, lax.axis_size("fsdp"), 2)) for c in (0, 1)]

        def along_grp(value):
            return lax.psum_scatter(value, "grp", scatter_dimension=0, tiled=True)

        def along_chips(value):
            return lax.psum_scatter(
                value, "fsdp", scatter_dimension=0, tiled=True, axis_index_groups=groups
            )

        return [along_grp, along_chips]

    own = lax.axis_index("grp")
    x, y = own % 2, own // 2
    z = lax.axis_index("fsdp") // 2

    def one(value):
        value = value.reshape(2, 2, 2, value.shape[0] // 8, value.shape[1])
        return meet(value[:, :, 0], x, 1, "grp", 1), meet(value[:, :, 1], y, 0, "grp", 2)

    def two(pair):
        value = jnp.concatenate(
            [meet(pair[0], y, 0, "grp", 2), meet(pair[1], x, 0, "grp", 1)], axis=0
        )
        return value.reshape(2, 2, value.shape[0] // 4, value.shape[1])

    def three(value):
        return meet(value, z % 2, 1, "fsdp", 2)

    def four(value):
        return meet(value, z // 2, 0, "fsdp", 4)

    return [one, two, three, four]


def reduce_parameters(value):
    for step in reduce_steps():
        value = step(value)
    return value


def own_rows(value, core):
    share = value.shape[0] // 2
    keep = lax.dynamic_slice_in_dim(value, core * share, share, 0)
    other = swap(lax.dynamic_slice_in_dim(value, (1 - core) * share, share, 0))
    return keep, other


def pin(first, second):
    return lax.optimization_barrier((first, second))


def square_steps(core):
    own = lax.axis_index("grp")
    x, y = own % 2, own // 2

    def one(value):
        cols = value.shape[-1] // 2
        value = value.reshape((2, 2) + value.shape[1:])
        return (
            meet(value[..., :cols], x, 1, "grp", 1),
            meet(value[..., cols:], y, 0, "grp", 2),
        )

    def two(pair):
        return jnp.concatenate(
            [meet(pair[0], y, 0, "grp", 2), meet(pair[1], x, 0, "grp", 1)], axis=1
        )

    return [one, two]


def body(
    prompt_in,
    cont_in,
    prompt_cot,
    cont_cot,
    cont_prompt,
    cont_len,
    ln1_gain,
    ln1_bias,
    attn_weight,
    attn_bias,
    proj_weight,
    proj_bias,
    ln2_gain,
    ln2_bias,
    fc_weight,
    fc_bias,
    out_weight,
    out_bias,
):
    fsdp = lax.axis_size("fsdp")
    devices = fsdp * lax.axis_size("grp")
    prow = prompt_in.shape[1]
    crow = cont_in.shape[1]
    conts = cont_prompt.shape[2]
    clen = crow // conts
    mine = prow + crow
    TQ = min(256, prow, clen)
    prompt_rows = NPR * PLEN
    place = lax.axis_index("fsdp")
    core = place % 2
    share = D // devices
    wide = FF // D

    vectors = (ln1_gain, ln1_bias, attn_bias[0], attn_bias[1], proj_bias, ln2_gain, ln2_bias, out_bias)
    columns = jnp.concatenate(
        [v[:, None] for v in vectors] + [fc_bias.reshape(wide, share).T], axis=1
    )
    columns = jnp.pad(columns, ((0, 0), (0, SMALL_COLS - columns.shape[1])))
    packed = jnp.concatenate(
        [
            attn_weight.reshape(share, 3, 2, HALF).transpose(0, 2, 1, 3).reshape(share, 3 * D),
            columns,
            proj_weight,
            fc_weight.reshape(share, devices, wide, share).transpose(0, 2, 1, 3).reshape(share, FF),
            out_weight.reshape(wide, share, D).transpose(1, 0, 2).reshape(share, FF),
        ],
        axis=1,
    ).astype(BF)
    front, pieces, piece_rows, zone = gather_parameters(packed, core)
    w_heads = front[:, :HEAD_COLS]
    small = front[:, HEAD_COLS:].astype(F32)
    gain_a, shift_a, bias_q, bias_v, b_proj, gain_b, shift_b, b_out = (small[:, i] for i in range(8))
    b_fc = small[:, 8 : 8 + wide].T.reshape(1, FF)
    bias_q = lax.dynamic_slice_in_dim(bias_q, core * HALF, HALF)
    bias_v = lax.dynamic_slice_in_dim(bias_v, core * HALF, HALF)
    none = jnp.zeros((HALF,), F32)
    vec_a = jnp.stack(
        [gain_a, shift_a, jnp.concatenate([none, bias_v]), jnp.concatenate([bias_q, none])]
        + [jnp.zeros((D,), F32)] * 4
    )
    vec_b = jnp.pad(jnp.stack([b_proj, gain_b, shift_b, b_out]), ((0, 4), (0, 0)))

    prompt_all = [lax.all_gather(prompt_in[m], "fsdp", axis=0, tiled=True) for m in range(MB)]
    cont_mate = swap(cont_in)
    plan_mate = swap(cont_prompt[:, 0, :].astype(F32)).astype(jnp.int32)

    own_row = place * prow
    mate_row = (place + 1 - 2 * core) * prow

    def prompt_plan(row):
        row = row + TQ * jnp.arange(prow // TQ)
        spot = row % PLEN
        return jnp.stack(
            [
                row - spot,
                spot // TK,
                spot % TK // TQ,
                row - spot + spot // TK * TK,
                row,
            ],
            axis=1,
        )

    def cont_plan(follows, first):
        blocks = clen // TQ
        follows = jnp.repeat(follows, blocks)
        index = jnp.arange(conts * blocks)
        begin = prompt_rows + first + index // blocks * clen
        return jnp.stack(
            [
                follows * PLEN,
                jnp.full(index.shape, PLEN // TK),
                index % blocks,
                begin,
                begin + index % blocks * TQ,
            ],
            axis=1,
        )

    def plan_of(m):
        return jnp.concatenate(
            [
                prompt_plan(own_row),
                cont_plan(cont_prompt[m, 0], 0),
                prompt_plan(mate_row),
                cont_plan(plan_mate[m], crow),
            ],
            axis=0,
        ).astype(jnp.int32)

    tiles = (prompt_rows + 2 * crow) // TQ
    index = jnp.arange(tiles)
    part, cpart = prow // TQ, crow // TQ
    own_tile, mate_tile, cont_tile = own_row // TQ, mate_row // TQ, prompt_rows // TQ
    is_own = (index >= own_tile) & (index < own_tile + part)
    is_mate = (index >= mate_tile) & (index < mate_tile + part)
    is_cont = index >= cont_tile
    has = (is_own | is_mate | is_cont).astype(jnp.int32)
    order_own = index - own_tile
    order_mate = index - mate_tile + part + cpart
    order_cont = index - cont_tile
    order_cont = jnp.where(order_cont < cpart, part + order_cont, 2 * part + order_cont)
    exact = jnp.where(is_cont, order_cont, jnp.where(is_own, order_own, order_mate))
    first_tile = jnp.minimum(own_tile, mate_tile)
    clipped = jnp.clip(index, first_tile, first_tile + 2 * part - 1)
    early_spot = jnp.where(
        (clipped >= own_tile) & (clipped < own_tile + part),
        clipped - own_tile,
        clipped - mate_tile + part + cpart,
    )
    spot = jnp.where(is_cont, exact, early_spot).astype(jnp.int32)

    saved = []
    outs_mine = []
    outs_mate = []
    for m in range(MB):
        x_prompt = prompt_all[m]
        if m > 0:
            x_prompt, saved[-1][-1] = pin(x_prompt, saved[-1][-1])
        x_cont = jnp.concatenate([cont_in[m], cont_mate[m]], axis=0)
        kvp, kvc, query = project(has, spot, x_prompt, x_cont, w_heads, vec_a, 2 * mine, TQ)
        plan = plan_of(m)
        o, lse = attend_forward(plan, query, kvp, kvc, TQ)
        outs_mine.append(o[:mine])
        outs_mate.append(swap(o[mine:]))
        saved.append([x_prompt, x_cont, kvp, kvc, query, plan, o, lse])

    groups, block_share = (4, share) if is_square() else (1, 8)
    places = jnp.stack([core] + [jnp.asarray(row, jnp.int32) for row in piece_rows]).astype(jnp.int32)
    (
        prompt_out,
        cont_out,
        prompt_dh,
        cont_dh,
        d_mine,
        d_mate,
        g_vec,
        g_fc_bias,
        g_rest,
    ) = feed_forward(
        cont_len[:, 0, :],
        places,
        prompt_in,
        cont_in,
        prompt_cot,
        cont_cot,
        jnp.stack(outs_mine),
        jnp.stack(outs_mate),
        vec_b,
        b_fc,
        pieces,
        groups,
        block_share,
    )
    d_back = swap(d_mate)
    moves = []
    if is_square():
        g_rest = lax.psum_scatter(g_rest, "fsdp", scatter_dimension=0, tiled=True)
        moves = square_steps(core)
    else:
        g_rest = lax.psum_scatter(g_rest.reshape(D, D + 2 * FF), ALL, scatter_dimension=0, tiled=True)
    early = [g_rest]

    def advance(held):
        if moves:
            early[0] = moves.pop(0)(early[0])
            held, early[0] = pin(held, early[0])
        return held

    totals = None
    tables = []
    conts_back = []
    for m in range(MB):
        x_prompt, x_cont, kvp, kvc, query, plan, o, lse = saved[m]
        do = jnp.concatenate([d_mine[m], d_back[m]], axis=0)
        if m > 0:
            do, tables[-1] = pin(do, tables[-1])
            tables[-1] = lax.psum_scatter(tables[-1], "fsdp", scatter_dimension=0, tiled=True)
        if m > 1:
            do, tables[m - 2] = pin(do, tables[m - 2])
        dq, dkvp, dkvc = attend_backward(plan, query, do, o, lse, kvp, kvc, TQ)
        if m > 0:
            dkvp = advance(dkvp)
        table, table_cont, *totals = unproject(
            has, spot, x_prompt, x_cont, dkvp, dkvc, dq, w_heads, vec_a, totals, TQ
        )
        tables.append(table)
        conts_back.append(
            table_cont[:crow].astype(F32) + swap(table_cont[crow:]).astype(F32)
        )
    if MB > 1:
        tables[-1], tables[-2] = pin(tables[-1], tables[-2])
    tables[-1] = lax.psum_scatter(tables[-1], "fsdp", scatter_dimension=0, tiled=True)
    while moves:
        early[0] = moves.pop(0)(early[0])
    g_heads, g_first, g_bias = totals

    def spread(value):
        return jnp.where((jnp.arange(2) == core)[:, None], value[None, :], 0.0).reshape(D)

    sums = jnp.stack(
        [
            g_first[0],
            g_first[1],
            spread(g_bias[0, :HALF]),
            spread(g_bias[0, 2 * HALF :]),
            g_vec[0],
            g_vec[1],
            g_vec[2],
            g_vec[3],
        ]
        + [g_fc_bias[0, i * D : (i + 1) * D] for i in range(wide)],
        axis=0,
    )
    sums_high = sums.astype(BF)
    sums_low = (sums - sums_high.astype(F32)).astype(BF)
    count = sums.shape[0]
    sums = jnp.concatenate(
        [sums_high, sums_low, jnp.zeros((SMALL_COLS - 2 * count, D), BF)], axis=0
    ).T
    late = reduce_parameters(jnp.concatenate([g_heads.astype(BF), sums], axis=1))
    late_own, late_other = own_rows(late, core)
    sums = late_own[:, HEAD_COLS:].astype(F32) + late_other[:, HEAD_COLS:].astype(F32)
    sums = (sums[:, :count] + sums[:, count : 2 * count]).T

    def by_core(own, other):
        return jnp.where(core == 0, own, other), jnp.where(core == 0, other, own)

    late = jnp.stack(by_core(late_own[:, :HEAD_COLS], late_other[:, :HEAD_COLS]), axis=1)
    late = late.reshape(share, 2, 3, HALF).transpose(0, 2, 1, 3).reshape(share, 3 * D)
    early = early[0].astype(F32)
    g_fc = early[:, D : D + FF].reshape(share, wide, devices, share)
    g_fc = g_fc.transpose(0, 2, 1, 3).reshape(share, FF)
    g_out = early[:, D + FF :].reshape(share, wide, D).transpose(1, 0, 2).reshape(share * wide, D)

    def input_grad(source, slope, change):
        source = source.astype(F32)
        center = source - jnp.mean(source, axis=-1, keepdims=True)
        rate = lax.rsqrt(jnp.mean(center * center, axis=-1, keepdims=True) + EPSILON)
        hat = center * rate
        e1 = change * gain_a
        change = e1 - jnp.mean(e1, axis=-1, keepdims=True)
        change = change - hat * jnp.mean(e1 * hat, axis=-1, keepdims=True)
        return (slope.astype(F32) + rate * change).astype(BF)

    prompt_grad = jnp.stack(
        [input_grad(prompt_in[m], prompt_dh[m], tables[m].astype(F32)) for m in range(MB)]
    )
    cont_grad = jnp.stack([input_grad(cont_in[m], cont_dh[m], conts_back[m]) for m in range(MB)])
    return (
        prompt_out,
        cont_out,
        prompt_grad,
        cont_grad,
        sums[0],
        sums[1],
        late.astype(F32),
        sums[2:4],
        early[:, :D],
        sums[4],
        sums[5],
        sums[6],
        g_fc,
        sums[8:].reshape(share * wide),
        g_out,
        sums[7],
    )


def solution(mesh):
    rows = P(None, ALL, None)
    conts = P(None, "grp", "fsdp")
    vector = P(ALL)
    matrix = P(ALL, None)
    pair = P(None, ALL)
    params = (
        vector,
        vector,
        matrix,
        pair,
        matrix,
        vector,
        vector,
        vector,
        matrix,
        vector,
        matrix,
        vector,
    )
    return jax.shard_map(
        body,
        mesh=mesh,
        in_specs=(rows, rows, rows, rows, conts, conts) + params,
        out_specs=(rows, rows, rows, rows) + params,
        check_vma=False,
    )
```

time: 1350 us -> 903 us (0.67)
  waiting for transfers between devices: 494 us -> 166 us
  matrix products: 253 us -> 0 us
  Pallas kernels: 241 us -> 487 us
  other arithmetic: 154 us -> 50.2 us
  starting transfers between devices: 3.11 us -> 70.5 us
  blocking collectives: 39.6 us -> 0 us
  local copies, waits for them, and re-layouts: 137 us -> 100 us
    reduce_scatter x5 -> x4, waiting for transfers between devices: 305 us -> 21.8 us  [the longest x3 21.8 us: body(): lax.psum_scatter(tables[-1], 'fsdp', scatter_dimension=0, tiled=True)]
    dot_general x36 -> x0, matrix products: 253 us -> none  [the longest x1 38 us: body(): d_active = jnp.einsum('rd,fd->rf', dz, w_out, preferred_element_type=F32)]
    pallas_call x0 -> x7, Pallas kernels: none -> 246 us  [the longest x1 108 us: feed_forward(): pl.pallas_call(functools.partial(feed_forward_kernel, prompt_parts, clen,...]
    all_gather x3, waiting for transfers between devices: 152 us -> 51.5 us  [body(): lax.all_gather(prompt_in[m], 'fsdp', axis=0, tiled=True)]
    ppermute x11 -> x32, starting transfers between devices: 2.71 us -> 70.2 us  [neighbour(): return lax.ppermute(value, axis, pairs)]
    ppermute x11 -> x32, waiting for transfers between devices: 0.82 us -> 60.3 us  [neighbour(): return lax.ppermute(value, axis, pairs)]
    reduce_sum x32 -> x7, other arithmetic: 69.1 us -> 9.93 us  [the longest x1 3.27 us: input_grad(): change = change - hat * jnp.mean(e1 * hat, axis=-1, keepdims=True)]
    psum x1 -> x0, blocking collectives: 39.6 us -> none  [body(): sums = lax.psum(sums, ALL)]
  transfers between devices with their start and end apart: 21 -> 40, of which waited for: 10 -> 17; matrix products, arithmetic and copies ran while one was open for 25% -> 9% of each run, Pallas kernels for 14% -> 42%
where the time goes in v2:
time: 903 us; the launch traced here: 894 us
  Pallas kernels  487 us (54%)
  waiting for transfers between devices  166 us (18%)
  local copies, waits for them, and re-layouts  100 us (11%)
  starting transfers between devices  70.5 us (8%)
  other arithmetic  50.2 us (6%)
  between operations  20 us (2%)
    pallas_call x3, Pallas kernels, attend_backward(): pl.pallas_call(attend_backward_kernel, grid_spec=pltpu.PrefetchScalarGrid...  155 us
    pallas_call x1, Pallas kernels, feed_forward(): pl.pallas_call(functools.partial(feed_forward_kernel, prompt_parts, clen,...  108 us
    pallas_call x3, Pallas kernels, unproject(): pl.pallas_call(functools.partial(unproject_kernel, prompt_tiles, totals i...  89.9 us
    pallas_call x3, Pallas kernels, attend_forward(): pl.pallas_call(attend_forward_kernel, grid_spec=pltpu.PrefetchScalarGridS...  86.5 us
    ppermute x32, starting transfers between devices, neighbour(): return lax.ppermute(value, axis, pairs)  70.2 us
    ppermute x32, waiting for transfers between devices, neighbour(): return lax.ppermute(value, axis, pairs)  60.3 us
    all_gather x3, waiting for transfers between devices, body(): lax.all_gather(prompt_in[m], 'fsdp', axis=0, tiled=True)  51.5 us
    unnamed x240, local copies, waits for them, and re-layouts  48.3 us
  transfers between devices with their start and end apart: 40, of which 17 were waited for; matrix products, arithmetic and copies ran while one was open for 9% of the time, Pallas kernels for 42%

profile of v2, /device:TPU:0, one launch (start us, length us, event | category | flops | bytes accessed | tf_op | source)
XLA Modules:
  0.0 894.2 jit_solution(18148849126900822719)
XLA Ops:
  35.1 31.5 %all-gather.8.cloned.1.call-done = bf16[192,9344]{1,0:T(8,128)(2,1)} async-done(((bf16[24,9344]{1,0:T(8,128)(2,1)}), bf16[192,9344]{1,0:T(8,128)(2,1)}) %all-gather.8.cloned.1.call-update) | async-done | bytes 3588112 | tf_op jit(solution)/shard_map/all_gather | solution.py:841
  74.4 3.2 collective-permute-done.3
  80.8 12.5 %collective-permute-done.9 = bf16[48,6912]{1,0:T(8,128)(2,1)S(1)} collective-permute-done((bf16[48,6912]{1,0:T(8,128)(2,1)S(1)}, bf16[48,6912]{1,0:T(8,128)(2,1)S(1)}, u32[]{:S(2)}, u32[]{:S(2)}) %collective-permute-start.9) | collective-permute-done | bytes 663584 | tf_op jit(solution)/shard_map/ppermute | solution.py:810
  97.7 6.1 collective-permute-done.4
  106.7 25.8 %all-gather.10.cloned.1.call-done = bf16[1,4096,768]{2,1,0:T(8,128)(2,1)} async-done(((bf16[1,512,768]{2,1,0:T(8,128)(2,1)}), bf16[1,4096,768]{2,1,0:T(8,128)(2,1)}) %all-gather.10.cloned.1.call-update) | async-done | bytes 6291472 | tf_op jit(solution)/shard_map/all_gather | solution.py:1011
  132.5 2.8 copy-done.34
  135.3 16.1 %project.3 = (bf16[4096,768]{1,0:T(8,128)(2,1)S(1)}, bf16[512,768]{1,0:T(8,128)(2,1)S(1)}, bf16[1536,384]{1,0:T(8,128)(2,1)S(1)}) custom-call(s32[18]{0:T(128)S(1)} %or_convert_fusion.has, s32[18]{0:T(128)S(1)} %select_select_fusion.spot, bf16[4096,768]{1,0:T(8,128)(2,1)S(1)} %bitcast.353, bf16[512,768]{1,0:T(8,128)(2,1)S(1)} %pad_maximum_fusion.13.xc_ref, ...), custom_call_target="tpu_custom_call" | custom-call | flops 6341787648 | bytes 20971520 | tf_op jit(solution)/shard_map/project/pallas_call | solution.py:408
  151.5 2.6 copy-done.37
  154.1 28.9 %attend_forward.3 = (bf16[1536,384]{1,0:T(8,128)(2,1)S(1)}, f32[6,8,256]{2,1,0:T(8,128)S(1)}) custom-call(s32[6,5]{1,0:T(8,128)S(1)} %get-tuple-element.320.info, bf16[1536,384]{1,0:T(8,128)(2,1)S(1)} %get-tuple-element.81.q_ref, bf16[4096,768]{1,0:T(8,128)(2,1)} %copy-done.37, bf16[512,768]{1,0:T(8,128)(2,1)S(1)} %get-tuple-element.83.kvc_hbm), custom_call_target="tpu_custom_call" | custom-call | flops 19327352832 | bytes 20971520 | tf_op jit(solution)/shard_map/attend_forward/pallas_call | solution.py:151
  185.9 12.3 %all-gather.12.cloned.1.call-done = bf16[1,4096,768]{2,1,0:T(8,128)(2,1)} async-done(((bf16[1,512,768]{2,1,0:T(8,128)(2,1)}), bf16[1,4096,768]{2,1,0:T(8,128)(2,1)}) %all-gather.12.cloned.1.call-update) | async-done | bytes 6291472 | tf_op jit(solution)/shard_map/all_gather | solution.py:1011
  198.2 2.8 copy-done.33
  201.0 15.9 %project.4 = (bf16[4096,768]{1,0:T(8,128)(2,1)S(1)}, bf16[512,768]{1,0:T(8,128)(2,1)S(1)}, bf16[1536,384]{1,0:T(8,128)(2,1)S(1)}) custom-call(s32[18]{0:T(128)S(1)} %or_convert_fusion.has, s32[18]{0:T(128)S(1)} %select_select_fusion.spot, bf16[4096,768]{1,0:T(8,128)(2,1)S(1)} %bitcast.351, bf16[512,768]{1,0:T(8,128)(2,1)S(1)} %get-tuple-element.340.xc_ref, ...), custom_call_target="tpu_custom_call" | custom-call | flops 6341787648 | bytes 20971520 | tf_op jit(solution)/shard_map/project/pallas_call | solution.py:408
  216.9 2.5 copy-done.36
  219.5 28.8 %attend_forward.4 = (bf16[1536,384]{1,0:T(8,128)(2,1)S(1)}, f32[6,8,256]{2,1,0:T(8,128)S(1)}) custom-call(s32[6,5]{1,0:T(8,128)S(1)} %get-tuple-element.321.info, bf16[1536,384]{1,0:T(8,128)(2,1)S(1)} %get-tuple-element.87.q_ref, bf16[4096,768]{1,0:T(8,128)(2,1)} %copy-done.36, bf16[512,768]{1,0:T(8,128)(2,1)S(1)} %get-tuple-element.89.kvc_hbm), custom_call_target="tpu_custom_call" | custom-call | flops 19327352832 | bytes 20971520 | tf_op jit(solution)/shard_map/attend_forward/pallas_call | solution.py:151
  250.3 13.4 %all-gather.14.cloned.1.call-done = bf16[1,4096,768]{2,1,0:T(8,128)(2,1)} async-done(((bf16[1,512,768]{2,1,0:T(8,128)(2,1)}), bf16[1,4096,768]{2,1,0:T(8,128)(2,1)}) %all-gather.14.cloned.1.call-update) | async-done | bytes 6291472 | tf_op jit(solution)/shard_map/all_gather | solution.py:1011
  264.8 2.8 copy-done.32
  267.6 16.0 %project.5 = (bf16[4096,768]{1,0:T(8,128)(2,1)S(1)}, bf16[512,768]{1,0:T(8,128)(2,1)S(1)}, bf16[1536,384]{1,0:T(8,128)(2,1)S(1)}) custom-call(s32[18]{0:T(128)S(1)} %or_convert_fusion.has, s32[18]{0:T(128)S(1)} %select_select_fusion.spot, bf16[4096,768]{1,0:T(8,128)(2,1)S(1)} %bitcast.349, bf16[512,768]{1,0:T(8,128)(2,1)S(1)} %copy-done.17, ...), custom_call_target="tpu_custom_call" | custom-call | flops 6341787648 | bytes 20971520 | tf_op jit(solution)/shard_map/project/pallas_call | solution.py:408
  283.7 2.6 copy-done.35
  286.3 28.8 %attend_forward.5 = (bf16[1536,384]{1,0:T(8,128)(2,1)S(1)}, f32[6,8,256]{2,1,0:T(8,128)S(1)}) custom-call(s32[6,5]{1,0:T(8,128)S(1)} %fusion.91.info, bf16[1536,384]{1,0:T(8,128)(2,1)S(1)} %get-tuple-element.93.q_ref, bf16[4096,768]{1,0:T(8,128)(2,1)} %copy-done.35, bf16[512,768]{1,0:T(8,128)(2,1)S(1)} %get-tuple-element.95.kvc_hbm), custom_call_target="tpu_custom_call" | custom-call | flops 19327352832 | bytes 20971520 | tf_op jit(solution)/shard_map/attend_forward/pallas_call | solution.py:151
  323.2 3.8 collective-permute-done.6
  326.9 2.5 pad_maximum_fusion.5.mate_ref
  329.5 108.0 %feed_forward.1 = (bf16[3,512,768]{2,1,0:T(8,128)(2,1)}, bf16[3,256,768]{2,1,0:T(8,128)(2,1)}, bf16[3,512,768]{2,1,0:T(8,128)(2,1)}, bf16[3,256,768]{2,1,0:T(8,1...) custom-call(s32[3,1]{1,0:T(4,128)} %copy.203.lens, ...), custom_call_target="tpu_custom_call" | custom-call | flops 73383542784 | bytes 52428800 | tf_op jit(solution)/shard_map/feed_forward/pallas_call | solution.py:753
  444.8 51.5 %attend_backward.3 = (bf16[1536,384]{1,0:T(8,128)(2,1)}, bf16[4096,768]{1,0:T(8,128)(2,1)}, bf16[512,768]{1,0:T(8,128)(2,1)}) custom-call(s32[6,5]{1,0:T(8,128)} %copy-done.24, bf16[1536,384]{1,0:T(8,128)(2,1)} %copy-done.40, bf16[1536,384]{1,0:T(8,128)(2,1)} %pad_maximum_fusion.10.do_ref, bf16[1536,384]{1,0:T(8,128)(2,1)} %copy-done.13, ...), custom_call_target="tpu_custom_call" | custom-call | flops 48318382080 | bytes 31457280 | tf_op jit(solution)/shard_map/attend_backward/pallas_call | solution.py:326
  498.8 29.6 %unproject.3 = (bf16[4096,768]{1,0:T(8,128)(2,1)}, bf16[512,768]{1,0:T(8,128)(2,1)S(1)}, f32[768,1152]{1,0:T(8,128)S(1)}, f32[8,768]{1,0:T(8,128)S(1)}, f32[8,1152]{1,0:T(8,128)S(1)}) custom-call(s32[18]{0:T(128)S(1)} %or_convert_fusion.has, s32[18]{0:T(128)S(1)} %select_select_fusion.spot, bf16[4096,768]{1,0:T(8,128)(2,1)} %bitcast.352, ...), custom_call_target="tpu_custom_call" | custom-call | flops 12683575296 | bytes 31457280 | tf_op jit(solution)/shard_map/unproject/pallas_call | solution.py:509
  529.4 1.7 copy-done.43
  533.5 51.7 %attend_backward.4 = (bf16[1536,384]{1,0:T(8,128)(2,1)}, bf16[4096,768]{1,0:T(8,128)(2,1)}, bf16[512,768]{1,0:T(8,128)(2,1)}) custom-call(s32[6,5]{1,0:T(8,128)} %copy-done.23, bf16[1536,384]{1,0:T(8,128)(2,1)} %copy-done.39, bf16[1536,384]{1,0:T(8,128)(2,1)} %pad_maximum_fusion.9.do_ref, bf16[1536,384]{1,0:T(8,128)(2,1)} %copy-done.12, ...), custom_call_target="tpu_custom_call" | custom-call | flops 48318382080 | bytes 31457280 | tf_op jit(solution)/shard_map/attend_backward/pallas_call | solution.py:326
  589.9 6.9 collective-permute-done.19
  600.1 30.3 %unproject.4 = (bf16[4096,768]{1,0:T(8,128)(2,1)}, bf16[512,768]{1,0:T(8,128)(2,1)S(1)}, f32[768,1152]{1,0:T(8,128)S(1)}, f32[8,768]{1,0:T(8,128)S(1)}, f32[8,1152]{1,0:T(8,128)S(1)}) custom-call(s32[18]{0:T(128)S(1)} %or_convert_fusion.has, s32[18]{0:T(128)S(1)} %select_select_fusion.spot, bf16[4096,768]{1,0:T(8,128)(2,1)} %bitcast.350, ...), custom_call_target="tpu_custom_call" | custom-call | flops 12683575296 | bytes 31457280 | tf_op jit(solution)/shard_map/unproject/pallas_call | solution.py:509
  631.3 1.8 copy-done.41
  641.2 51.8 %attend_backward.5 = (bf16[1536,384]{1,0:T(8,128)(2,1)}, bf16[4096,768]{1,0:T(8,128)(2,1)}, bf16[512,768]{1,0:T(8,128)(2,1)}) custom-call(s32[6,5]{1,0:T(8,128)} %copy-done.25, bf16[1536,384]{1,0:T(8,128)(2,1)} %copy-done.38, bf16[1536,384]{1,0:T(8,128)(2,1)} %pad_maximum_fusion.8.do_ref, bf16[1536,384]{1,0:T(8,128)(2,1)} %copy-done.11, ...), custom_call_target="tpu_custom_call" | custom-call | flops 48318382080 | bytes 31457280 | tf_op jit(solution)/shard_map/attend_backward/pallas_call | solution.py:326
  694.5 2.0 copy-done.42
  697.9 29.9 %unproject.5 = (bf16[4096,768]{1,0:T(8,128)(2,1)}, bf16[512,768]{1,0:T(8,128)(2,1)S(1)}, f32[768,1152]{1,0:T(8,128)S(1)}, f32[8,768]{1,0:T(8,128)S(1)}, f32[8,1152]{1,0:T(8,128)S(1)}) custom-call(s32[18]{0:T(128)S(1)} %copy-done.28, s32[18]{0:T(128)S(1)} %copy-done.30, bf16[4096,768]{1,0:T(8,128)(2,1)} %bitcast.348, bf16[512,768]{1,0:T(8,128)(2,1)S(1)} %copy-done.18, ...), custom_call_target="tpu_custom_call" | custom-call | flops 12683575296 | bytes 31457280 | tf_op jit(solution)/shard_map/unproject/pallas_call | solution.py:509
  730.0 21.8 %reduce-scatter.9.cloned.1.call-done = bf16[512,768]{1,0:T(8,128)(2,1)} async-done(((bf16[4096,768]{1,0:T(8,128)(2,1)}), bf16[512,768]{1,0:T(8,128)(2,1)}) %reduce-scatter.9.cloned.1.call-update) | async-done | bytes 786448 | tf_op jit(solution)/shard_map/reduce_scatter | solution.py:1146
  753.1 2.5 fusion.10
  764.3 2.7 stack.336
  768.4 1.7 copy.204
  770.1 1.7 copy.205
  782.9 2.4 copy.210
  785.3 4.1 reshape.675
  789.4 1.7 copy.227
  791.2 2.4 fusion.73
  793.7 1.9 fusion.82
  799.4 6.0 collective-permute-done.26
  807.0 45.8 %collective-permute-start.29 = (bf16[2,48,1280]{2,1,0:T(8,128)(2,1)S(1)}, bf16[2,48,1280]{2,1,0:T(8,128)(2,1)S(1)}, u32[]{:S(2)}, u32[]{:S(2)}) collective-permute-start(bf16[2,48,1280]{2,1,0:T(8,128)(2,1)S(1)} %dynamic-slice_bitcast_fusion.8), channel_id=1, source_target_pairs={{0,2},{1,3},{2,0},{3,1},{4,6},{5,7},{6,4},{7,5},{8,10},{9,11},{10,... | collective-permute-start | bytes 737288 | tf_op jit(solution)/shard_map/ppermute | solution.py:810
  852.9 12.0 %collective-permute-done.29 = bf16[2,48,1280]{2,1,0:T(8,128)(2,1)S(1)} collective-permute-done((bf16[2,48,1280]{2,1,0:T(8,128)(2,1)S(1)}, bf16[2,48,1280]{2,1,0:T(8,128)(2,1)S(1)}, u32[]{:S(2)}, u32[]{:S(2)}) %collective-permute-start.29) | collective-permute-done | bytes 245792 | tf_op jit(solution)/shard_map/ppermute | solution.py:810
  865.0 1.9 collective-permute-start.30
  868.3 6.1 collective-permute-done.30
  879.4 3.3 fusion.5
  (502 shorter events, 129.2 us)
Async XLA Ops:
  7.2 59.5 %all-gather.8.cloned.1.call-start = ((), (), s32[]{:S(2)}) async-start(), calls=%async_computation.4 | async-start | bytes 4036608 | tf_op jit(solution)/shard_map/all_gather | solution.py:841
  21.9 110.7 %all-gather.10.cloned.1.call-start = ((), (), s32[]{:S(2)}) async-start(), calls=%async_computation.9 | async-start | bytes 7077888 | tf_op jit(solution)/shard_map/all_gather | solution.py:1011
  23.4 174.8 %all-gather.12.cloned.1.call-start = ((), (), s32[]{:S(2)}) async-start(), calls=%async_computation.10 | async-start | bytes 7077888 | tf_op jit(solution)/shard_map/all_gather | solution.py:1011
  24.1 239.6 %all-gather.14.cloned.1.call-start = ((), (), s32[]{:S(2)}) async-start(), calls=%async_computation.11 | async-start | bytes 7077888 | tf_op jit(solution)/shard_map/all_gather | solution.py:1011
  24.6 7.6 collective-permute-start.1
  25.2 4.2 collective-permute-start
  25.3 559.9 %reduce-scatter.5.cloned.1.call-start = ((), (), s32[]{:S(2)}) async-start(), calls=%async_computation.5 | async-start | bytes 11943936 | tf_op jit(solution)/shard_map/reduce_scatter | solution.py:1126
  28.5 570.4 %copy-start.29 = (s32[18]{0:T(128)}, s32[18]{0:T(128)S(1)}, u32[]{:S(2)}) copy-start(s32[18]{0:T(128)S(1)} %select_select_fusion.spot) | copy-start | bytes 220
  28.5 570.4 %copy-start.27 = (s32[18]{0:T(128)}, s32[18]{0:T(128)S(1)}, u32[]{:S(2)}) copy-start(s32[18]{0:T(128)S(1)} %or_convert_fusion.has) | copy-start | bytes 220
  32.2 254.1 %copy-start.25 = (s32[6,5]{1,0:T(8,128)}, s32[6,5]{1,0:T(8,128)S(1)}, u32[]{:S(2)}) copy-start(s32[6,5]{1,0:T(8,128)S(1)} %fusion.91.info) | copy-start | bytes 364
  32.2 121.8 %copy-start.24 = (s32[6,5]{1,0:T(8,128)}, s32[6,5]{1,0:T(8,128)S(1)}, u32[]{:S(2)}) copy-start(s32[6,5]{1,0:T(8,128)S(1)} %get-tuple-element.320.info) | copy-start | bytes 364
  32.3 187.2 %copy-start.23 = (s32[6,5]{1,0:T(8,128)}, s32[6,5]{1,0:T(8,128)S(1)}, u32[]{:S(2)}) copy-start(s32[6,5]{1,0:T(8,128)S(1)} %get-tuple-element.321.info) | copy-start | bytes 364
  35.1 163.1 %copy-start.19 = (bf16[512,768]{1,0:T(8,128)(2,1)}, bf16[512,768]{1,0:T(8,128)(2,1)S(1)}, u32[]{:S(2)}) copy-start(bf16[512,768]{1,0:T(8,128)(2,1)S(1)} %get-tuple-element.340.xc_ref) | copy-start | bytes 2359300
  68.7 8.9 collective-permute-start.3
  70.3 8.9 collective-permute-start.2
  73.1 20.2 %collective-permute-start.9 = (bf16[48,6912]{1,0:T(8,128)(2,1)S(1)}, bf16[48,6912]{1,0:T(8,128)(2,1)S(1)}, u32[]{:S(2)}, u32[]{:S(2)}) collective-permute-start(bf16[48,6912]{1,0:T(8,128)(2,1)S(1)} %get-tuple-element.266), channel_id=1, source_target_pairs={{0,8},{8,0},{16,24},{24,16},{1,9},{9,1},{17,25},{25,17},{2,10},{10... | collective-permute-start | bytes 1990664 | tf_op jit(solution)/shard_map/ppermute | solution.py:810
  73.8 21.3 %collective-permute-start.13 = (bf16[48,6912]{1,0:T(8,128)(2,1)S(1)}, bf16[48,6912]{1,0:T(8,128)(2,1)S(1)}, u32[]{:S(2)}, u32[]{:S(2)}) collective-permute-start(bf16[48,6912]{1,0:T(8,128)(2,1)S(1)} %get-tuple-element.265), channel_id=1, source_target_pairs={{0,16},{8,24},{16,0},{24,8},{1,17},{9,25},{17,1},{25,9},{2,18},{10... | collective-permute-start | bytes 1990664 | tf_op jit(solution)/shard_map/ppermute | solution.py:810
  77.6 26.2 %collective-permute-start.4 = (bf16[2,96,1280]{2,1,0:T(8,128)(2,1)S(1)}, bf16[2,96,1280]{2,1,0:T(8,128)(2,1)S(1)}, u32[]{:S(2)}, u32[]{:S(2)}) collective-permute-start(bf16[2,96,1280]{2,1,0:T(8,128)(2,1)S(1)} %pad_maximum_fusion.16), channel_id=1, source_target_pairs={{0,8},{8,0},{16,24},{24,16},{1,9},{9,1},{17,25},{25,17},{2,10},{10... | collective-permute-start | bytes 1474568 | tf_op jit(solution)/shard_map/ppermute | solution.py:810
  79.2 24.7 %collective-permute-start.5 = (bf16[2,96,1280]{2,1,0:T(8,128)(2,1)S(1)}, bf16[2,96,1280]{2,1,0:T(8,128)(2,1)S(1)}, u32[]{:S(2)}, u32[]{:S(2)}) collective-permute-start(bf16[2,96,1280]{2,1,0:T(8,128)(2,1)S(1)} %pad_maximum_fusion.17), channel_id=1, source_target_pairs={{0,16},{8,24},{16,0},{24,8},{1,17},{9,25},{17,1},{25,9},{2,18},{10... | collective-permute-start | bytes 1474568 | tf_op jit(solution)/shard_map/ppermute | solution.py:810
  94.5 222.1 %collective-permute-start.11 = (bf16[2,48,6912]{2,1,0:T(8,128)(2,1)}, bf16[2,48,6912]{2,1,0:T(8,128)(2,1)}, u32[]{:S(2)}, u32[]{:S(2)}) collective-permute-start(bf16[2,48,6912]{2,1,0:T(8,128)(2,1)} %pad_maximum_fusion.6.refs_0_), channel_id=1, source_target_pairs={{0,16},{8,24},{16,0},{24,8},{1,17},{9,25},{17,1},{25,9},{2,18},{10... | collective-permute-start | bytes 3981320 | tf_op jit(solution)/shard_map/ppermute | solution.py:810
  96.3 220.6 %collective-permute-start.15 = (bf16[2,48,6912]{2,1,0:T(8,128)(2,1)}, bf16[2,48,6912]{2,1,0:T(8,128)(2,1)}, u32[]{:S(2)}, u32[]{:S(2)}) collective-permute-start(bf16[2,48,6912]{2,1,0:T(8,128)(2,1)} %pad_maximum_fusion.7.refs_4_), channel_id=1, source_target_pairs={{0,8},{8,0},{16,24},{24,16},{1,9},{9,1},{17,25},{25,17},{2,10},{10... | collective-permute-start | bytes 3981320 | tf_op jit(solution)/shard_map/ppermute | solution.py:810
  106.7 157.0 %copy-start.6 = (bf16[768,1152]{1,0:T(8,128)(2,1)}, bf16[768,1152]{1,0:T(8,128)(2,1)S(1)}, u32[]{:S(2)}) copy-start(bf16[768,1152]{1,0:T(8,128)(2,1)S(1)} %slice.390.w_ref) | copy-start | bytes 5308420
  106.7 492.2 %copy-start.21 = (f32[8,768]{1,0:T(8,128)}, f32[8,768]{1,0:T(8,128)S(1)}, u32[]{:S(2)}) copy-start(f32[8,768]{1,0:T(8,128)S(1)} %stack.306.vec_ref) | copy-start | bytes 73732
  315.2 2.1 collective-permute-start.8
  316.1 2.4 collective-permute-start.7
  316.3 13.2 %collective-permute-start.10 = (bf16[2,48,6912]{2,1,0:T(8,128)(2,1)}, bf16[2,48,6912]{2,1,0:T(8,128)(2,1)}, u32[]{:S(2)}, u32[]{:S(2)}) collective-permute-start(bf16[2,48,6912]{2,1,0:T(8,128)(2,1)} %pad_maximum_fusion.6.refs_0_), channel_id=1, source_target_pairs={{0,1},{1,0},{2,3},{3,2},{4,5},{5,4},{6,7},{7,6},{8,9},{9,8},{10,11... | collective-permute-start | bytes 3981320 | tf_op jit(solution)/shard_map/ppermute | solution.py:810
  316.6 12.9 %collective-permute-start.14 = (bf16[2,48,6912]{2,1,0:T(8,128)(2,1)}, bf16[2,48,6912]{2,1,0:T(8,128)(2,1)}, u32[]{:S(2)}, u32[]{:S(2)}) collective-permute-start(bf16[2,48,6912]{2,1,0:T(8,128)(2,1)} %pad_maximum_fusion.7.refs_4_), channel_id=1, source_target_pairs={{0,1},{1,0},{2,3},{3,2},{4,5},{5,4},{6,7},{7,6},{8,9},{9,8},{10,11... | collective-permute-start | bytes 3981320 | tf_op jit(solution)/shard_map/ppermute | solution.py:810
  316.8 12.6 %collective-permute-start.12 = (bf16[2,48,6912]{2,1,0:T(8,128)(2,1)}, bf16[2,48,6912]{2,1,0:T(8,128)(2,1)}, u32[]{:S(2)}, u32[]{:S(2)}) collective-permute-start(bf16[2,48,6912]{2,1,0:T(8,128)(2,1)} %collective-permute-done.11.refs_2_), channel_id=1, source_target_pairs={{0,1},{1,0},{2,3},{3,2},{4,5},{5,4},{6,7},{7,6},{8,9},{9,8},{10,11... | collective-permute-start | bytes 3981320 | tf_op jit(solution)/shard_map/ppermute | solution.py:810
  317.3 12.2 %collective-permute-start.16 = (bf16[2,48,6912]{2,1,0:T(8,128)(2,1)}, bf16[2,48,6912]{2,1,0:T(8,128)(2,1)}, u32[]{:S(2)}, u32[]{:S(2)}) collective-permute-start(bf16[2,48,6912]{2,1,0:T(8,128)(2,1)} %collective-permute-done.15.refs_6_), channel_id=1, source_target_pairs={{0,1},{1,0},{2,3},{3,2},{4,5},{5,4},{6,7},{7,6},{8,9},{9,8},{10,11... | collective-permute-start | bytes 3981320 | tf_op jit(solution)/shard_map/ppermute | solution.py:810
  318.5 8.4 collective-permute-start.6
  437.5 203.7 %reduce-scatter.7.cloned.1.call-start = ((), (), s32[]{:S(2)}) async-start(), calls=%async_computation.6 | async-start | bytes 7077888 | tf_op jit(solution)/shard_map/reduce_scatter | solution.py:1146
  437.5 4.0 collective-permute-start.17
  531.1 220.6 %reduce-scatter.9.cloned.1.call-start = ((), (), s32[]{:S(2)}) async-start(), calls=%async_computation.7 | async-start | bytes 7077888 | tf_op jit(solution)/shard_map/reduce_scatter | solution.py:1146
  586.8 10.0 %collective-permute-start.19 = (bf16[2,24,3456]{2,1,0:T(8,128)(2,1)S(1)}, bf16[2,24,3456]{2,1,0:T(8,128)(2,1)S(1)}, u32[]{:S(2)}, u32[]{:S(2)}) collective-permute-start(bf16[2,24,3456]{2,1,0:T(8,128)(2,1)S(1)} %dynamic-slice_bitcast_fusion.6), channel_id=1, source_target_pairs={{0,16},{8,24},{16,0},{24,8},{1,17},{9,25},{17,1},{25,9},{2,18},{10... | collective-permute-start | bytes 995336 | tf_op jit(solution)/shard_map/ppermute | solution.py:810
  588.4 9.7 %collective-permute-start.18 = (bf16[2,24,3456]{2,1,0:T(8,128)(2,1)S(1)}, bf16[2,24,3456]{2,1,0:T(8,128)(2,1)S(1)}, u32[]{:S(2)}, u32[]{:S(2)}) collective-permute-start(bf16[2,24,3456]{2,1,0:T(8,128)(2,1)S(1)} %dynamic-slice_bitcast_fusion.7), channel_id=1, source_target_pairs={{0,8},{8,0},{16,24},{24,16},{1,9},{9,1},{17,25},{25,17},{2,10},{10... | collective-permute-start | bytes 995336 | tf_op jit(solution)/shard_map/ppermute | solution.py:810
  634.3 245.0 %reduce-scatter.11.cloned.1.call-start = ((), (), s32[]{:S(2)}) async-start(), calls=%async_computation.8 | async-start | bytes 7077888 | tf_op jit(solution)/shard_map/reduce_scatter | solution.py:1161
  638.6 54.5 %collective-permute-start.20 = (bf16[24,3456]{1,0:T(8,128)(2,1)S(1)}, bf16[24,3456]{1,0:T(8,128)(2,1)S(1)}, u32[]{:S(2)}, u32[]{:S(2)}) collective-permute-start(bf16[24,3456]{1,0:T(8,128)(2,1)S(1)} %dynamic-slice_bitcast_fusion.12), channel_id=1, source_target_pairs={{0,16},{8,24},{16,0},{24,8},{1,17},{9,25},{17,1},{25,9},{2,18},{10... | collective-permute-start | bytes 497672 | tf_op jit(solution)/shard_map/ppermute | solution.py:810
  639.6 53.5 %collective-permute-start.21 = (bf16[24,3456]{1,0:T(8,128)(2,1)S(1)}, bf16[24,3456]{1,0:T(8,128)(2,1)S(1)}, u32[]{:S(2)}, u32[]{:S(2)}) collective-permute-start(bf16[24,3456]{1,0:T(8,128)(2,1)S(1)} %dynamic-slice_bitcast_fusion.11), channel_id=1, source_target_pairs={{0,8},{8,0},{16,24},{24,16},{1,9},{9,1},{17,25},{25,17},{2,10},{10... | collective-permute-start | bytes 497672 | tf_op jit(solution)/shard_map/ppermute | solution.py:810
  759.6 31.5 %collective-permute-start.22 = (bf16[256,768]{1,0:T(8,128)(2,1)}, bf16[256,768]{1,0:T(8,128)(2,1)}, u32[]{:S(2)}, u32[]{:S(2)}) collective-permute-start(bf16[256,768]{1,0:T(8,128)(2,1)} %slice.345), channel_id=1, source_target_pairs={{0,1},{1,0},{2,3},{3,2},{4,5},{5,4},{6,7},{7,6},{8,9},{9,8},{10,11... | collective-permute-start | bytes 1179656 | tf_op jit(solution)/shard_map/ppermute | solution.py:810
  760.4 30.7 %collective-permute-start.23 = (bf16[256,768]{1,0:T(8,128)(2,1)}, bf16[256,768]{1,0:T(8,128)(2,1)}, u32[]{:S(2)}, u32[]{:S(2)}) collective-permute-start(bf16[256,768]{1,0:T(8,128)(2,1)} %slice.348), channel_id=1, source_target_pairs={{0,1},{1,0},{2,3},{3,2},{4,5},{5,4},{6,7},{7,6},{8,9},{9,8},{10,11... | collective-permute-start | bytes 1179656 | tf_op jit(solution)/shard_map/ppermute | solution.py:810
  775.8 19.8 %collective-permute-start.25 = (bf16[2,96,1280]{2,1,0:T(8,128)(2,1)}, bf16[2,96,1280]{2,1,0:T(8,128)(2,1)}, u32[]{:S(2)}, u32[]{:S(2)}) collective-permute-start(bf16[2,96,1280]{2,1,0:T(8,128)(2,1)} %dynamic-slice_bitcast_fusion.1), channel_id=1, source_target_pairs={{0,8},{8,0},{16,24},{24,16},{1,9},{9,1},{17,25},{25,17},{2,10},{10... | collective-permute-start | bytes 1474568 | tf_op jit(solution)/shard_map/ppermute | solution.py:810
  778.1 19.4 %collective-permute-start.27 = (bf16[2,96,1280]{2,1,0:T(8,128)(2,1)}, bf16[2,96,1280]{2,1,0:T(8,128)(2,1)}, u32[]{:S(2)}, u32[]{:S(2)}) collective-permute-start(bf16[2,96,1280]{2,1,0:T(8,128)(2,1)} %dynamic-slice_bitcast_fusion), channel_id=1, source_target_pairs={{0,16},{8,24},{16,0},{24,8},{1,17},{9,25},{17,1},{25,9},{2,18},{10... | collective-permute-start | bytes 1474568 | tf_op jit(solution)/shard_map/ppermute | solution.py:810
  780.4 10.8 %collective-permute-start.24 = (bf16[256,768]{1,0:T(8,128)(2,1)}, bf16[256,768]{1,0:T(8,128)(2,1)}, u32[]{:S(2)}, u32[]{:S(2)}) collective-permute-start(bf16[256,768]{1,0:T(8,128)(2,1)} %slice.351), channel_id=1, source_target_pairs={{0,1},{1,0},{2,3},{3,2},{4,5},{5,4},{6,7},{7,6},{8,9},{9,8},{10,11... | collective-permute-start | bytes 1179656 | tf_op jit(solution)/shard_map/ppermute | solution.py:810
  796.9 8.4 collective-permute-start.26
  798.7 8.2 collective-permute-start.28
  807.0 57.8 %collective-permute-start.29 = (bf16[2,48,1280]{2,1,0:T(8,128)(2,1)S(1)}, bf16[2,48,1280]{2,1,0:T(8,128)(2,1)S(1)}, u32[]{:S(2)}, u32[]{:S(2)}) collective-permute-start(bf16[2,48,1280]{2,1,0:T(8,128)(2,1)S(1)} %dynamic-slice_bitcast_fusion.8), channel_id=1, source_target_pairs={{0,2},{1,3},{2,0},{3,1},{4,6},{5,7},{6,4},{7,5},{8,10},{9,11},{10,... | collective-permute-start | bytes 737288 | tf_op jit(solution)/shard_map/ppermute | solution.py:810
  865.0 9.4 %collective-permute-start.30 = (bf16[48,1280]{1,0:T(8,128)(2,1)S(1)}, bf16[48,1280]{1,0:T(8,128)(2,1)S(1)}, u32[]{:S(2)}, u32[]{:S(2)}) collective-permute-start(bf16[48,1280]{1,0:T(8,128)(2,1)S(1)} %dynamic-slice_bitcast_fusion.13), channel_id=1, source_target_pairs={{0,4},{1,5},{2,6},{3,7},{4,0},{5,1},{6,2},{7,3},{8,12},{9,13},{10,... | collective-permute-start | bytes 368648 | tf_op jit(solution)/shard_map/ppermute | solution.py:810
  874.4 1.3 collective-permute-start.31
  (109 other events, 947.2 us)
Sparse Core Ops, SparseCore 0:
  22.0 44.6 all-gather.7
  68.9 63.6 all-gather.9
  134.7 63.3 all-gather.11
  200.3 63.3 all-gather.13
  437.6 121.1 reduce-scatter.4
  561.1 69.7 reduce-scatter.6
  633.8 117.8 reduce-scatter.8
  754.2 118.0 reduce-scatter.10

commit v3 on v2

--- a/solution.py
+++ b/solution.py
@@ -43,23 +43,95 @@
     return (lane < HEAD_DIM, lane >= HEAD_DIM)
 
 
+def normal_form(value):
+    center = value - jnp.mean(value, axis=1, keepdims=True)
+    return center * lax.rsqrt(jnp.mean(center * center, axis=1, keepdims=True) + EPSILON)
+
+
+def flip(value):
+    return jnp.transpose(value.astype(F32)).astype(BF)
+
+
+def stream_rows(xp_hbm, xc_hbm, rows, sems, visit):
+    size = rows.shape[1]
+    count = xp_hbm.shape[0] // size
+    crow = xc_hbm.shape[0] // 2
+    part = min(size, crow)
+
+    def fetch(index, slot):
+        row = pl.multiple_of(index * size, size)
+        return pltpu.make_async_copy(xp_hbm.at[pl.ds(row, size)], rows.at[slot], sems.at[slot])
+
+    fetch(0, 0).start()
+
+    def one(index, carry):
+        slot = lax.rem(index, 2)
+
+        @pl.when(index + 1 < count)
+        def _():
+            fetch(index + 1, 1 - slot).start()
+
+        fetch(index, slot).wait()
+        visit(pl.multiple_of(index * size, size), size, rows[slot].astype(F32))
+        return carry
+
+    lax.fori_loop(0, count, one, 0)
+    for index in range(2 * crow // part):
+        copy = pltpu.make_async_copy(
+            xc_hbm.at[pl.ds(index * part, part)], rows.at[0, pl.ds(0, part)], sems.at[0]
+        )
+        copy.start()
+        copy.wait()
+        visit(count * size + index * part, part, rows[0, :part].astype(F32))
+
+
 def attend_forward_kernel(
-    info, q_ref, kvp_hbm, kvc_hbm, o_ref, lse_ref, kv, qm, s_ref, mx, acc, sems
+    info,
+    spot,
+    xp_hbm,
+    xc_hbm,
+    xqp_ref,
+    xqc_ref,
+    w_ref,
+    vec_ref,
+    o_ref,
+    lse_ref,
+    q_ref,
+    kv_hbm,
+    kv,
+    rows,
+    qm,
+    s_ref,
+    mx,
+    acc,
+    sems,
+    done,
 ):
     block = pl.program_id(0)
-    prompt_rows = kvp_hbm.shape[0]
-    cont_rows = kvc_hbm.shape[0]
+    gain, shift, bias_kv, bias_q = (vec_ref[i : i + 1, :] for i in range(4))
+
+    def store(row, size):
+        index = row // rows.shape[1]
+        if isinstance(row, int):
+            index = xp_hbm.shape[0] // rows.shape[1] + (row - xp_hbm.shape[0]) // size
+        return pltpu.make_async_copy(
+            kv.at[pl.ds(row, size)], kv_hbm.at[pl.ds(row, size)], done.at[index]
+        )
 
     @pl.when(block == 0)
     def _():
-        one = pltpu.make_async_copy(kvp_hbm, kv.at[pl.ds(0, prompt_rows)], sems.at[0])
-        two = pltpu.make_async_copy(kvc_hbm, kv.at[pl.ds(prompt_rows, cont_rows)], sems.at[1])
-        one.start()
-        two.start()
-        one.wait()
-        two.wait()
+        def visit(row, size, x):
+            normed = (normal_form(x) * gain + shift).astype(BF)
+            kv[pl.ds(row, size), :] = (dot_nn(normed, w_ref[:, HALF:]) + bias_kv).astype(BF)
+            store(row, size).start()
+
+        stream_rows(xp_hbm, xc_hbm, rows, sems, visit)
 
     TQ = q_ref.shape[0]
+    x = jnp.where(spot[block, 0] > 0, xqc_ref[...].astype(F32), xqp_ref[...].astype(F32))
+    normed = (normal_form(x) * gain + shift).astype(BF)
+    query = ((dot_nn(normed, w_ref[:, :HALF]) + bias_q[:, :HALF]) * QSCALE).astype(BF)
+    q_ref[...] = query
     base = pl.multiple_of(info[block, 0], TQ)
     tiles = info[block, 1]
     extra = info[block, 2]
@@ -68,7 +140,7 @@
     low, high = half_masks(TQ)
     zero = jnp.zeros((TQ, 128), BF)
     for pair in range(PAIRS):
-        part = q_ref[:, pair * 128 : (pair + 1) * 128]
+        part = query[:, pair * 128 : (pair + 1) * 128]
         qm[2 * pair] = jnp.where(low, part, zero)
         qm[2 * pair + 1] = jnp.where(high, part, zero)
 
@@ -143,94 +215,148 @@
             lse_ref[0, 2 * pair + side] = tall[0]
         o_ref[:, pair * 128 : (pair + 1) * 128] = jnp.where(low, sides[0], sides[1]).astype(BF)
 
-
-def attend_forward(info, q, kvp, kvc, TQ):
-    rows = q.shape[0]
-    keys = kvp.shape[0] + kvc.shape[0]
-    blocks = rows // TQ
+    @pl.when(block == pl.num_programs(0) - 1)
+    def _():
+        size = rows.shape[1]
+        part = min(size, xc_hbm.shape[0] // 2)
+        for row in range(0, xp_hbm.shape[0], size):
+            pltpu.make_async_copy(
+                kv.at[pl.ds(row, size)], kv_hbm.at[pl.ds(row, size)], done.at[row // size]
+            ).wait()
+        for row in range(xp_hbm.shape[0], kv.shape[0], part):
+            store(row, part).wait()
+
+
+def query_specs(TQ):
+    prompts = pl.BlockSpec((TQ, D), lambda i, s, t: (t[i, 1], 0))
+    conts = pl.BlockSpec((TQ, D), lambda i, s, t: (t[i, 2], 0))
+    return prompts, conts
+
+
+def attend_forward(info, spot, xp, xc, weight, vec, TQ, size):
+    blocks = info.shape[0]
+    count = blocks * TQ
+    keys = xp.shape[0] + xc.shape[0]
+    tiles = xp.shape[0] // size + xc.shape[0] // min(size, xc.shape[0] // 2)
+    whole = pl.BlockSpec(memory_space=pl.ANY)
+    heads = pl.BlockSpec((TQ, HALF), lambda i, s, t: (i, 0))
+    shape = jax.ShapeDtypeStruct
     return pl.pallas_call(
         attend_forward_kernel,
         grid_spec=pltpu.PrefetchScalarGridSpec(
-            num_scalar_prefetch=1,
+            num_scalar_prefetch=2,
             grid=(blocks,),
             in_specs=[
-                pl.BlockSpec((TQ, HALF), lambda i, s: (i, 0)),
-                pl.BlockSpec(memory_space=pl.ANY),
-                pl.BlockSpec(memory_space=pl.ANY),
+                whole,
+                whole,
+                *query_specs(TQ),
+                pl.BlockSpec(weight.shape, lambda i, s, t: (0, 0)),
+                pl.BlockSpec(vec.shape, lambda i, s, t: (0, 0)),
             ],
-            out_specs=[
-                pl.BlockSpec((TQ, HALF), lambda i, s: (i, 0)),
-                pl.BlockSpec((1, 8, TQ), lambda i, s: (i, 0, 0)),
-            ],
+            out_specs=[heads, pl.BlockSpec((1, 8, TQ), lambda i, s, t: (i, 0, 0)), heads, whole],
             scratch_shapes=[
                 pltpu.VMEM((keys, D), BF),
+                pltpu.VMEM((2, size, D), BF),
                 pltpu.VMEM((NH, TQ, 128), BF),
                 pltpu.VMEM((4, TQ, PLEN + TK), F32),
                 pltpu.VMEM((4, TQ, 128), F32),
                 pltpu.VMEM((2, TQ, 256), F32),
                 pltpu.SemaphoreType.DMA((2,)),
+                pltpu.SemaphoreType.DMA((tiles,)),
             ],
         ),
         out_shape=(
-            jax.ShapeDtypeStruct((rows, HALF), BF),
-            jax.ShapeDtypeStruct((blocks, 8, TQ), F32),
+            shape((count, HALF), BF),
+            shape((blocks, 8, TQ), F32),
+            shape((count, HALF), BF),
+            shape((keys, D), BF),
         ),
         compiler_params=pltpu.CompilerParams(
-            dimension_semantics=("arbitrary",), vmem_limit_bytes=50 << 20
+            dimension_semantics=("arbitrary",), vmem_limit_bytes=56 << 20
         ),
         cost_estimate=pl.CostEstimate(
-            flops=int(4 * rows * PLEN * HALF * 4), bytes_accessed=20 << 20, transcendentals=0
+            flops=int(4 * count * PLEN * HALF * 4) + 2 * D * D * keys,
+            bytes_accessed=20 << 20,
+            transcendentals=0,
         ),
         name="attend_forward",
-    )(info, q, kvp, kvc)
+    )(info, spot, xp, xc, xp, xc, weight, vec)
 
 
 def attend_backward_kernel(
+    chained,
     info,
+    spot,
+    xp_hbm,
+    xc_hbm,
+    kv_hbm,
+    xqp_ref,
+    xqc_ref,
     q_ref,
     do_ref,
     o_ref,
     lse_ref,
-    kvp_hbm,
-    kvc_hbm,
-    dq_ref,
-    dkvp_hbm,
-    dkvc_hbm,
-    kv,
-    kt,
-    dkv,
-    qm,
-    dom,
-    dqt,
-    drow,
-    sems,
+    w_ref,
+    vec_ref,
+    *refs,
 ):
+    if chained:
+        old_w, old_vec, old_bias = refs[:3]
+        refs = refs[3:]
+    (
+        tp_hbm,
+        tc_hbm,
+        gw_hbm,
+        gvec_ref,
+        gbias_ref,
+        kv,
+        kt,
+        dkv,
+        gw,
+        qd,
+        rows,
+        table,
+        qm,
+        dom,
+        dqt,
+        drow,
+        sems,
+        done,
+    ) = refs
+    block = pl.program_id(0)
     TQ = q_ref.shape[0]
-    block = pl.program_id(0)
-    prompt_rows = kvp_hbm.shape[0]
-    cont_rows = kvc_hbm.shape[0]
-    keys_all = prompt_rows + cont_rows
+    keys_all = kv.shape[0]
+    gain, shift = (vec_ref[i : i + 1, :] for i in range(2))
 
     @pl.when(block == 0)
     def _():
-        one = pltpu.make_async_copy(kvp_hbm, kv.at[pl.ds(0, prompt_rows)], sems.at[0])
-        two = pltpu.make_async_copy(kvc_hbm, kv.at[pl.ds(prompt_rows, cont_rows)], sems.at[1])
-        one.start()
-        two.start()
-        one.wait()
-        two.wait()
+        load = pltpu.make_async_copy(kv_hbm, kv, sems.at[0])
+        load.start()
+        if chained:
+            more = pltpu.make_async_copy(old_w, gw, sems.at[1])
+            more.start()
+            gvec_ref[...] = old_vec[...]
+            gbias_ref[...] = old_bias[...]
+        else:
+            gw[...] = jnp.zeros_like(gw)
+            gvec_ref[...] = jnp.zeros_like(gvec_ref)
+            gbias_ref[...] = jnp.zeros_like(gbias_ref)
+
+        def clear(index, carry):
+            dkv[pl.ds(pl.multiple_of(index * TQ, TQ), TQ), :] = jnp.zeros((TQ, D), F32)
+            return carry
+
+        lax.fori_loop(0, keys_all // TQ, clear, 0)
+        load.wait()
 
         def prepare(index, carry):
             row = pl.multiple_of(index * TQ, TQ)
-            dkv[pl.ds(row, TQ), :] = jnp.zeros((TQ, D), F32)
-            for pair in range(PAIRS):
-                piece = kv[pl.ds(row, TQ), pair * 128 : (pair + 1) * 128]
-                kt[pair * 128 : (pair + 1) * 128, pl.ds(row, TQ)] = jnp.transpose(
-                    piece.astype(F32)
-                ).astype(BF)
+            kt[:, pl.ds(row, TQ)] = flip(kv[pl.ds(row, TQ), :HALF])
             return carry
 
         lax.fori_loop(0, keys_all // TQ, prepare, 0)
+        if chained:
+            more.wait()
 
     base = pl.multiple_of(info[block, 0], TQ)
     tiles = info[block, 1]
@@ -296,246 +422,153 @@
         return carry
 
     lax.fori_loop(0, tiles, one, 0)
-    for pair in range(PAIRS):
-        lanes = slice(pair * 128, (pair + 1) * 128)
-        dq_ref[:, lanes] = (jnp.transpose(dqt[lanes, :]) * HEAD_DIM ** (-0.5)).astype(BF)
+    x = jnp.where(spot[block, 0] > 0, xqc_ref[...].astype(F32), xqp_ref[...].astype(F32))
+    dq_full = jnp.transpose(dqt[...]) * HEAD_DIM ** (-0.5)
+    dq = dq_full.astype(BF)
+    gw[:, :HALF] += dot_nn(flip(normal_form(x) * gain + shift), dq)
+    gbias_ref[0:1, :HALF] += jnp.sum(dq_full, axis=0, keepdims=True)
+    qd[pl.ds(pl.multiple_of(block * TQ, TQ), TQ), :] = dot_nt(dq, w_ref[:, :HALF])
 
     @pl.when(block == pl.num_programs(0) - 1)
     def _():
-        def finish(index, carry):
-            row = pl.multiple_of(index * TQ, TQ)
-            kv[pl.ds(row, TQ), :HALF] = (dkv[pl.ds(row, TQ), :HALF] * (1.0 / LOG2E)).astype(BF)
-            kv[pl.ds(row, TQ), HALF:] = dkv[pl.ds(row, TQ), HALF:].astype(BF)
-            return carry
-
-        lax.fori_loop(0, keys_all // TQ, finish, 0)
-        one = pltpu.make_async_copy(kv.at[pl.ds(0, prompt_rows)], dkvp_hbm, sems.at[0])
-        two = pltpu.make_async_copy(kv.at[pl.ds(prompt_rows, cont_rows)], dkvc_hbm, sems.at[1])
-        one.start()
-        two.start()
-        one.wait()
-        two.wait()
-
-
-def attend_backward(info, q, do, o, lse, kvp, kvc, TQ):
-    rows = q.shape[0]
-    keys = kvp.shape[0] + kvc.shape[0]
-    blocks = rows // TQ
-    tile = pl.BlockSpec((TQ, HALF), lambda i, s: (i, 0))
+        prompt_rows = xp_hbm.shape[0]
+        size = rows.shape[1]
+        crow = xc_hbm.shape[0] // 2
+        part = min(size, crow)
+        count = prompt_rows // size
+        own, mate = spot[0, 3], spot[0, 4]
+
+        def send(slot, row):
+            return pltpu.make_async_copy(
+                table.at[slot], tp_hbm.at[pl.ds(row, size)], done.at[slot]
+            )
+
+        def visit(row, size_now, x):
+            hat = normal_form(x)
+            grad_k = dkv[pl.ds(row, size_now), :HALF] * (1.0 / LOG2E)
+            grad_v = dkv[pl.ds(row, size_now), HALF:]
+            grad = jnp.concatenate([grad_k.astype(BF), grad_v.astype(BF)], axis=1)
+            gw[:, HALF:] += dot_nn(flip(hat * gain + shift), grad)
+            gbias_ref[0:1, HALF : 2 * HALF] += jnp.sum(grad_k, axis=0, keepdims=True)
+            gbias_ref[0:1, 2 * HALF :] += jnp.sum(grad_v, axis=0, keepdims=True)
+            change = dot_nt(grad, w_ref[:, HALF:])
+            if isinstance(row, int):
+                first = row - prompt_rows
+                which = first // crow
+                begin = which * (size + crow) + size + first - which * crow
+                change = change + qd[begin : begin + size_now, :]
+            else:
+                index = row // size
+                begin = jnp.where(index == mate, size + crow, 0)
+                begin = pl.multiple_of(begin, math.gcd(size, crow))
+                weight = jnp.where((index == own) | (index == mate), 1.0, 0.0)
+                change = change + weight * qd[pl.ds(begin, size_now), :]
+            gvec_ref[0:1, :] += jnp.sum(change * hat, axis=0, keepdims=True)
+            gvec_ref[1:2, :] += jnp.sum(change, axis=0, keepdims=True)
+            change = change.astype(BF)
+            if isinstance(row, int):
+                slot = (first // part) % 2
+                if first // part >= 2:
+                    pltpu.make_async_copy(
+                        table.at[slot, pl.ds(0, part)],
+                        tc_hbm.at[pl.ds(first - 2 * part, part)],
+                        done.at[slot],
+                    ).wait()
+                else:
+                    send(slot, prompt_rows - (2 - slot) * size).wait()
+                table[slot, :part] = change
+                pltpu.make_async_copy(
+                    table.at[slot, pl.ds(0, part)],
+                    tc_hbm.at[pl.ds(first, part)],
+                    done.at[slot],
+                ).start()
+            else:
+                slot = lax.rem(index, 2)
+
+                @pl.when(index >= 2)
+                def _():
+                    send(slot, pl.multiple_of(row - 2 * size, size)).wait()
+
+                table[slot] = change
+                send(slot, row).start()
+
+        stream_rows(xp_hbm, xc_hbm, rows, sems, visit)
+        last = 2 * crow // part
+        for index in range(last - 2, last):
+            pltpu.make_async_copy(
+                table.at[index % 2, pl.ds(0, part)],
+                tc_hbm.at[pl.ds(index * part, part)],
+                done.at[index % 2],
+            ).wait()
+        out = pltpu.make_async_copy(gw, gw_hbm, sems.at[0])
+        out.start()
+        out.wait()
+
+
+def attend_backward(info, spot, xp, xc, kv, q, do, o, lse, weight, vec, totals, TQ, size):
+    blocks = info.shape[0]
+    count = blocks * TQ
+    keys = kv.shape[0]
     whole = pl.BlockSpec(memory_space=pl.ANY)
+    heads = pl.BlockSpec((TQ, HALF), lambda i, s, t: (i, 0))
+    shape = jax.ShapeDtypeStruct
+    fixed = [
+        pl.BlockSpec((8, D), lambda i, s, t: (0, 0)),
+        pl.BlockSpec((8, 3 * HALF), lambda i, s, t: (0, 0)),
+    ]
+    extra = () if totals is None else tuple(totals)
     return pl.pallas_call(
-        attend_backward_kernel,
+        functools.partial(attend_backward_kernel, totals is not None),
         grid_spec=pltpu.PrefetchScalarGridSpec(
-            num_scalar_prefetch=1,
+            num_scalar_prefetch=2,
             grid=(blocks,),
             in_specs=[
-                tile,
-                tile,
-                tile,
-                pl.BlockSpec((1, 8, TQ), lambda i, s: (i, 0, 0)),
                 whole,
                 whole,
-            ],
-            out_specs=[tile, whole, whole],
+                whole,
+                *query_specs(TQ),
+                heads,
+                heads,
+                heads,
+                pl.BlockSpec((1, 8, TQ), lambda i, s, t: (i, 0, 0)),
+                pl.BlockSpec(weight.shape, lambda i, s, t: (0, 0)),
+                pl.BlockSpec(vec.shape, lambda i, s, t: (0, 0)),
+            ]
+            + ([whole] + fixed if extra else []),
+            out_specs=[whole, whole, whole] + fixed,
             scratch_shapes=[
                 pltpu.VMEM((keys, D), BF),
                 pltpu.VMEM((HALF, keys), BF),
                 pltpu.VMEM((keys, D), F32),
+                pltpu.VMEM((D, 3 * HALF), F32),
+                pltpu.VMEM((count, D), F32),
+                pltpu.VMEM((2, size, D), BF),
+                pltpu.VMEM((2, size, D), BF),
                 pltpu.VMEM((NH, TQ, 128), BF),
                 pltpu.VMEM((NH, TQ, 128), BF),
                 pltpu.VMEM((HALF, TQ), F32),
                 pltpu.VMEM((8, TQ), F32),
                 pltpu.SemaphoreType.DMA((2,)),
+                pltpu.SemaphoreType.DMA((2,)),
             ],
         ),
         out_shape=(
-            jax.ShapeDtypeStruct((rows, HALF), BF),
-            jax.ShapeDtypeStruct(kvp.shape, BF),
-            jax.ShapeDtypeStruct(kvc.shape, BF),
+            shape(xp.shape, BF),
+            shape(xc.shape, BF),
+            shape((D, 3 * HALF), F32),
+            shape((8, D), F32),
+            shape((8, 3 * HALF), F32),
         ),
         compiler_params=pltpu.CompilerParams(
-            dimension_semantics=("arbitrary",), vmem_limit_bytes=56 << 20
+            dimension_semantics=("arbitrary",), vmem_limit_bytes=62 << 20
         ),
         cost_estimate=pl.CostEstimate(
-            flops=int(10 * rows * PLEN * HALF * 4), bytes_accessed=30 << 20, transcendentals=0
+            flops=int(10 * count * PLEN * HALF * 4) + 4 * D * D * keys,
+            bytes_accessed=30 << 20,
+            transcendentals=0,
         ),
         name="attend_backward",
-    )(info, q, do, o, lse, kvp, kvc)
-
-
-def normal_form(value):
-    center = value - jnp.mean(value, axis=1, keepdims=True)
-    return center * lax.rsqrt(jnp.mean(center * center, axis=1, keepdims=True) + EPSILON)
-
-
-def flip(value):
-    return jnp.transpose(value.astype(F32)).astype(BF)
-
-
-def project_kernel(prompt_tiles, has, spot, xp_ref, xc_ref, w_ref, vec_ref, kvp_ref, kvc_ref, q_ref):
-    step = pl.program_id(0)
-    is_cont = step >= prompt_tiles
-    x = jnp.where(is_cont, xc_ref[...].astype(F32), xp_ref[...].astype(F32))
-    normed = (normal_form(x) * vec_ref[0:1, :] + vec_ref[1:2, :]).astype(BF)
-    kv = (dot_nn(normed, w_ref[:, HALF : 3 * HALF]) + vec_ref[2:3, :]).astype(BF)
-
-    @pl.when(jnp.logical_not(is_cont))
-    def _():
-        kvp_ref[...] = kv
-
-    @pl.when(is_cont)
-    def _():
-        kvc_ref[...] = kv
-
-    @pl.when(has[step] > 0)
-    def _():
-        query = dot_nn(normed, w_ref[:, :HALF]) + vec_ref[3:4, :HALF]
-        q_ref[...] = (query * QSCALE).astype(BF)
-
-
-def tile_specs(tile, prompt_tiles):
-    prompts = pl.BlockSpec((tile, D), lambda i, h, s: (jnp.minimum(i, prompt_tiles - 1), 0))
-    conts = pl.BlockSpec((tile, D), lambda i, h, s: (jnp.maximum(i - prompt_tiles, 0), 0))
-    heads = pl.BlockSpec((tile, HALF), lambda i, h, s: (s[i], 0))
-    return prompts, conts, heads
-
-
-def project(has, spot, xp, xc, weight, vec, rows, tile):
-    prompt_tiles = xp.shape[0] // tile
-    steps = prompt_tiles + xc.shape[0] // tile
-    prompts, conts, heads = tile_specs(tile, prompt_tiles)
-    total = xp.shape[0] + xc.shape[0]
-    return pl.pallas_call(
-        functools.partial(project_kernel, prompt_tiles),
-        grid_spec=pltpu.PrefetchScalarGridSpec(
-            num_scalar_prefetch=2,
-            grid=(steps,),
-            in_specs=[
-                prompts,
-                conts,
-                pl.BlockSpec(weight.shape, lambda i, h, s: (0, 0)),
-                pl.BlockSpec(vec.shape, lambda i, h, s: (0, 0)),
-            ],
-            out_specs=[prompts, conts, heads],
-        ),
-        out_shape=(
-            jax.ShapeDtypeStruct(xp.shape, BF),
-            jax.ShapeDtypeStruct(xc.shape, BF),
-            jax.ShapeDtypeStruct((rows, HALF), BF),
-        ),
-        compiler_params=pltpu.CompilerParams(
-            dimension_semantics=("arbitrary",), vmem_limit_bytes=32 << 20
-        ),
-        cost_estimate=pl.CostEstimate(
-            flops=2 * D * (total * D + rows * HALF), bytes_accessed=20 << 20, transcendentals=0
-        ),
-        name="project",
-    )(has, spot, xp, xc, weight, vec)
-
-
-def unproject_kernel(
-    prompt_tiles,
-    chained,
-    has,
-    spot,
-    xp_ref,
-    xc_ref,
-    dkvp_ref,
-    dkvc_ref,
-    dq_ref,
-    w_ref,
-    vec_ref,
-    *refs,
-):
-    if chained:
-        old_w, old_vec, old_bias = refs[:3]
-        refs = refs[3:]
-    tp_ref, tc_ref, gw_ref, gvec_ref, gbias_ref = refs
-    step = pl.program_id(0)
-    is_cont = step >= prompt_tiles
-
-    @pl.when(step == 0)
-    def _():
-        if chained:
-            gw_ref[...] = old_w[...]
-            gvec_ref[...] = old_vec[...]
-            gbias_ref[...] = old_bias[...]
-        else:
-            gw_ref[...] = jnp.zeros_like(gw_ref)
-            gvec_ref[...] = jnp.zeros_like(gvec_ref)
-            gbias_ref[...] = jnp.zeros_like(gbias_ref)
-
-    x = jnp.where(is_cont, xc_ref[...].astype(F32), xp_ref[...].astype(F32))
-    hat = normal_form(x)
-    normed_t = flip(hat * vec_ref[0:1, :] + vec_ref[1:2, :])
-    dkv = jnp.where(is_cont, dkvc_ref[...].astype(F32), dkvp_ref[...].astype(F32)).astype(BF)
-    gw_ref[:, HALF : 3 * HALF] += dot_nn(normed_t, dkv)
-    gbias_ref[0:1, HALF : 3 * HALF] += jnp.sum(dkv.astype(F32), axis=0, keepdims=True)
-    table = dot_nt(dkv, w_ref[:, HALF : 3 * HALF])
-
-    def finish(value):
-        gvec_ref[0:1, :] += jnp.sum(value * hat, axis=0, keepdims=True)
-        gvec_ref[1:2, :] += jnp.sum(value, axis=0, keepdims=True)
-        value = value.astype(BF)
-
-        @pl.when(jnp.logical_not(is_cont))
-        def _():
-            tp_ref[...] = value
-
-        @pl.when(is_cont)
-        def _():
-            tc_ref[...] = value
-
-    @pl.when(has[step] == 0)
-    def _():
-        finish(table)
-
-    @pl.when(has[step] > 0)
-    def _():
-        dq = dq_ref[...]
-        gw_ref[:, :HALF] += dot_nn(normed_t, dq)
-        gbias_ref[0:1, :HALF] += jnp.sum(dq.astype(F32), axis=0, keepdims=True)
-        finish(table + dot_nt(dq, w_ref[:, :HALF]))
-
-
-def unproject(has, spot, xp, xc, dkvp, dkvc, dq, weight, vec, totals, tile):
-    prompt_tiles = xp.shape[0] // tile
-    steps = prompt_tiles + xc.shape[0] // tile
-    prompts, conts, heads = tile_specs(tile, prompt_tiles)
-    total = xp.shape[0] + xc.shape[0]
-    shapes = ((D, 3 * HALF), (8, D), (8, 3 * HALF))
-    fixed = [pl.BlockSpec(shape, lambda i, h, s: (0, 0)) for shape in shapes]
-    extra = () if totals is None else tuple(totals)
-    return pl.pallas_call(
-        functools.partial(unproject_kernel, prompt_tiles, totals is not None),
-        grid_spec=pltpu.PrefetchScalarGridSpec(
-            num_scalar_prefetch=2,
-            grid=(steps,),
-            in_specs=[
-                prompts,
-                conts,
-                prompts,
-                conts,
-                heads,
-                pl.BlockSpec(weight.shape, lambda i, h, s: (0, 0)),
-                pl.BlockSpec(vec.shape, lambda i, h, s: (0, 0)),
-            ]
-            + (fixed if extra else []),
-            out_specs=[prompts, conts] + fixed,
-        ),
-        out_shape=(
-            jax.ShapeDtypeStruct(xp.shape, BF),
-            jax.ShapeDtypeStruct(xc.shape, BF),
-        )
-        + tuple(jax.ShapeDtypeStruct(shape, F32) for shape in shapes),
-        compiler_params=pltpu.CompilerParams(
-            dimension_semantics=("arbitrary",), vmem_limit_bytes=40 << 20
-        ),
-        cost_estimate=pl.CostEstimate(
-            flops=4 * D * (total * D + dq.shape[0] * HALF), bytes_accessed=30 << 20, transcendentals=0
-        ),
-        name="unproject",
-    )(has, spot, xp, xc, dkvp, dkvc, dq, weight, vec, *extra)
+    )(info, spot, xp, xc, kv, xp, xc, q, do, o, lse, weight, vec, *extra)
 
 
 def gelu_parts(value):
@@ -574,6 +607,7 @@
         gvec_ref,
         gbfc_ref,
         grads_hbm,
+        more_hbm,
         wp,
         wfc,
         wout,
@@ -592,28 +626,48 @@
 
     @pl.when(begin)
     def _():
-        loads = []
-        for index, piece in enumerate(pieces):
-            size = piece.shape[1]
-            for inner in range(piece.shape[0]):
-                row = pl.multiple_of(places[1 + index * piece.shape[0] + inner], 16)
-                turned = pl.multiple_of(lax.rem(row + core * HALF, D), 16)
-                source = piece.at[inner]
-                moves = [
-                    (source.at[:, pl.ds(0, D)], wp.at[pl.ds(turned, size), :]),
-                    (source.at[:, pl.ds(D, FF)], wfc.at[pl.ds(row, size), :]),
-                ]
-                for block in range(FF // D):
-                    moves.append(
-                        (
-                            source.at[:, pl.ds(D + FF + block * D, D)],
-                            wout.at[pl.ds(block * D + row, size), :],
-                        )
-                    )
-                for one, two in moves:
-                    loads.append(pltpu.make_async_copy(one, two, sems.at[len(loads)]))
-        for load in loads:
-            load.start()
+        def loads_of(first_half):
+            moves = []
+            for index, piece in enumerate(pieces):
+                size = piece.shape[1]
+                half = None
+                if first_half is not None:
+                    half = first_half if index < count // 2 else 1 - first_half
+                split = (D + 2 * FF) // 2 - D
+                spans = [(wp, 0, 0, D), (wfc, 0, D, FF)]
+                spans += [(wout, block * D, D + FF + block * D, D) for block in range(FF // D)]
+                if half == 0:
+                    spans = [(wp, 0, 0, D), (wfc, (0, 0), D, split)]
+                elif half == 1:
+                    spans = [(wfc, (0, split), 0, FF - split)]
+                    spans += [
+                        (wout, block * D, FF - split + block * D, D) for block in range(FF // D)
+                    ]
+                for inner in range(piece.shape[0]):
+                    row = pl.multiple_of(places[1 + index * piece.shape[0] + inner], 16)
+                    turned = pl.multiple_of(lax.rem(row + core * HALF, D), 16)
+                    for target, offset, column, width in spans:
+                        source = piece.at[inner, :, pl.ds(column, width)]
+                        if target is wp:
+                            view = wp.at[pl.ds(turned, size), :]
+                        elif target is wfc:
+                            begin = offset[1] if isinstance(offset, tuple) else 0
+                            view = wfc.at[pl.ds(row, size), pl.ds(begin, width)]
+                        else:
+                            view = wout.at[pl.ds(offset + row, size), :]
+                        moves.append((source, view))
+            return [
+                pltpu.make_async_copy(source, view, sems.at[index])
+                for index, (source, view) in enumerate(moves)
+            ]
+
+        def load_all(first_half):
+            loads = loads_of(first_half)
+            for load in loads:
+                load.start()
+            for load in loads:
+                load.wait()
+
         ap[...] = jnp.zeros_like(ap)
         gvec_ref[...] = jnp.zeros_like(gvec_ref)
         gbfc_ref[...] = jnp.zeros_like(gbfc_ref)
@@ -625,8 +679,17 @@
             return carry
 
         lax.fori_loop(0, D // 64, clear, 0)
-        for load in loads:
-            load.wait()
+        if groups == 1:
+            load_all(None)
+        else:
+
+            @pl.when(core == 0)
+            def _():
+                load_all(0)
+
+            @pl.when(core != 0)
+            def _():
+                load_all(1)
 
     b_proj = vec_ref[0:1, :]
     gain = vec_ref[1:2, :]
@@ -706,11 +769,12 @@
                 sends[-2].wait()
             for block in range(blocks):
                 stage[slot, block] = fetch(block).astype(BF)
-            sends.append(
-                pltpu.make_async_copy(
-                    stage.at[slot], grads_hbm.at[:, :, pl.ds(column, D)], sems.at[slot]
-                )
-            )
+            width = grads_hbm.shape[2]
+            if column < width:
+                target = grads_hbm.at[:, :, pl.ds(column, D)]
+            else:
+                target = more_hbm.at[:, :, pl.ds(column - width, D)]
+            sends.append(pltpu.make_async_copy(stage.at[slot], target, sems.at[slot]))
             sends[-1].start()
 
         def first_row(block):
@@ -766,7 +830,7 @@
                 pl.BlockSpec((1, FF), lambda m, i, s, t: (0, 0)),
             ]
             + [whole] * len(pieces),
-            out_specs=[prompts, conts, prompts, conts, heads, heads, fixed, long, whole],
+            out_specs=[prompts, conts, prompts, conts, heads, heads, fixed, long, whole, whole],
             scratch_shapes=[
                 pltpu.VMEM((D, D), BF),
                 pltpu.VMEM((D, FF), BF),
@@ -789,7 +853,8 @@
             shape(mate.shape, BF),
             shape((8, D), F32),
             shape((8, FF), F32),
-            shape((D // share, share, D + 2 * FF), BF),
+            shape((D // share, share, D + FF + FF // 2), BF),
+            shape((D // share, share, FF // 2), BF),
         ),
         compiler_params=pltpu.CompilerParams(
             dimension_semantics=("arbitrary", "arbitrary"), vmem_limit_bytes=63 << 20
@@ -818,48 +883,69 @@
     return lax.axis_size("grp") == 4 and lax.axis_size("fsdp") == 8
 
 
-def square_halves(block):
+def spread_one(block):
     half = block.shape[0] // 2
-    pieces = []
-    for index, (one, two) in enumerate(((1, 2), (2, 1))):
-        piece = block[index * half : (index + 1) * half]
-        both = jnp.stack([piece, neighbour(piece, "grp", one)])
-        far = neighbour(both, "grp", two)
-        pieces.append((both, (0, one), index))
-        pieces.append((far, (two, 3), index))
-    return pieces
-
-
-def gather_parameters(packed, core):
+    pieces = [block[:half], block[half:]]
+    return [
+        jnp.stack([piece, neighbour(piece, "grp", distance)])
+        for piece, distance in zip(pieces, (1, 2))
+    ]
+
+
+def spread_two(boths):
+    return [neighbour(both, "grp", distance) for both, distance in zip(boths, (2, 1))]
+
+
+def spread_pieces(boths, fars):
+    return [
+        (boths[0], (0, 1), 0),
+        (fars[0], (2, 3), 0),
+        (boths[1], (0, 2), 1),
+        (fars[1], (1, 3), 1),
+    ]
+
+
+def gather_zone(packed):
+    if not is_square():
+        return lax.all_gather(packed, ALL, axis=0, tiled=True)
+    groups = [list(range(c, lax.axis_size("fsdp"), 2)) for c in (0, 1)]
+    return lax.all_gather(packed, "fsdp", axis=0, tiled=True, axis_index_groups=groups)
+
+
+def chip_rows(keep, send, core):
+    other = swap(send)
+    return jnp.where(
+        core == 0,
+        jnp.concatenate([keep, other], axis=0),
+        jnp.concatenate([other, keep], axis=0),
+    )
+
+
+def join_front(boths, fars):
     own = lax.axis_index("grp")
-    cut = 3 * D + SMALL_COLS
-    if not is_square():
-        whole = lax.all_gather(packed, ALL, axis=0, tiled=True)
-        heads = lax.dynamic_slice_in_dim(whole[:, : 3 * D], core * HEAD_COLS, HEAD_COLS, 1)
-        front = jnp.concatenate([heads, whole[:, 3 * D : cut]], axis=1)
-        return front, [whole[:, cut:].reshape(2, HALF, -1)], [0, HALF], whole
-    zone = lax.all_gather(packed, "fsdp", axis=0, tiled=True)
-    group_rows = zone.shape[0]
-    heads = lax.dynamic_slice_in_dim(zone[:, : 3 * D], core * HEAD_COLS, HEAD_COLS, 1)
     parts = {}
-    for both, offsets, index in square_halves(
-        jnp.concatenate([heads, zone[:, 3 * D : cut]], axis=1)
-    ):
+    for pair, offsets, index in spread_pieces(boths, fars):
         for which, offset in enumerate(offsets):
-            parts[offset, index] = both[which]
+            parts[offset, index] = pair[which]
     table = jnp.stack([jnp.concatenate([parts[k, 0], parts[k, 1]], axis=0) for k in range(4)])
-    front = jnp.concatenate(
+    return jnp.concatenate(
         [lax.dynamic_index_in_dim(table, own ^ k, 0, keepdims=False) for k in range(4)], axis=0
     )
-    half = group_rows // 2
-    rest = lax.dynamic_slice(zone, (core * half, cut), (half, zone.shape[1] - cut))
+
+
+def join_rest(boths, fars):
+    own = lax.axis_index("grp")
+    size = boths[0].shape[1]
     pieces, rows = [], []
-    for both, offsets, index in square_halves(rest):
-        for source, side in ((both, core), (swap(both), 1 - core)):
-            pieces.append(source)
-            for offset in offsets:
-                rows.append((own ^ offset) * group_rows + side * half + index * (half // 2))
-    return front, pieces, rows, zone
+    for pair, offsets, index in spread_pieces(boths, fars):
+        pieces.append(pair)
+        for offset in offsets:
+            rows.append((own ^ offset) * 2 * size + index * size)
+    return pieces + [swap(piece) for piece in pieces], rows + rows
+
+
+def pin(*values):
+    return list(lax.optimization_barrier(tuple(values)))
 
 
 def pick(array, index, axis):
@@ -919,10 +1005,6 @@
     keep = lax.dynamic_slice_in_dim(value, core * share, share, 0)
     other = swap(lax.dynamic_slice_in_dim(value, (1 - core) * share, share, 0))
     return keep, other
-
-
-def pin(first, second):
-    return lax.optimization_barrier((first, second))
 
 
 def square_steps(core):
@@ -984,17 +1066,57 @@
         [v[:, None] for v in vectors] + [fc_bias.reshape(wide, share).T], axis=1
     )
     columns = jnp.pad(columns, ((0, 0), (0, SMALL_COLS - columns.shape[1])))
-    packed = jnp.concatenate(
+    prompt_all = [lax.all_gather(prompt_in[m], "fsdp", axis=0, tiled=True) for m in range(MB)]
+    square = is_square()
+    columns = columns.astype(BF)
+    heads = attn_weight.astype(BF).reshape(share, 3, 2, HALF)
+    keep = lax.dynamic_index_in_dim(heads, core, 2, keepdims=False).reshape(share, HEAD_COLS)
+    send = lax.dynamic_index_in_dim(heads, 1 - core, 2, keepdims=False).reshape(share, HEAD_COLS)
+    rest = jnp.concatenate(
         [
-            attn_weight.reshape(share, 3, 2, HALF).transpose(0, 2, 1, 3).reshape(share, 3 * D),
-            columns,
             proj_weight,
             fc_weight.reshape(share, devices, wide, share).transpose(0, 2, 1, 3).reshape(share, FF),
             out_weight.reshape(wide, share, D).transpose(1, 0, 2).reshape(share, FF),
         ],
         axis=1,
     ).astype(BF)
-    front, pieces, piece_rows, zone = gather_parameters(packed, core)
+    if square:
+        zone = gather_zone(
+            chip_rows(
+                jnp.concatenate([keep, columns], axis=1),
+                jnp.concatenate([send, columns], axis=1),
+                core,
+            )
+        )
+        half = rest.shape[1] // 2
+        rest = chip_rows(
+            lax.dynamic_slice_in_dim(rest, core * half, half, 1),
+            lax.dynamic_slice_in_dim(rest, (1 - core) * half, half, 1),
+            core,
+        )
+        cut = half // 256 * 128
+        first, zone = pin(rest[:, :cut], zone)
+        zones = [gather_zone(first)]
+        front_boths = spread_one(zone)
+        zones[0], second, *front_boths = pin(zones[0], rest[:, cut:], *front_boths)
+        zones.append(gather_zone(second))
+        front_fars = spread_two(front_boths)
+        zones[1], *front_fars = pin(zones[1], *front_fars)
+        front = join_front(front_boths, front_fars)
+        rest_boths = spread_one(jnp.concatenate(zones, axis=1))
+    else:
+        zone = gather_zone(jnp.concatenate([heads.reshape(share, 3 * D), columns], axis=1))
+        front = jnp.concatenate(
+            [
+                lax.dynamic_index_in_dim(
+                    zone[:, : 3 * D].reshape(D, 3, 2, HALF), core, 2, keepdims=False
+                ).reshape(D, HEAD_COLS),
+                zone[:, 3 * D :],
+            ],
+            axis=1,
+        )
+        pieces = [gather_zone(rest).reshape(2, HALF, -1)]
+        piece_rows = [0, HALF]
     w_heads = front[:, :HEAD_COLS]
     small = front[:, HEAD_COLS:].astype(F32)
     gain_a, shift_a, bias_q, bias_v, b_proj, gain_b, shift_b, b_out = (small[:, i] for i in range(8))
@@ -1008,12 +1130,36 @@
     )
     vec_b = jnp.pad(jnp.stack([b_proj, gain_b, shift_b, b_out]), ((0, 4), (0, 0)))
 
-    prompt_all = [lax.all_gather(prompt_in[m], "fsdp", axis=0, tiled=True) for m in range(MB)]
     cont_mate = swap(cont_in)
     plan_mate = swap(cont_prompt[:, 0, :].astype(F32)).astype(jnp.int32)
 
-    own_row = place * prow
-    mate_row = (place + 1 - 2 * core) * prow
+    def balanced(index):
+        ends = fsdp // NPR
+        other = index // ends * ends + ends - 1 - (index % ends - index % 2)
+        return index + (index % 2) * (other - index)
+
+    own_place = balanced(place)
+    mate_place = balanced(place + 1 - 2 * core)
+    own_row = own_place * prow
+    mate_row = mate_place * prow
+    own_pairs = [(i, balanced(i)) for i in range(fsdp)]
+    mate_pairs = [(i, balanced(i ^ 1)) for i in range(fsdp)]
+
+    def send_home(own, other):
+        return (
+            jnp.concatenate([lax.ppermute(own[:prow], "fsdp", own_pairs), own[prow:]], axis=0),
+            jnp.concatenate(
+                [lax.ppermute(other[:prow], "fsdp", mate_pairs), swap(other[prow:])], axis=0
+            ),
+        )
+
+    def send_back(own, other):
+        return [
+            lax.ppermute(own[:prow], "fsdp", [(b, a) for a, b in own_pairs]),
+            own[prow:],
+            lax.ppermute(other[:prow], "fsdp", [(b, a) for a, b in mate_pairs]),
+            swap(other[prow:]),
+        ]
 
     def prompt_plan(row):
         row = row + TQ * jnp.arange(prow // TQ)
@@ -1056,27 +1202,22 @@
             axis=0,
         ).astype(jnp.int32)
 
-    tiles = (prompt_rows + 2 * crow) // TQ
-    index = jnp.arange(tiles)
-    part, cpart = prow // TQ, crow // TQ
-    own_tile, mate_tile, cont_tile = own_row // TQ, mate_row // TQ, prompt_rows // TQ
-    is_own = (index >= own_tile) & (index < own_tile + part)
-    is_mate = (index >= mate_tile) & (index < mate_tile + part)
-    is_cont = index >= cont_tile
-    has = (is_own | is_mate | is_cont).astype(jnp.int32)
-    order_own = index - own_tile
-    order_mate = index - mate_tile + part + cpart
-    order_cont = index - cont_tile
-    order_cont = jnp.where(order_cont < cpart, part + order_cont, 2 * part + order_cont)
-    exact = jnp.where(is_cont, order_cont, jnp.where(is_own, order_own, order_mate))
-    first_tile = jnp.minimum(own_tile, mate_tile)
-    clipped = jnp.clip(index, first_tile, first_tile + 2 * part - 1)
-    early_spot = jnp.where(
-        (clipped >= own_tile) & (clipped < own_tile + part),
-        clipped - own_tile,
-        clipped - mate_tile + part + cpart,
-    )
-    spot = jnp.where(is_cont, exact, early_spot).astype(jnp.int32)
+    blocks = []
+    for kind, count in (("own", prow), ("cont", crow), ("mate", prow), ("other", crow)):
+        for index in range(count // TQ):
+            prompt = (mate_row if kind in ("mate", "other") else own_row) // TQ
+            last = prow // TQ - 1
+            if kind in ("own", "mate"):
+                blocks.append((0, prompt + index, 0 if kind == "own" else crow // TQ - 1))
+            else:
+                first = 0 if kind == "cont" else crow // TQ
+                blocks.append((1, prompt + last, first + index))
+    spot = jnp.stack(
+        [
+            jnp.stack([jnp.asarray(value, jnp.int32) for value in entry + (own_place, mate_place)])
+            for entry in blocks
+        ]
+    ).astype(jnp.int32)
 
     saved = []
     outs_mine = []
@@ -1085,15 +1226,23 @@
         x_prompt = prompt_all[m]
         if m > 0:
             x_prompt, saved[-1][-1] = pin(x_prompt, saved[-1][-1])
+        if square and m == 1:
+            x_prompt, *rest_boths = pin(x_prompt, *rest_boths)
+            rest_fars = spread_two(rest_boths)
         x_cont = jnp.concatenate([cont_in[m], cont_mate[m]], axis=0)
-        kvp, kvc, query = project(has, spot, x_prompt, x_cont, w_heads, vec_a, 2 * mine, TQ)
         plan = plan_of(m)
-        o, lse = attend_forward(plan, query, kvp, kvc, TQ)
-        outs_mine.append(o[:mine])
-        outs_mate.append(swap(o[mine:]))
-        saved.append([x_prompt, x_cont, kvp, kvc, query, plan, o, lse])
-
-    groups, block_share = (4, share) if is_square() else (1, 8)
+        o, lse, query, kv = attend_forward(plan, spot, x_prompt, x_cont, w_heads, vec_a, TQ, prow)
+        if square and m == 1:
+            lse, *rest_fars = pin(lse, *rest_fars)
+        own, other = send_home(o[:mine], o[mine:])
+        outs_mine.append(own)
+        outs_mate.append(other)
+        saved.append([x_prompt, x_cont, kv, query, plan, o, lse])
+
+    if square:
+        pieces, piece_rows = join_rest(rest_boths, rest_fars)
+
+    groups, block_share = (4, share) if square else (1, 8)
     places = jnp.stack([core] + [jnp.asarray(row, jnp.int32) for row in piece_rows]).astype(jnp.int32)
     (
         prompt_out,
@@ -1105,6 +1254,7 @@
         g_vec,
         g_fc_bias,
         g_rest,
+        g_more,
     ) = feed_forward(
         cont_len[:, 0, :],
         places,
@@ -1120,47 +1270,44 @@
         groups,
         block_share,
     )
-    d_back = swap(d_mate)
-    moves = []
-    if is_square():
-        g_rest = lax.psum_scatter(g_rest, "fsdp", scatter_dimension=0, tiled=True)
-        moves = square_steps(core)
-    else:
-        g_rest = lax.psum_scatter(g_rest.reshape(D, D + 2 * FF), ALL, scatter_dimension=0, tiled=True)
-    early = [g_rest]
-
-    def advance(held):
-        if moves:
-            early[0] = moves.pop(0)(early[0])
-            held, early[0] = pin(held, early[0])
-        return held
+    returned = [send_back(d_mine[m], d_mate[m]) for m in range(MB)]
+    g_rest, g_more, *returned[0] = pin(g_rest, g_more, *returned[0])
+
+    def along_fsdp(value):
+        if square:
+            return lax.psum_scatter(value, "fsdp", scatter_dimension=0, tiled=True)
+        value = value.reshape(D, value.shape[2])
+        return lax.psum_scatter(value, ALL, scatter_dimension=0, tiled=True)
+
+    g_rest, g_more = along_fsdp(g_rest), along_fsdp(g_more)
 
     totals = None
     tables = []
     conts_back = []
     for m in range(MB):
-        x_prompt, x_cont, kvp, kvc, query, plan, o, lse = saved[m]
-        do = jnp.concatenate([d_mine[m], d_back[m]], axis=0)
+        x_prompt, x_cont, kv, query, plan, o, lse = saved[m]
         if m > 0:
-            do, tables[-1] = pin(do, tables[-1])
+            tables[-1], *returned[m] = pin(tables[-1], *returned[m])
             tables[-1] = lax.psum_scatter(tables[-1], "fsdp", scatter_dimension=0, tiled=True)
         if m > 1:
-            do, tables[m - 2] = pin(do, tables[m - 2])
-        dq, dkvp, dkvc = attend_backward(plan, query, do, o, lse, kvp, kvc, TQ)
-        if m > 0:
-            dkvp = advance(dkvp)
-        table, table_cont, *totals = unproject(
-            has, spot, x_prompt, x_cont, dkvp, dkvc, dq, w_heads, vec_a, totals, TQ
+            g_more, *returned[m] = pin(g_more, *returned[m])
+        if m == 1:
+            g_rest, *returned[m] = pin(g_rest, *returned[m])
+        do = jnp.concatenate(returned[m], axis=0)
+        table, table_cont, *totals = attend_backward(
+            plan, spot, x_prompt, x_cont, kv, query, do, o, lse, w_heads, vec_a, totals, TQ, prow
         )
         tables.append(table)
         conts_back.append(
             table_cont[:crow].astype(F32) + swap(table_cont[crow:]).astype(F32)
         )
     if MB > 1:
-        tables[-1], tables[-2] = pin(tables[-1], tables[-2])
+        *tables, conts_back[-1] = pin(*tables, conts_back[-1])
     tables[-1] = lax.psum_scatter(tables[-1], "fsdp", scatter_dimension=0, tiled=True)
-    while moves:
-        early[0] = moves.pop(0)(early[0])
+    early = jnp.concatenate([g_rest, g_more], axis=-1)
+    for step in square_steps(core) if square else ():
+        early = step(early)
+    *totals, conts_back[-1] = pin(*totals, conts_back[-1])
     g_heads, g_first, g_bias = totals
 
     def spread(value):
@@ -1196,7 +1343,7 @@
 
     late = jnp.stack(by_core(late_own[:, :HEAD_COLS], late_other[:, :HEAD_COLS]), axis=1)
     late = late.reshape(share, 2, 3, HALF).transpose(0, 2, 1, 3).reshape(share, 3 * D)
-    early = early[0].astype(F32)
+    early = early.astype(F32)
     g_fc = early[:, D : D + FF].reshape(share, wide, devices, share)
     g_fc = g_fc.transpose(0, 2, 1, 3).reshape(share, FF)
     g_out = early[:, D + FF :].reshape(share, wide, D).transpose(1, 0, 2).reshape(share * wide, D)

time: 903 us -> 847 us (0.938)
  waiting for transfers between devices: 166 us -> 52.1 us
  blocking collectives: 0 us -> 72.6 us
  Pallas kernels: 487 us -> 524 us
  local copies, waits for them, and re-layouts: 100 us -> 65.9 us
  starting transfers between devices: 70.5 us -> 49 us
    all_gather x0 -> x3, blocking collectives: none -> 72.6 us  [gather_zone(): lax.all_gather(packed, 'fsdp', axis=0, tiled=True, axis_index_groups=groups)]
    pallas_call x3, Pallas kernels: 86.5 us -> 154 us  [attend_forward(): pl.pallas_call(attend_forward_kernel, grid_spec=pltpu.PrefetchScalarGridS...]
    all_gather x3, waiting for transfers between devices: 51.5 us -> 0.02 us  [body(): lax.all_gather(prompt_in[m], 'fsdp', axis=0, tiled=True)]
    ppermute x32 -> x36, starting transfers between devices: 70.2 us -> 28.4 us  [neighbour(): return lax.ppermute(value, axis, pairs)]
    unnamed x240 -> x182, local copies, waits for them, and re-layouts: 48.3 us -> 8.52 us
    pallas_call x9 -> x3, Pallas kernels: 293 us -> 260 us  [attend_backward(): pl.pallas_call(functools.partial(attend_backward_kernel, totals is not No...]
    all_gather x1 -> x0, waiting for transfers between devices: 31.5 us -> none  [gather_parameters(): zone = lax.all_gather(packed, 'fsdp', axis=0, tiled=True)]
    ppermute x32 -> x36, waiting for transfers between devices: 60.3 us -> 40.4 us  [neighbour(): return lax.ppermute(value, axis, pairs)]
  transfers between devices with their start and end apart: 40 -> 56, of which waited for: 17 -> 12; matrix products, arithmetic and copies ran while one was open for 9% -> 12% of each run, Pallas kernels for 42% -> 49%
where the time goes in v3:
time: 847 us; the launch traced here: 837 us
  Pallas kernels  524 us (62%)
  blocking collectives  72.6 us (9%)
  local copies, waits for them, and re-layouts  65.9 us (8%)
  other arithmetic  53 us (6%)
  waiting for transfers between devices  52.1 us (6%)
  starting transfers between devices  49 us (6%)
  between operations  20.2 us (2%)
    pallas_call x3, Pallas kernels, attend_backward(): pl.pallas_call(functools.partial(attend_backward_kernel, totals is not No...  260 us
    pallas_call x3, Pallas kernels, attend_forward(): pl.pallas_call(attend_forward_kernel, grid_spec=pltpu.PrefetchScalarGridS...  154 us
    pallas_call x1, Pallas kernels, feed_forward(): pl.pallas_call(functools.partial(feed_forward_kernel, prompt_parts, clen,...  110 us
    all_gather x3, blocking collectives, gather_zone(): lax.all_gather(packed, 'fsdp', axis=0, tiled=True, axis_index_groups=groups)  72.6 us
    ppermute x36, waiting for transfers between devices, neighbour(): return lax.ppermute(value, axis, pairs)  40.4 us
    ppermute x36, starting transfers between devices, neighbour(): return lax.ppermute(value, axis, pairs)  28.4 us
  transfers between devices with their start and end apart: 56, of which 12 were waited for; matrix products, arithmetic and copies ran while one was open for 12% of the time, Pallas kernels for 49%

profile of v3, /device:TPU:0, one launch (start us, length us, event | category | flops | bytes accessed | tf_op | source)
XLA Modules:
  0.0 836.8 jit_solution(11273952387397845982)
XLA Ops:
  7.2 3.1 fusion.95
  27.9 23.5 %all_gather.19 = bf16[192,1280]{1,0:T(8,128)(2,1)S(1)} all-gather(bf16[48,1280]{1,0:T(8,128)(2,1)S(1)} %maximum_select_fusion.1), channel_id=1, replica_groups={{0,2,4,6},{1,3,5,7},{8,10,12,14},{9,11,13,15},{16,18,20,22},{17,19,21,2..., dimensions={0}, use_global_device_ids=true | all-gather | bytes 614400 | tf_op jit(solution)/shard_map/all_gather | solution.py:912
  51.6 1.6 collective-permute-start.5
  55.2 25.0 %all_gather.20 = bf16[192,1664]{1,0:T(8,128)(2,1)S(1)} all-gather(bf16[48,1664]{1,0:T(8,128)(2,1)S(1)} %slice.527), channel_id=1, replica_groups={{0,2,4,6},{1,3,5,7},{8,10,12,14},{9,11,13,15},{16,18,20,22},{17,19,21,2..., dimensions={0}, use_global_device_ids=true | all-gather | bytes 798720 | tf_op jit(solution)/shard_map/all_gather | solution.py:912
  81.6 24.1 %all_gather.21 = bf16[192,1792]{1,0:T(8,128)(2,1)S(1)} all-gather(bf16[48,1792]{1,0:T(8,128)(2,1)S(1)} %slice-done), channel_id=1, replica_groups={{0,2,4,6},{1,3,5,7},{8,10,12,14},{9,11,13,15},{16,18,20,22},{17,19,21,2..., dimensions={0}, use_global_device_ids=true | all-gather | bytes 860160 | tf_op jit(solution)/shard_map/all_gather | solution.py:912
  114.7 1.7 slice_bitcast_fusion.1
  118.7 3.7 collective-permute-done.10
  122.4 2.3 pad_maximum_fusion.7.refs_2_
  125.6 2.4 pad_maximum_fusion.6.refs_0_
  128.0 51.6 %attend_forward.3 = (bf16[1536,384]{1,0:T(8,128)(2,1)}, f32[6,8,256]{2,1,0:T(8,128)}, bf16[1536,384]{1,0:T(8,128)(2,1)}, bf16[4608,768]{1,0:T(8,128)(2,1)}) custom-call(s32[6,5]{1,0:T(8,128)} %get-tuple-element.394.info, s32[6,5]{1,0:T(8,128)} %stack.355.spot, bf16[4096,768]{1,0:T(8,128)(2,1)} %bitcast.415, ...), custom_call_target="tpu_custom_call" | custom-call | flops 24763170816 | bytes 20971520 | tf_op jit(solution)/shard_map/attend_forward/pallas_call | solution.py:244
  181.8 51.0 %attend_forward.4 = (bf16[1536,384]{1,0:T(8,128)(2,1)}, f32[6,8,256]{2,1,0:T(8,128)}, bf16[1536,384]{1,0:T(8,128)(2,1)}, bf16[4608,768]{1,0:T(8,128)(2,1)}) custom-call(s32[6,5]{1,0:T(8,128)} %get-tuple-element.395.info, s32[6,5]{1,0:T(8,128)} %stack.355.spot, bf16[4096,768]{1,0:T(8,128)(2,1)} %bitcast.411, ...), custom_call_target="tpu_custom_call" | custom-call | flops 24763170816 | bytes 20971520 | tf_op jit(solution)/shard_map/attend_forward/pallas_call | solution.py:244
  232.9 2.2 fusion.100
  235.1 1.8 fusion.101
  239.8 4.5 collective-permute-start.8
  244.3 51.1 %attend_forward.5 = (bf16[1536,384]{1,0:T(8,128)(2,1)}, f32[6,8,256]{2,1,0:T(8,128)}, bf16[1536,384]{1,0:T(8,128)(2,1)}, bf16[4608,768]{1,0:T(8,128)(2,1)}) custom-call(s32[6,5]{1,0:T(8,128)} %fusion.88.info, s32[6,5]{1,0:T(8,128)} %stack.355.spot, bf16[4096,768]{1,0:T(8,128)(2,1)} %bitcast.407, bf16[512,768]{1,0:T(8,128)(2,1)} %get-tuple-element.415.xc_hbm.xqc_ref, ...), custom_call_target="tpu_custom_call" | custom-call | flops 24763170816 | bytes 20971520 | tf_op jit(solution)/shard_map/attend_forward/pallas_call | solution.py:244
  296.1 1.7 fusion.103
  298.1 2.1 fusion.102
  307.6 1.8 collective-permute-start.14
  315.8 109.7 %feed_forward.1 = (bf16[3,512,768]{2,1,0:T(8,128)(2,1)}, bf16[3,256,768]{2,1,0:T(8,128)(2,1)}, bf16[3,512,768]{2,1,0:T(8,128)(2,1)}, bf16[3,256,768]{2,1,0:T(8,1...) custom-call(s32[3,1]{1,0:T(4,128)} %copy.200.lens, ...), custom_call_target="tpu_custom_call" | custom-call | flops 73383542784 | bytes 52428800 | tf_op jit(solution)/shard_map/feed_forward/pallas_call | solution.py:817
  425.5 2.2 slice_bitcast_fusion.5
  429.4 7.0 collective-permute-start.26
  437.1 1.9 slice_bitcast_fusion.22
  439.0 6.3 collective-permute-done.26
  449.1 87.2 %attend_backward.3 = (bf16[4096,768]{1,0:T(8,128)(2,1)}, bf16[512,768]{1,0:T(8,128)(2,1)}, f32[768,1152]{1,0:T(8,128)}, f32[8,768]{1,0:T(8,128)}, f32[8,1152]{1,0:T(8,128)}) custom-call(s32[6,5]{1,0:T(8,128)} %get-tuple-element.394.info, s32[6,5]{1,0:T(8,128)} %stack.355.spot, bf16[4096,768]{1,0:T(8,128)(2,1)} %bitcast.417, ...), custom_call_target="tpu_custom_call" | custom-call | flops 59190018048 | bytes 31457280 | tf_op jit(solution)/shard_map/attend_backward/pallas_call | solution.py:520
  542.4 1.7 collective-permute-start.31
  544.7 2.4 pad_maximum_fusion.10.do_ref
  547.1 86.5 %attend_backward.4 = (bf16[4096,768]{1,0:T(8,128)(2,1)}, bf16[512,768]{1,0:T(8,128)(2,1)}, f32[768,1152]{1,0:T(8,128)}, f32[8,768]{1,0:T(8,128)}, f32[8,1152]{1,0:T(8,128)}) custom-call(s32[6,5]{1,0:T(8,128)} %get-tuple-element.395.info, s32[6,5]{1,0:T(8,128)} %stack.355.spot, bf16[4096,768]{1,0:T(8,128)(2,1)} %bitcast.413, ...), custom_call_target="tpu_custom_call" | custom-call | flops 59190018048 | bytes 31457280 | tf_op jit(solution)/shard_map/attend_backward/pallas_call | solution.py:520
  648.9 2.0 pad_maximum_fusion.11.do_ref
  651.0 86.7 %attend_backward.5 = (bf16[4096,768]{1,0:T(8,128)(2,1)}, bf16[512,768]{1,0:T(8,128)(2,1)}, f32[768,1152]{1,0:T(8,128)}, f32[8,768]{1,0:T(8,128)}, f32[8,1152]{1,0:T(8,128)}) custom-call(s32[6,5]{1,0:T(8,128)} %fusion.88.info, s32[6,5]{1,0:T(8,128)} %stack.355.spot, bf16[4096,768]{1,0:T(8,128)(2,1)} %bitcast.409, ...), custom_call_target="tpu_custom_call" | custom-call | flops 59190018048 | bytes 31457280 | tf_op jit(solution)/shard_map/attend_backward/pallas_call | solution.py:520
  738.9 1.8 slice.495
  742.9 1.8 fusion.71
  748.6 3.2 collective-permute-done.47
  752.8 2.1 reshape.690
  754.9 2.4 copy.207
  757.4 4.0 reshape.691
  765.0 2.3 convert_element_type.316
  769.1 1.6 collective-permute-start.39
  770.8 2.2 fusion.73
  773.1 1.7 fusion.80
  774.8 5.2 collective-permute-done.37
  783.1 3.3 collective-permute-done.38
  786.4 1.6 collective-permute-done.40
  789.6 11.9 %collective-permute-done.41 = bf16[2,48,1280]{2,1,0:T(8,128)(2,1)S(1)} collective-permute-done((bf16[2,48,1280]{2,1,0:T(8,128)(2,1)S(1)}, bf16[2,48,1280]{2,1,0:T(8,128)(2,1)S(1)}, u32[]{:S(2)}, u32[]{:S(2)}) %collective-permute-start.41) | collective-permute-done | bytes 245792 | tf_op jit(solution)/shard_map/ppermute | solution.py:875
  801.5 2.1 collective-permute-start.42
  805.0 9.0 %collective-permute-done.42 = bf16[48,1280]{1,0:T(8,128)(2,1)S(1)} collective-permute-done((bf16[48,1280]{1,0:T(8,128)(2,1)S(1)}, bf16[48,1280]{1,0:T(8,128)(2,1)S(1)}, u32[]{:S(2)}, u32[]{:S(2)}) %collective-permute-start.42) | collective-permute-done | bytes 122912 | tf_op jit(solution)/shard_map/ppermute | solution.py:875
  818.9 3.2 reduce-scatter.14.cloned.1.call-done
  822.1 3.1 fusion.5
  828.1 1.7 pad_maximum_fusion
  (495 shorter events, 103.7 us)
Async XLA Ops:
  7.2 120.8 %all-gather.7.cloned.1.call-start = ((), (), s32[]{:S(2)}) async-start(), calls=%async_computation.10 | async-start | bytes 7077888 | tf_op jit(solution)/shard_map/all_gather | solution.py:1069
  10.3 169.3 %all-gather.9.cloned.1.call-start = ((), (), s32[]{:S(2)}) async-start(), calls=%async_computation.11 | async-start | bytes 7077888 | tf_op jit(solution)/shard_map/all_gather | solution.py:1069
  11.1 233.2 %all-gather.11.cloned.1.call-start = ((), (), s32[]{:S(2)}) async-start(), calls=%async_computation.12 | async-start | bytes 7077888 | tf_op jit(solution)/shard_map/all_gather | solution.py:1069
  14.3 37.1 %collective-permute-start.2 = (bf16[24,3456]{1,0:T(8,128)(2,1)S(1)}, bf16[24,3456]{1,0:T(8,128)(2,1)S(1)}, u32[]{:S(2)}, u32[]{:S(2)}) collective-permute-start(bf16[24,3456]{1,0:T(8,128)(2,1)S(1)} %get-tuple-element.387), channel_id=1, source_target_pairs={{0,1},{1,0},{2,3},{3,2},{4,5},{5,4},{6,7},{7,6},{8,9},{9,8},{10,11... | collective-permute-start | bytes 497672 | tf_op jit(solution)/shard_map/ppermute | solution.py:875
  16.9 11.0 %collective-permute-start.3 = (bf16[24,1280]{1,0:T(8,128)(2,1)S(1)}, bf16[24,1280]{1,0:T(8,128)(2,1)S(1)}, u32[]{:S(2)}, u32[]{:S(2)}) collective-permute-start(bf16[24,1280]{1,0:T(8,128)(2,1)S(1)} %pad_maximum_fusion.21), channel_id=1, source_target_pairs={{0,1},{1,0},{2,3},{3,2},{4,5},{5,4},{6,7},{7,6},{8,9},{9,8},{10,11... | collective-permute-start | bytes 184328 | tf_op jit(solution)/shard_map/ppermute | solution.py:875
  17.1 7.4 collective-permute-start
  17.5 97.1 %collective-permute-start.1 = (bf16[3,256,768]{2,1,0:T(8,128)(2,1)S(1)}, bf16[3,256,768]{2,1,0:T(8,128)(2,1)}, u32[]{:S(2)}, u32[]{:S(2)}) collective-permute-start(bf16[3,256,768]{2,1,0:T(8,128)(2,1)S(1)} %copy-done.3), channel_id=1, source_target_pairs={{0,1},{1,0},{2,3},{3,2},{4,5},{5,4},{6,7},{7,6},{8,9},{9,8},{10,11... | collective-permute-start | bytes 3538952 | tf_op jit(solution)/shard_map/ppermute | solution.py:875
  17.6 527.0 %reduce-scatter.8.cloned.1.call-start = ((), (), s32[]{:S(2)}) async-start(), calls=%async_computation.6 | async-start | bytes 9289728 | tf_op jit(solution)/shard_map/reduce_scatter | solution.py:1278
  51.6 28.7 %collective-permute-start.5 = (bf16[96,1280]{1,0:T(8,128)(2,1)S(1)}, bf16[96,1280]{1,0:T(8,128)(2,1)S(1)}, u32[]{:S(2)}, u32[]{:S(2)}) collective-permute-start(bf16[96,1280]{1,0:T(8,128)(2,1)S(1)} %get-tuple-element.374), channel_id=1, source_target_pairs={{0,16},{8,24},{16,0},{24,8},{1,17},{9,25},{17,1},{25,9},{2,18},{10... | collective-permute-start | bytes 737288 | tf_op jit(solution)/shard_map/ppermute | solution.py:875
  53.7 26.5 %collective-permute-start.4 = (bf16[96,1280]{1,0:T(8,128)(2,1)S(1)}, bf16[96,1280]{1,0:T(8,128)(2,1)S(1)}, u32[]{:S(2)}, u32[]{:S(2)}) collective-permute-start(bf16[96,1280]{1,0:T(8,128)(2,1)S(1)} %get-tuple-element.375), channel_id=1, source_target_pairs={{0,8},{8,0},{16,24},{24,16},{1,9},{9,1},{17,25},{25,17},{2,10},{10... | collective-permute-start | bytes 737288 | tf_op jit(solution)/shard_map/ppermute | solution.py:875
  80.4 25.5 %collective-permute-start.6 = (bf16[2,96,1280]{2,1,0:T(8,128)(2,1)S(1)}, bf16[2,96,1280]{2,1,0:T(8,128)(2,1)S(1)}, u32[]{:S(2)}, u32[]{:S(2)}) collective-permute-start(bf16[2,96,1280]{2,1,0:T(8,128)(2,1)S(1)} %pad_maximum_fusion.16), channel_id=1, source_target_pairs={{0,16},{8,24},{16,0},{24,8},{1,17},{9,25},{17,1},{25,9},{2,18},{10... | collective-permute-start | bytes 1474568 | tf_op jit(solution)/shard_map/ppermute | solution.py:875
  81.0 24.8 %collective-permute-start.7 = (bf16[2,96,1280]{2,1,0:T(8,128)(2,1)S(1)}, bf16[2,96,1280]{2,1,0:T(8,128)(2,1)S(1)}, u32[]{:S(2)}, u32[]{:S(2)}) collective-permute-start(bf16[2,96,1280]{2,1,0:T(8,128)(2,1)S(1)} %pad_maximum_fusion.17), channel_id=1, source_target_pairs={{0,8},{8,0},{16,24},{24,16},{1,9},{9,1},{17,25},{25,17},{2,10},{10... | collective-permute-start | bytes 1474568 | tf_op jit(solution)/shard_map/ppermute | solution.py:875
  107.2 15.2 %collective-permute-start.10 = (bf16[96,3456]{1,0:T(8,128)(2,1)}, bf16[96,3456]{1,0:T(8,128)(2,1)}, u32[]{:S(2)}, u32[]{:S(2)}) collective-permute-start(bf16[96,3456]{1,0:T(8,128)(2,1)} %get-tuple-element.344), channel_id=1, source_target_pairs={{0,16},{8,24},{16,0},{24,8},{1,17},{9,25},{17,1},{25,9},{2,18},{10... | collective-permute-start | bytes 1990664 | tf_op jit(solution)/shard_map/ppermute | solution.py:875
  110.8 14.8 %collective-permute-start.9 = (bf16[96,3456]{1,0:T(8,128)(2,1)}, bf16[96,3456]{1,0:T(8,128)(2,1)}, u32[]{:S(2)}, u32[]{:S(2)}) collective-permute-start(bf16[96,3456]{1,0:T(8,128)(2,1)} %get-tuple-element.345), channel_id=1, source_target_pairs={{0,8},{8,0},{16,24},{24,16},{1,9},{9,1},{17,25},{25,17},{2,10},{10... | collective-permute-start | bytes 1990664 | tf_op jit(solution)/shard_map/ppermute | solution.py:875
  179.6 59.7 %collective-permute-start.12 = (bf16[2,96,3456]{2,1,0:T(8,128)(2,1)S(1)}, bf16[2,96,3456]{2,1,0:T(8,128)(2,1)}, u32[]{:S(2)}, u32[]{:S(2)}) collective-permute-start(bf16[2,96,3456]{2,1,0:T(8,128)(2,1)S(1)} %copy-done.24), channel_id=1, source_target_pairs={{0,16},{8,24},{16,0},{24,8},{1,17},{9,25},{17,1},{25,9},{2,18},{10... | collective-permute-start | bytes 3981320 | tf_op jit(solution)/shard_map/ppermute | solution.py:875
  180.6 59.2 %collective-permute-start.13 = (bf16[2,96,3456]{2,1,0:T(8,128)(2,1)S(1)}, bf16[2,96,3456]{2,1,0:T(8,128)(2,1)}, u32[]{:S(2)}, u32[]{:S(2)}) collective-permute-start(bf16[2,96,3456]{2,1,0:T(8,128)(2,1)S(1)} %copy-done.23), channel_id=1, source_target_pairs={{0,8},{8,0},{16,24},{24,16},{1,9},{9,1},{17,25},{25,17},{2,10},{10... | collective-permute-start | bytes 3981320 | tf_op jit(solution)/shard_map/ppermute | solution.py:875
  235.1 65.1 %collective-permute-start.17 = (bf16[512,384]{1,0:T(8,128)(2,1)}, bf16[512,384]{1,0:T(8,128)(2,1)S(1)}, u32[]{:S(2)}, u32[]{:S(2)}) collective-permute-start(bf16[512,384]{1,0:T(8,128)(2,1)} %get-tuple-element.350), channel_id=1, source_target_pairs={{0,3},{1,0},{2,1},{3,2},{4,7},{5,4},{6,5},{7,6},{8,11},{9,8},{10,9... | collective-permute-start | bytes 1179656 | tf_op jit(solution)/shard_map/ppermute | solution.py:1152
  236.9 58.5 %collective-permute-start.18 = (bf16[256,384]{1,0:T(8,128)(2,1)}, bf16[256,384]{1,0:T(8,128)(2,1)}, u32[]{:S(2)}, u32[]{:S(2)}) collective-permute-start(bf16[256,384]{1,0:T(8,128)(2,1)} %get-tuple-element.352), channel_id=1, source_target_pairs={{0,1},{1,0},{2,3},{3,2},{4,5},{5,4},{6,7},{7,6},{8,9},{9,8},{10,11... | collective-permute-start | bytes 589832 | tf_op jit(solution)/shard_map/ppermute | solution.py:875
  238.4 62.1 %collective-permute-start.15 = (bf16[512,384]{1,0:T(8,128)(2,1)}, bf16[512,384]{1,0:T(8,128)(2,1)}, u32[]{:S(2)}, u32[]{:S(2)}) collective-permute-start(bf16[512,384]{1,0:T(8,128)(2,1)} %get-tuple-element.346), channel_id=1, source_target_pairs={{0,3},{1,0},{2,1},{3,2},{4,7},{5,4},{6,5},{7,6},{8,11},{9,8},{10,9... | collective-permute-start | bytes 1179656 | tf_op jit(solution)/shard_map/ppermute | solution.py:1152
  239.3 58.6 %collective-permute-start.16 = (bf16[256,384]{1,0:T(8,128)(2,1)}, bf16[256,384]{1,0:T(8,128)(2,1)}, u32[]{:S(2)}, u32[]{:S(2)}) collective-permute-start(bf16[256,384]{1,0:T(8,128)(2,1)} %get-tuple-element.348), channel_id=1, source_target_pairs={{0,1},{1,0},{2,3},{3,2},{4,5},{5,4},{6,7},{7,6},{8,9},{9,8},{10,11... | collective-permute-start | bytes 589832 | tf_op jit(solution)/shard_map/ppermute | solution.py:875
  239.8 60.9 %collective-permute-start.8 = (bf16[512,384]{1,0:T(8,128)(2,1)}, bf16[512,384]{1,0:T(8,128)(2,1)}, u32[]{:S(2)}, u32[]{:S(2)}) collective-permute-start(bf16[512,384]{1,0:T(8,128)(2,1)} %get-tuple-element.347), channel_id=1, source_target_pairs={{0,0},{1,3},{2,2},{3,1},{4,4},{5,7},{6,6},{7,5},{8,8},{9,11},{10,1... | collective-permute-start | bytes 1179656 | tf_op jit(solution)/shard_map/ppermute | solution.py:1150
  295.4 6.5 collective-permute-start.11
  300.2 15.7 %collective-permute-start.21 = (bf16[2,96,3456]{2,1,0:T(8,128)(2,1)S(1)}, bf16[2,96,3456]{2,1,0:T(8,128)(2,1)}, u32[]{:S(2)}, u32[]{:S(2)}) collective-permute-start(bf16[2,96,3456]{2,1,0:T(8,128)(2,1)S(1)} %copy-done.24), channel_id=1, source_target_pairs={{0,1},{1,0},{2,3},{3,2},{4,5},{5,4},{6,7},{7,6},{8,9},{9,8},{10,11... | collective-permute-start | bytes 3981320 | tf_op jit(solution)/shard_map/ppermute | solution.py:875
  300.5 15.4 %collective-permute-start.23 = (bf16[2,96,3456]{2,1,0:T(8,128)(2,1)S(1)}, bf16[2,96,3456]{2,1,0:T(8,128)(2,1)}, u32[]{:S(2)}, u32[]{:S(2)}) collective-permute-start(bf16[2,96,3456]{2,1,0:T(8,128)(2,1)S(1)} %copy-done.23), channel_id=1, source_target_pairs={{0,1},{1,0},{2,3},{3,2},{4,5},{5,4},{6,7},{7,6},{8,9},{9,8},{10,11... | collective-permute-start | bytes 3981320 | tf_op jit(solution)/shard_map/ppermute | solution.py:875
  300.7 6.9 collective-permute-start.19
  301.9 13.9 %collective-permute-start.22 = (bf16[2,96,3456]{2,1,0:T(8,128)(2,1)}, bf16[2,96,3456]{2,1,0:T(8,128)(2,1)}, u32[]{:S(2)}, u32[]{:S(2)}) collective-permute-start(bf16[2,96,3456]{2,1,0:T(8,128)(2,1)} %collective-permute-done.12.refs_1_), channel_id=1, source_target_pairs={{0,1},{1,0},{2,3},{3,2},{4,5},{5,4},{6,7},{7,6},{8,9},{9,8},{10,11... | collective-permute-start | bytes 3981320 | tf_op jit(solution)/shard_map/ppermute | solution.py:875
  302.8 13.0 %collective-permute-start.24 = (bf16[2,96,3456]{2,1,0:T(8,128)(2,1)}, bf16[2,96,3456]{2,1,0:T(8,128)(2,1)}, u32[]{:S(2)}, u32[]{:S(2)}) collective-permute-start(bf16[2,96,3456]{2,1,0:T(8,128)(2,1)} %collective-permute-done.13.refs_3_), channel_id=1, source_target_pairs={{0,1},{1,0},{2,3},{3,2},{4,5},{5,4},{6,7},{7,6},{8,9},{9,8},{10,11... | collective-permute-start | bytes 3981320 | tf_op jit(solution)/shard_map/ppermute | solution.py:875
  427.8 11.3 %collective-permute-start.25 = (bf16[512,384]{1,0:T(8,128)(2,1)S(1)}, bf16[512,384]{1,0:T(8,128)(2,1)S(1)}, u32[]{:S(2)}, u32[]{:S(2)}) collective-permute-start(bf16[512,384]{1,0:T(8,128)(2,1)S(1)} %get-tuple-element.339), channel_id=1, source_target_pairs={{0,0},{3,1},{2,2},{1,3},{4,4},{7,5},{6,6},{5,7},{8,8},{11,9},{10,1... | collective-permute-start | bytes 1179656 | tf_op jit(solution)/shard_map/ppermute | solution.py:1158
  429.4 16.0 %collective-permute-start.26 = (bf16[512,384]{1,0:T(8,128)(2,1)S(1)}, bf16[512,384]{1,0:T(8,128)(2,1)S(1)}, u32[]{:S(2)}, u32[]{:S(2)}) collective-permute-start(bf16[512,384]{1,0:T(8,128)(2,1)S(1)} %get-tuple-element.333), channel_id=1, source_target_pairs={{3,0},{0,1},{1,2},{2,3},{7,4},{4,5},{5,6},{6,7},{11,8},{8,9},{9,10... | collective-permute-start | bytes 1179656 | tf_op jit(solution)/shard_map/ppermute | solution.py:1160
  445.4 197.3 %reduce-scatter.12.cloned.1.call-start = ((), (), s32[]{:S(2)}) async-start(), calls=%async_computation.8 | async-start | bytes 2654208 | tf_op jit(solution)/shard_map/reduce_scatter | solution.py:1278
  445.4 90.8 %collective-permute-start.28 = (bf16[512,384]{1,0:T(8,128)(2,1)S(1)}, bf16[512,384]{1,0:T(8,128)(2,1)S(1)}, u32[]{:S(2)}, u32[]{:S(2)}) collective-permute-start(bf16[512,384]{1,0:T(8,128)(2,1)S(1)} %get-tuple-element.338), channel_id=1, source_target_pairs={{0,0},{3,1},{2,2},{1,3},{4,4},{7,5},{6,6},{5,7},{8,8},{11,9},{10,1... | collective-permute-start | bytes 1179656 | tf_op jit(solution)/shard_map/ppermute | solution.py:1158
  446.3 90.0 %collective-permute-start.29 = (bf16[512,384]{1,0:T(8,128)(2,1)S(1)}, bf16[512,384]{1,0:T(8,128)(2,1)S(1)}, u32[]{:S(2)}, u32[]{:S(2)}) collective-permute-start(bf16[512,384]{1,0:T(8,128)(2,1)S(1)} %get-tuple-element.332), channel_id=1, source_target_pairs={{3,0},{0,1},{1,2},{2,3},{7,4},{4,5},{5,6},{6,7},{11,8},{8,9},{9,10... | collective-permute-start | bytes 1179656 | tf_op jit(solution)/shard_map/ppermute | solution.py:1160
  446.9 89.3 %collective-permute-start.30 = (bf16[256,384]{1,0:T(8,128)(2,1)S(1)}, bf16[256,384]{1,0:T(8,128)(2,1)S(1)}, u32[]{:S(2)}, u32[]{:S(2)}) collective-permute-start(bf16[256,384]{1,0:T(8,128)(2,1)S(1)} %get-tuple-element.329), channel_id=1, source_target_pairs={{0,1},{1,0},{2,3},{3,2},{4,5},{5,4},{6,7},{7,6},{8,9},{9,8},{10,11... | collective-permute-start | bytes 589832 | tf_op jit(solution)/shard_map/ppermute | solution.py:875
  447.8 297.0 %reduce-scatter.6.cloned.1.call-start = ((), (), s32[]{:S(2)}) async-start(), calls=%async_computation.5 | async-start | bytes 7077888 | tf_op jit(solution)/shard_map/reduce_scatter | solution.py:1291
  537.2 207.6 %reduce-scatter.10.cloned.1.call-start = ((), (), s32[]{:S(2)}) async-start(), calls=%async_computation.7 | async-start | bytes 7077888 | tf_op jit(solution)/shard_map/reduce_scatter | solution.py:1291
  542.4 91.3 %collective-permute-start.31 = (bf16[512,384]{1,0:T(8,128)(2,1)}, bf16[512,384]{1,0:T(8,128)(2,1)S(1)}, u32[]{:S(2)}, u32[]{:S(2)}) collective-permute-start(bf16[512,384]{1,0:T(8,128)(2,1)} %get-tuple-element.337), channel_id=1, source_target_pairs={{0,0},{3,1},{2,2},{1,3},{4,4},{7,5},{6,6},{5,7},{8,8},{11,9},{10,1... | collective-permute-start | bytes 1179656 | tf_op jit(solution)/shard_map/ppermute | solution.py:1158
  544.0 89.7 %collective-permute-start.32 = (bf16[512,384]{1,0:T(8,128)(2,1)}, bf16[512,384]{1,0:T(8,128)(2,1)S(1)}, u32[]{:S(2)}, u32[]{:S(2)}) collective-permute-start(bf16[512,384]{1,0:T(8,128)(2,1)} %get-tuple-element.331), channel_id=1, source_target_pairs={{3,0},{0,1},{1,2},{2,3},{7,4},{4,5},{5,6},{6,7},{11,8},{8,9},{9,10... | collective-permute-start | bytes 1179656 | tf_op jit(solution)/shard_map/ppermute | solution.py:1160
  544.6 89.0 %collective-permute-start.33 = (bf16[256,384]{1,0:T(8,128)(2,1)}, bf16[256,384]{1,0:T(8,128)(2,1)}, u32[]{:S(2)}, u32[]{:S(2)}) collective-permute-start(bf16[256,384]{1,0:T(8,128)(2,1)} %get-tuple-element.328), channel_id=1, source_target_pairs={{0,1},{1,0},{2,3},{3,2},{4,5},{5,4},{6,7},{7,6},{8,9},{9,8},{10,11... | collective-permute-start | bytes 589832 | tf_op jit(solution)/shard_map/ppermute | solution.py:875
  634.6 187.5 %reduce-scatter.14.cloned.1.call-start = ((), (), s32[]{:S(2)}) async-start(), calls=%async_computation.9 | async-start | bytes 7077888 | tf_op jit(solution)/shard_map/reduce_scatter | solution.py:1306
  642.2 128.5 %collective-permute-start.35 = (bf16[256,768]{1,0:T(8,128)(2,1)}, bf16[256,768]{1,0:T(8,128)(2,1)}, u32[]{:S(2)}, u32[]{:S(2)}) collective-permute-start(bf16[256,768]{1,0:T(8,128)(2,1)} %slice.492), channel_id=1, source_target_pairs={{0,1},{1,0},{2,3},{3,2},{4,5},{5,4},{6,7},{7,6},{8,9},{9,8},{10,11... | collective-permute-start | bytes 1179656 | tf_op jit(solution)/shard_map/ppermute | solution.py:875
  645.8 95.4 %collective-permute-start.44 = (bf16[2,24,3456]{2,1,0:T(8,128)(2,1)}, bf16[2,24,3456]{2,1,0:T(8,128)(2,1)}, u32[]{:S(2)}, u32[]{:S(2)}) collective-permute-start(bf16[2,24,3456]{2,1,0:T(8,128)(2,1)} %dynamic-slice_bitcast_fusion.7), channel_id=1, source_target_pairs={{0,8},{8,0},{16,24},{24,16},{1,9},{9,1},{17,25},{25,17},{2,10},{10... | collective-permute-start | bytes 995336 | tf_op jit(solution)/shard_map/ppermute | solution.py:875
  647.5 95.4 %collective-permute-start.46 = (bf16[2,24,3456]{2,1,0:T(8,128)(2,1)}, bf16[2,24,3456]{2,1,0:T(8,128)(2,1)}, u32[]{:S(2)}, u32[]{:S(2)}) collective-permute-start(bf16[2,24,3456]{2,1,0:T(8,128)(2,1)} %dynamic-slice_bitcast_fusion.6), channel_id=1, source_target_pairs={{0,16},{8,24},{16,0},{24,8},{1,17},{9,25},{17,1},{25,9},{2,18},{10... | collective-permute-start | bytes 995336 | tf_op jit(solution)/shard_map/ppermute | solution.py:875
  740.7 30.0 %collective-permute-start.36 = (bf16[256,768]{1,0:T(8,128)(2,1)}, bf16[256,768]{1,0:T(8,128)(2,1)}, u32[]{:S(2)}, u32[]{:S(2)}) collective-permute-start(bf16[256,768]{1,0:T(8,128)(2,1)} %slice.495), channel_id=1, source_target_pairs={{0,1},{1,0},{2,3},{3,2},{4,5},{5,4},{6,7},{7,6},{8,9},{9,8},{10,11... | collective-permute-start | bytes 1179656 | tf_op jit(solution)/shard_map/ppermute | solution.py:875
  742.3 6.3 collective-permute-start.45
  767.9 12.1 %collective-permute-start.37 = (bf16[2,96,1280]{2,1,0:T(8,128)(2,1)S(1)}, bf16[2,96,1280]{2,1,0:T(8,128)(2,1)S(1)}, u32[]{:S(2)}, u32[]{:S(2)}) collective-permute-start(bf16[2,96,1280]{2,1,0:T(8,128)(2,1)S(1)} %dynamic-slice_bitcast_fusion.1), channel_id=1, source_target_pairs={{0,8},{8,0},{16,24},{24,16},{1,9},{9,1},{17,25},{25,17},{2,10},{10... | collective-permute-start | bytes 1474568 | tf_op jit(solution)/shard_map/ppermute | solution.py:875
  769.1 12.5 %collective-permute-start.39 = (bf16[2,96,1280]{2,1,0:T(8,128)(2,1)S(1)}, bf16[2,96,1280]{2,1,0:T(8,128)(2,1)S(1)}, u32[]{:S(2)}, u32[]{:S(2)}) collective-permute-start(bf16[2,96,1280]{2,1,0:T(8,128)(2,1)S(1)} %dynamic-slice_bitcast_fusion), channel_id=1, source_target_pairs={{0,16},{8,24},{16,0},{24,8},{1,17},{9,25},{17,1},{25,9},{2,18},{10... | collective-permute-start | bytes 1474568 | tf_op jit(solution)/shard_map/ppermute | solution.py:875
  788.2 13.2 %collective-permute-start.41 = (bf16[2,48,1280]{2,1,0:T(8,128)(2,1)S(1)}, bf16[2,48,1280]{2,1,0:T(8,128)(2,1)S(1)}, u32[]{:S(2)}, u32[]{:S(2)}) collective-permute-start(bf16[2,48,1280]{2,1,0:T(8,128)(2,1)S(1)} %dynamic-slice_bitcast_fusion.8), channel_id=1, source_target_pairs={{0,2},{1,3},{2,0},{3,1},{4,6},{5,7},{6,4},{7,5},{8,10},{9,11},{10,... | collective-permute-start | bytes 737288 | tf_op jit(solution)/shard_map/ppermute | solution.py:875
  801.5 12.4 %collective-permute-start.42 = (bf16[48,1280]{1,0:T(8,128)(2,1)S(1)}, bf16[48,1280]{1,0:T(8,128)(2,1)S(1)}, u32[]{:S(2)}, u32[]{:S(2)}) collective-permute-start(bf16[48,1280]{1,0:T(8,128)(2,1)S(1)} %dynamic-slice_bitcast_fusion.13), channel_id=1, source_target_pairs={{0,4},{1,5},{2,6},{3,7},{4,0},{5,1},{6,2},{7,3},{8,12},{9,13},{10,... | collective-permute-start | bytes 368648 | tf_op jit(solution)/shard_map/ppermute | solution.py:875
  (96 other events, 506.8 us)
Sparse Core Ops, SparseCore 0:
  10.4 94.9 all-gather.6
  107.6 63.3 all-gather.8
  173.3 63.4 all-gather.10
  445.5 91.7 reduce-scatter.7
  539.6 38.9 reduce-scatter.11
  580.9 69.5 reduce-scatter.5
  652.9 68.1 reduce-scatter.9
  745.0 77.0 reduce-scatter.13

commit v4 on v3

--- a/solution.py
+++ b/solution.py
@@ -285,6 +285,7 @@
 
 def attend_backward_kernel(
     chained,
+    bounds,
     info,
     spot,
     xp_hbm,
@@ -293,13 +294,13 @@
     xqp_ref,
     xqc_ref,
     q_ref,
-    do_ref,
     o_ref,
     lse_ref,
     w_ref,
     vec_ref,
     *refs,
 ):
+    parts, refs = refs[:4], refs[4:]
     if chained:
         old_w, old_vec, old_bias = refs[:3]
         refs = refs[3:]
@@ -320,6 +321,7 @@
         dom,
         dqt,
         drow,
+        do_ref,
         sems,
         done,
     ) = refs
@@ -327,6 +329,12 @@
     TQ = q_ref.shape[0]
     keys_all = kv.shape[0]
     gain, shift = (vec_ref[i : i + 1, :] for i in range(2))
+    for part, (begin, end) in zip(parts, bounds):
+
+        @pl.when((block >= begin) & (block < end))
+        def _():
+            do_ref[...] = part[...]
+
 
     @pl.when(block == 0)
     def _():
@@ -517,8 +525,19 @@
         pl.BlockSpec((8, 3 * HALF), lambda i, s, t: (0, 0)),
     ]
     extra = () if totals is None else tuple(totals)
+    bounds, parts_in, begin = [], [], 0
+    for part in do:
+        end = begin + part.shape[0] // TQ
+        bounds.append((begin, end))
+        parts_in.append(
+            pl.BlockSpec(
+                (TQ, HALF),
+                lambda i, s, t, begin=begin, end=end: (jnp.clip(i - begin, 0, end - begin - 1), 0),
+            )
+        )
+        begin = end
     return pl.pallas_call(
-        functools.partial(attend_backward_kernel, totals is not None),
+        functools.partial(attend_backward_kernel, totals is not None, bounds),
         grid_spec=pltpu.PrefetchScalarGridSpec(
             num_scalar_prefetch=2,
             grid=(blocks,),
@@ -529,10 +548,10 @@
                 *query_specs(TQ),
                 heads,
                 heads,
-                heads,
                 pl.BlockSpec((1, 8, TQ), lambda i, s, t: (i, 0, 0)),
                 pl.BlockSpec(weight.shape, lambda i, s, t: (0, 0)),
                 pl.BlockSpec(vec.shape, lambda i, s, t: (0, 0)),
+                *parts_in,
             ]
             + ([whole] + fixed if extra else []),
             out_specs=[whole, whole, whole] + fixed,
@@ -548,6 +567,7 @@
                 pltpu.VMEM((NH, TQ, 128), BF),
                 pltpu.VMEM((HALF, TQ), F32),
                 pltpu.VMEM((8, TQ), F32),
+                pltpu.VMEM((TQ, HALF), BF),
                 pltpu.SemaphoreType.DMA((2,)),
                 pltpu.SemaphoreType.DMA((2,)),
             ],
@@ -568,7 +588,7 @@
             transcendentals=0,
         ),
         name="attend_backward",
-    )(info, spot, xp, xc, kv, xp, xc, q, do, o, lse, weight, vec, *extra)
+    )(info, spot, xp, xc, kv, xp, xc, q, o, lse, weight, vec, *do, *extra)
 
 
 def gelu_parts(value):
@@ -590,12 +610,11 @@
     xc_ref,
     gp_ref,
     gc_ref,
-    mine_ref,
-    mate_ref,
     vec_ref,
     bfc_ref,
     *refs,
 ):
+    heads, refs = refs[: 4 * MB], refs[4 * MB :]
     pieces = refs[:count]
     (
         fp_ref,
@@ -615,12 +634,14 @@
         afc,
         aout,
         stage,
+        mine_ref,
+        mate_ref,
         sems,
     ) = refs[count:]
     core = places[0]
     batch = pl.program_id(0)
     part = pl.program_id(1)
-    tile = mine_ref.shape[1]
+    tile = mine_ref.shape[0]
     is_cont = part >= prompt_parts
     begin = (batch == 0) & (part == 0)
 
@@ -702,8 +723,16 @@
     place = lax.broadcasted_iota(jnp.int32, (tile, 1), 0) + start % clen
     valid = jnp.where(jnp.logical_not(is_cont) | (place < length), 1.0, 0.0)
 
-    mine = mine_ref[0]
-    mate = mate_ref[0]
+    for m in range(MB):
+        for kind, wanted in enumerate((jnp.logical_not(is_cont), is_cont)):
+
+            @pl.when((batch == m) & wanted)
+            def _():
+                mine_ref[...] = heads[4 * m + kind][...]
+                mate_ref[...] = heads[4 * m + 2 + kind][...]
+
+    mine = mine_ref[...]
+    mate = mate_ref[...]
     h = x + valid * (dot_nn(mine, wp[:HALF, :]) + dot_nn(mate, wp[HALF:, :]) + b_proj)
     center = h - jnp.mean(h, axis=1, keepdims=True)
     rate = lax.rsqrt(jnp.mean(center * center, axis=1, keepdims=True) + EPSILON)
@@ -799,7 +828,7 @@
             copy.wait()
 
 
-def feed_forward(lens, places, prompt_in, cont_in, prompt_cot, cont_cot, mine, mate, vec, bfc, pieces, groups, share):
+def feed_forward(lens, places, prompt_in, cont_in, prompt_cot, cont_cot, heads_in, vec, bfc, pieces, groups, share):
     prow = prompt_in.shape[1]
     crow = cont_in.shape[1]
     clen = crow // lens.shape[1]
@@ -810,6 +839,16 @@
     conts = pl.BlockSpec((1, tile, D), lambda m, i, s, t: (m, jnp.maximum(i - prompt_parts, 0), 0))
     heads = pl.BlockSpec((1, tile, HALF), lambda m, i, s, t: (m, i, 0))
     whole = pl.BlockSpec(memory_space=pl.ANY)
+    def part_spec(own, first, count):
+        def place(m, i, s, t):
+            inside = jnp.clip(i - first, 0, count - 1)
+            return (jnp.where(m == own, inside, jnp.where(m < own, 0, count - 1)), 0)
+
+        return pl.BlockSpec((tile, HALF), place)
+
+    parts_in = []
+    for own in range(MB):
+        parts_in += [part_spec(own, 0, prompt_parts), part_spec(own, prompt_parts, crow // tile)] * 2
     fixed = pl.BlockSpec((8, D), lambda m, i, s, t: (0, 0))
     long = pl.BlockSpec((8, FF), lambda m, i, s, t: (0, 0))
     shape = jax.ShapeDtypeStruct
@@ -824,11 +863,10 @@
                 conts,
                 prompts,
                 conts,
-                heads,
-                heads,
                 fixed,
                 pl.BlockSpec((1, FF), lambda m, i, s, t: (0, 0)),
             ]
+            + parts_in
             + [whole] * len(pieces),
             out_specs=[prompts, conts, prompts, conts, heads, heads, fixed, long, whole, whole],
             scratch_shapes=[
@@ -839,6 +877,8 @@
                 pltpu.VMEM((D, FF), F32),
                 pltpu.VMEM((D, FF), F32),
                 pltpu.VMEM((2, D // share, share, D), BF),
+                pltpu.VMEM((tile, HALF), BF),
+                pltpu.VMEM((tile, HALF), BF),
                 pltpu.SemaphoreType.DMA(
                     (max(16, (2 + FF // D) * sum(piece.shape[0] for piece in pieces)),)
                 ),
@@ -849,8 +889,8 @@
             shape(cont_in.shape, BF),
             shape(prompt_in.shape, BF),
             shape(cont_in.shape, BF),
-            shape(mine.shape, BF),
-            shape(mate.shape, BF),
+            shape((MB, prow + crow, HALF), BF),
+            shape((MB, prow + crow, HALF), BF),
             shape((8, D), F32),
             shape((8, FF), F32),
             shape((D // share, share, D + FF + FF // 2), BF),
@@ -863,7 +903,51 @@
             flops=6 * rows * (D * D + 2 * D * FF), bytes_accessed=50 << 20, transcendentals=0
         ),
         name="feed_forward",
-    )(lens, places, prompt_in, cont_in, prompt_cot, cont_cot, mine, mate, vec, bfc, *pieces)
+    )(lens, places, prompt_in, cont_in, prompt_cot, cont_cot, vec, bfc, *heads_in, *pieces)
+
+
+def input_grad_kernel(x_ref, slope_ref, vec_ref, *refs):
+    batch = pl.program_id(0)
+    out_ref, change_ref = refs[MB:]
+    for m in range(MB):
+
+        @pl.when(batch == m)
+        def _():
+            change_ref[...] = refs[m][...].astype(F32)
+
+    x = x_ref[0].astype(F32)
+    center = x - jnp.mean(x, axis=1, keepdims=True)
+    rate = lax.rsqrt(jnp.mean(center * center, axis=1, keepdims=True) + EPSILON)
+    hat = center * rate
+    e1 = change_ref[...] * vec_ref[0:1, :]
+    change = e1 - jnp.mean(e1, axis=1, keepdims=True)
+    change = change - hat * jnp.mean(e1 * hat, axis=1, keepdims=True)
+    out_ref[0] = (slope_ref[0].astype(F32) + rate * change).astype(BF)
+
+
+def input_grads(x, slope, vec, tables, tile):
+    count = x.shape[1] // tile
+
+    def table_spec(own):
+        def place(m, i):
+            return (jnp.where(m == own, i, jnp.where(m < own, 0, count - 1)), 0)
+
+        return pl.BlockSpec((tile, D), place)
+
+    rows = pl.BlockSpec((1, tile, D), lambda m, i: (m, i, 0))
+    return pl.pallas_call(
+        input_grad_kernel,
+        grid=(MB, count),
+        in_specs=[rows, rows, pl.BlockSpec(vec.shape, lambda m, i: (0, 0))]
+        + [table_spec(own) for own in range(MB)],
+        out_specs=rows,
+        out_shape=jax.ShapeDtypeStruct(x.shape, BF),
+        scratch_shapes=[pltpu.VMEM((tile, D), F32)],
+        compiler_params=pltpu.CompilerParams(
+            dimension_semantics=("arbitrary", "arbitrary"), vmem_limit_bytes=24 << 20
+        ),
+        name="input_grads",
+    )(x, slope, vec, *tables)
 
 
 HEAD_COLS = 3 * HALF
@@ -1147,10 +1231,10 @@
 
     def send_home(own, other):
         return (
-            jnp.concatenate([lax.ppermute(own[:prow], "fsdp", own_pairs), own[prow:]], axis=0),
-            jnp.concatenate(
-                [lax.ppermute(other[:prow], "fsdp", mate_pairs), swap(other[prow:])], axis=0
-            ),
+            lax.ppermute(own[:prow], "fsdp", own_pairs),
+            own[prow:],
+            lax.ppermute(other[:prow], "fsdp", mate_pairs),
+            swap(other[prow:]),
         )
 
     def send_back(own, other):
@@ -1220,8 +1304,7 @@
     ).astype(jnp.int32)
 
     saved = []
-    outs_mine = []
-    outs_mate = []
+    outs = []
     for m in range(MB):
         x_prompt = prompt_all[m]
         if m > 0:
@@ -1234,9 +1317,7 @@
         o, lse, query, kv = attend_forward(plan, spot, x_prompt, x_cont, w_heads, vec_a, TQ, prow)
         if square and m == 1:
             lse, *rest_fars = pin(lse, *rest_fars)
-        own, other = send_home(o[:mine], o[mine:])
-        outs_mine.append(own)
-        outs_mate.append(other)
+        outs.append(send_home(o[:mine], o[mine:]))
         saved.append([x_prompt, x_cont, kv, query, plan, o, lse])
 
     if square:
@@ -1262,8 +1343,7 @@
         cont_in,
         prompt_cot,
         cont_cot,
-        jnp.stack(outs_mine),
-        jnp.stack(outs_mate),
+        [part for parts in outs for part in parts],
         vec_b,
         b_fc,
         pieces,
@@ -1293,7 +1373,7 @@
             g_more, *returned[m] = pin(g_more, *returned[m])
         if m == 1:
             g_rest, *returned[m] = pin(g_rest, *returned[m])
-        do = jnp.concatenate(returned[m], axis=0)
+        do = returned[m]
         table, table_cont, *totals = attend_backward(
             plan, spot, x_prompt, x_cont, kv, query, do, o, lse, w_heads, vec_a, totals, TQ, prow
         )
@@ -1302,12 +1382,8 @@
             table_cont[:crow].astype(F32) + swap(table_cont[crow:]).astype(F32)
         )
     if MB > 1:
-        *tables, conts_back[-1] = pin(*tables, conts_back[-1])
+        tables = pin(*tables)
     tables[-1] = lax.psum_scatter(tables[-1], "fsdp", scatter_dimension=0, tiled=True)
-    early = jnp.concatenate([g_rest, g_more], axis=-1)
-    for step in square_steps(core) if square else ():
-        early = step(early)
-    *totals, conts_back[-1] = pin(*totals, conts_back[-1])
     g_heads, g_first, g_bias = totals
 
     def spread(value):
@@ -1333,7 +1409,14 @@
     sums = jnp.concatenate(
         [sums_high, sums_low, jnp.zeros((SMALL_COLS - 2 * count, D), BF)], axis=0
     ).T
-    late = reduce_parameters(jnp.concatenate([g_heads.astype(BF), sums], axis=1))
+    late = jnp.concatenate([g_heads.astype(BF), sums], axis=1)
+    for index, step in enumerate(reduce_steps()):
+        late = step(late)
+        if square and index == 1:
+            late, g_rest, g_more = pin(late, g_rest, g_more)
+    early = jnp.concatenate([g_rest, g_more], axis=-1)
+    for step in square_steps(core) if square else ():
+        early = step(early)
     late_own, late_other = own_rows(late, core)
     sums = late_own[:, HEAD_COLS:].astype(F32) + late_other[:, HEAD_COLS:].astype(F32)
     sums = (sums[:, :count] + sums[:, count : 2 * count]).T
@@ -1358,9 +1441,7 @@
         change = change - hat * jnp.mean(e1 * hat, axis=-1, keepdims=True)
         return (slope.astype(F32) + rate * change).astype(BF)
 
-    prompt_grad = jnp.stack(
-        [input_grad(prompt_in[m], prompt_dh[m], tables[m].astype(F32)) for m in range(MB)]
-    )
+    prompt_grad = input_grads(prompt_in, prompt_dh, vec_a, tables, TQ)
     cont_grad = jnp.stack([input_grad(cont_in[m], cont_dh[m], conts_back[m]) for m in range(MB)])
     return (
         prompt_out,

time: 847 us -> 838 us (0.989)
  other arithmetic: 53 us -> 23.4 us
  waiting for transfers between devices: 52.1 us -> 73.2 us
  Pallas kernels: 524 us -> 534 us
    reduce_scatter x3, waiting for transfers between devices: 3.25 us -> 22.7 us  [body(): lax.psum_scatter(tables[-1], 'fsdp', scatter_dimension=0, tiled=True)]
    another operation x16 -> x5, other arithmetic: 11.4 us -> 0.05 us  [the longest x4 4.88 us: body(): jnp.stack(outs_mate)]
  transfers between devices with their start and end apart: 56 -> 56, of which waited for: 12 -> 12; matrix products, arithmetic and copies ran while one was open for 12% -> 8% of each run, Pallas kernels for 49% -> 50%
where the time goes in v4:
time: 838 us; the launch traced here: 829 us
  Pallas kernels  534 us (64%)
  waiting for transfers between devices  73.2 us (9%)
  blocking collectives  73 us (9%)
  local copies, waits for them, and re-layouts  57.7 us (7%)
  starting transfers between devices  46.8 us (6%)
  other arithmetic  23.4 us (3%)
  between operations  20.1 us (2%)
    pallas_call x3, Pallas kernels, attend_backward(): pl.pallas_call(functools.partial(attend_backward_kernel, totals is not No...  263 us
    pallas_call x3, Pallas kernels, attend_forward(): pl.pallas_call(attend_forward_kernel, grid_spec=pltpu.PrefetchScalarGridS...  153 us
    pallas_call x1, Pallas kernels, feed_forward(): pl.pallas_call(functools.partial(feed_forward_kernel, prompt_parts, clen,...  113 us
    all_gather x3, blocking collectives, gather_zone(): lax.all_gather(packed, 'fsdp', axis=0, tiled=True, axis_index_groups=groups)  73 us
    ppermute x36, waiting for transfers between devices, neighbour(): return lax.ppermute(value, axis, pairs)  37.8 us
    ppermute x36, starting transfers between devices, neighbour(): return lax.ppermute(value, axis, pairs)  30.9 us
    reduce_scatter x3, waiting for transfers between devices, body(): lax.psum_scatter(tables[-1], 'fsdp', scatter_dimension=0, tiled=True)  22.7 us
  transfers between devices with their start and end apart: 56, of which 12 were waited for; matrix products, arithmetic and copies ran while one was open for 8% of the time, Pallas kernels for 50%

profile of v4, /device:TPU:0, one launch (start us, length us, event | category | flops | bytes accessed | tf_op | source)
XLA Modules:
  0.0 828.6 jit_solution(2873137040919200721)
XLA Ops:
  7.2 3.1 fusion.57
  26.5 23.5 %all_gather.18 = bf16[192,1280]{1,0:T(8,128)(2,1)S(1)} all-gather(bf16[48,1280]{1,0:T(8,128)(2,1)S(1)} %maximum_select_fusion.1), channel_id=1, replica_groups={{0,2,4,6},{1,3,5,7},{8,10,12,14},{9,11,13,15},{16,18,20,22},{17,19,21,2..., dimensions={0}, use_global_device_ids=true | all-gather | bytes 614400 | tf_op jit(solution)/shard_map/all_gather | solution.py:996
  50.2 1.6 collective-permute-start.3
  52.5 1.6 collective-permute-start.2
  54.1 24.9 %all_gather.19 = bf16[192,1664]{1,0:T(8,128)(2,1)S(1)} all-gather(bf16[48,1664]{1,0:T(8,128)(2,1)S(1)} %slice.511), channel_id=1, replica_groups={{0,2,4,6},{1,3,5,7},{8,10,12,14},{9,11,13,15},{16,18,20,22},{17,19,21,2..., dimensions={0}, use_global_device_ids=true | all-gather | bytes 798720 | tf_op jit(solution)/shard_map/all_gather | solution.py:996
  81.0 24.5 %all_gather.20 = bf16[192,1792]{1,0:T(8,128)(2,1)S(1)} all-gather(bf16[48,1792]{1,0:T(8,128)(2,1)S(1)} %slice-done), channel_id=1, replica_groups={{0,2,4,6},{1,3,5,7},{8,10,12,14},{9,11,13,15},{16,18,20,22},{17,19,21,2..., dimensions={0}, use_global_device_ids=true | all-gather | bytes 860160 | tf_op jit(solution)/shard_map/all_gather | solution.py:996
  106.9 1.6 collective-permute-start.12
  114.6 1.6 slice_bitcast_fusion
  118.4 2.9 collective-permute-done.12
  121.4 2.3 pad_maximum_fusion.6.refs_14_
  123.7 2.3 pad_maximum_fusion.5.refs_12_
  126.0 51.4 %attend_forward.3 = (bf16[1536,384]{1,0:T(8,128)(2,1)}, f32[6,8,256]{2,1,0:T(8,128)}, bf16[1536,384]{1,0:T(8,128)(2,1)}, bf16[4608,768]{1,0:T(8,128)(2,1)}) custom-call(s32[6,5]{1,0:T(8,128)} %fusion.48.info, s32[6,5]{1,0:T(8,128)} %stack.331.spot, bf16[4096,768]{1,0:T(8,128)(2,1)} %bitcast.312, bf16[512,768]{1,0:T(8,128)(2,1)} %pad_maximum_fusion.9.xc_hbm.xqc_ref, ...), custom_call_target="tpu_custom_call" | custom-call | flops 24763170816 | bytes 20971520 | tf_op jit(solution)/shard_map/attend_forward/pallas_call | solution.py:244
  177.4 1.6 collective-permute-start.16
  180.5 51.1 %attend_forward.4 = (bf16[1536,384]{1,0:T(8,128)(2,1)}, f32[6,8,256]{2,1,0:T(8,128)}, bf16[1536,384]{1,0:T(8,128)(2,1)}, bf16[4608,768]{1,0:T(8,128)(2,1)}) custom-call(s32[6,5]{1,0:T(8,128)} %get-tuple-element.377.info, s32[6,5]{1,0:T(8,128)} %stack.331.spot, bf16[4096,768]{1,0:T(8,128)(2,1)} %bitcast.308, ...), custom_call_target="tpu_custom_call" | custom-call | flops 24763170816 | bytes 20971520 | tf_op jit(solution)/shard_map/attend_forward/pallas_call | solution.py:244
  234.5 1.8 collective-permute-start.8
  236.3 1.8 fusion.62
  238.8 2.2 collective-permute-start.15
  245.8 2.2 collective-permute-start.24
  248.0 51.0 %attend_forward.5 = (bf16[1536,384]{1,0:T(8,128)(2,1)}, f32[6,8,256]{2,1,0:T(8,128)}, bf16[1536,384]{1,0:T(8,128)(2,1)}, bf16[4608,768]{1,0:T(8,128)(2,1)}) custom-call(s32[6,5]{1,0:T(8,128)} %get-tuple-element.376.info, s32[6,5]{1,0:T(8,128)} %stack.331.spot, bf16[4096,768]{1,0:T(8,128)(2,1)} %bitcast.304, ...), custom_call_target="tpu_custom_call" | custom-call | flops 24763170816 | bytes 20971520 | tf_op jit(solution)/shard_map/attend_forward/pallas_call | solution.py:244
  301.7 1.9 collective-permute-start.19
  303.6 1.7 fusion.60
  307.8 3.5 collective-permute-done.19.refs_10_
  311.4 113.2 %feed_forward.1 = (bf16[3,512,768]{2,1,0:T(8,128)(2,1)}, bf16[3,256,768]{2,1,0:T(8,128)(2,1)}, bf16[3,512,768]{2,1,0:T(8,128)(2,1)}, bf16[3,256,768]{2,1,0:T(8,1...) custom-call(s32[3,1]{1,0:T(4,128)} %copy.200.lens, ...), custom_call_target="tpu_custom_call" | custom-call | flops 73383542784 | bytes 52428800 | tf_op jit(solution)/shard_map/feed_forward/pallas_call | solution.py:856
  426.9 3.5 collective-permute-start.26
  430.6 1.9 slice_bitcast_fusion.22
  432.5 8.3 collective-permute-done.26.refs_2_
  444.0 87.8 %attend_backward.3 = (bf16[4096,768]{1,0:T(8,128)(2,1)}, bf16[512,768]{1,0:T(8,128)(2,1)}, f32[768,1152]{1,0:T(8,128)}, f32[8,768]{1,0:T(8,128)}, f32[8,1152]{1,0:T(8,128)}) custom-call(s32[6,5]{1,0:T(8,128)} %fusion.48.info, s32[6,5]{1,0:T(8,128)} %stack.331.spot, bf16[4096,768]{1,0:T(8,128)(2,1)} %bitcast.314, ...), custom_call_target="tpu_custom_call" | custom-call | flops 59190018048 | bytes 31457280 | tf_op jit(solution)/shard_map/attend_backward/pallas_call | solution.py:539
  532.6 2.4 collective-permute-start.32
  535.1 87.6 %attend_backward.4 = (bf16[4096,768]{1,0:T(8,128)(2,1)}, bf16[512,768]{1,0:T(8,128)(2,1)}, f32[768,1152]{1,0:T(8,128)}, f32[8,768]{1,0:T(8,128)}, f32[8,1152]{1,0:T(8,128)}) custom-call(s32[6,5]{1,0:T(8,128)} %get-tuple-element.377.info, s32[6,5]{1,0:T(8,128)} %stack.331.spot, bf16[4096,768]{1,0:T(8,128)(2,1)} %bitcast.310, ...), custom_call_target="tpu_custom_call" | custom-call | flops 59190018048 | bytes 31457280 | tf_op jit(solution)/shard_map/attend_backward/pallas_call | solution.py:539
  627.7 87.8 %attend_backward.5 = (bf16[4096,768]{1,0:T(8,128)(2,1)}, bf16[512,768]{1,0:T(8,128)(2,1)}, f32[768,1152]{1,0:T(8,128)}, f32[8,768]{1,0:T(8,128)}, f32[8,1152]{1,0:T(8,128)}) custom-call(s32[6,5]{1,0:T(8,128)} %get-tuple-element.376.info, s32[6,5]{1,0:T(8,128)} %stack.331.spot, bf16[4096,768]{1,0:T(8,128)(2,1)} %bitcast.306, ...), custom_call_target="tpu_custom_call" | custom-call | flops 59190018048 | bytes 31457280 | tf_op jit(solution)/shard_map/attend_backward/pallas_call | solution.py:539
  717.7 2.3 convert_element_type.256
  722.8 2.1 fusion.34
  725.5 1.7 fusion.42
  728.3 6.2 collective-permute-done.37
  737.2 1.5 collective-permute-start.40
  738.7 3.4 collective-permute-done.38
  742.2 1.8 collective-permute-done.40
  744.3 1.6 collective-permute-start.44
  746.9 12.4 %collective-permute-done.41 = bf16[2,48,1280]{2,1,0:T(8,128)(2,1)S(1)} collective-permute-done((bf16[2,48,1280]{2,1,0:T(8,128)(2,1)S(1)}, bf16[2,48,1280]{2,1,0:T(8,128)(2,1)S(1)}, u32[]{:S(2)}, u32[]{:S(2)}) %collective-permute-start.41) | collective-permute-done | bytes 245792 | tf_op jit(solution)/shard_map/ppermute | solution.py:959
  759.4 3.3 collective-permute-start.42
  764.0 8.4 %collective-permute-done.42 = bf16[48,1280]{1,0:T(8,128)(2,1)S(1)} collective-permute-done((bf16[48,1280]{1,0:T(8,128)(2,1)S(1)}, bf16[48,1280]{1,0:T(8,128)(2,1)S(1)}, u32[]{:S(2)}, u32[]{:S(2)}) %collective-permute-start.42) | collective-permute-done | bytes 122912 | tf_op jit(solution)/shard_map/ppermute | solution.py:959
  777.4 1.9 collective-permute-done.47
  781.3 2.4 copy.207
  783.7 4.1 reshape.625
  787.8 1.7 copy.227
  790.1 22.7 %reduce-scatter.14.cloned.1.call-done.refs_2_ = bf16[512,768]{1,0:T(8,128)(2,1)} async-done(((bf16[4096,768]{1,0:T(8,128)(2,1)}), bf16[512,768]{1,0:T(8,128)(2,1)}) %reduce-scatter.14.cloned.1.call-update) | async-done | bytes 786448 | tf_op jit(solution)/shard_map/reduce_scatter | solution.py:1386
  812.8 1.7 copy-done.1
  816.8 4.5 input_grads.1
  (390 shorter events, 71.9 us)
Async XLA Ops:
  7.2 118.8 %all-gather.7.cloned.1.call-start = ((), (), s32[]{:S(2)}) async-start(), calls=%async_computation.10 | async-start | bytes 7077888 | tf_op jit(solution)/shard_map/all_gather | solution.py:1153
  10.3 167.1 %all-gather.9.cloned.1.call-start = ((), (), s32[]{:S(2)}) async-start(), calls=%async_computation.11 | async-start | bytes 7077888 | tf_op jit(solution)/shard_map/all_gather | solution.py:1153
  11.1 233.4 %all-gather.11.cloned.1.call-start = ((), (), s32[]{:S(2)}) async-start(), calls=%async_computation.12 | async-start | bytes 7077888 | tf_op jit(solution)/shard_map/all_gather | solution.py:1153
  14.3 35.8 %collective-permute-start = (bf16[24,3456]{1,0:T(8,128)(2,1)S(1)}, bf16[24,3456]{1,0:T(8,128)(2,1)S(1)}, u32[]{:S(2)}, u32[]{:S(2)}) collective-permute-start(bf16[24,3456]{1,0:T(8,128)(2,1)S(1)} %get-tuple-element.369), channel_id=1, source_target_pairs={{0,1},{1,0},{2,3},{3,2},{4,5},{5,4},{6,7},{7,6},{8,9},{9,8},{10,11... | collective-permute-start | bytes 497672 | tf_op jit(solution)/shard_map/ppermute | solution.py:959
  16.9 9.6 %collective-permute-start.1 = (bf16[24,1280]{1,0:T(8,128)(2,1)S(1)}, bf16[24,1280]{1,0:T(8,128)(2,1)S(1)}, u32[]{:S(2)}, u32[]{:S(2)}) collective-permute-start(bf16[24,1280]{1,0:T(8,128)(2,1)S(1)} %pad_maximum_fusion.17), channel_id=1, source_target_pairs={{0,1},{1,0},{2,3},{3,2},{4,5},{5,4},{6,7},{7,6},{8,9},{9,8},{10,11... | collective-permute-start | bytes 184328 | tf_op jit(solution)/shard_map/ppermute | solution.py:959
  17.5 97.1 %collective-permute-start.7 = (bf16[3,256,768]{2,1,0:T(8,128)(2,1)S(1)}, bf16[3,256,768]{2,1,0:T(8,128)(2,1)}, u32[]{:S(2)}, u32[]{:S(2)}) collective-permute-start(bf16[3,256,768]{2,1,0:T(8,128)(2,1)S(1)} %copy-done.6), channel_id=1, source_target_pairs={{0,1},{1,0},{2,3},{3,2},{4,5},{5,4},{6,7},{7,6},{8,9},{9,8},{10,11... | collective-permute-start | bytes 3538952 | tf_op jit(solution)/shard_map/ppermute | solution.py:959
  17.6 517.5 %reduce-scatter.8.cloned.1.call-start = ((), (), s32[]{:S(2)}) async-start(), calls=%async_computation.6 | async-start | bytes 9289728 | tf_op jit(solution)/shard_map/reduce_scatter | solution.py:1358
  50.2 28.8 %collective-permute-start.3 = (bf16[96,1280]{1,0:T(8,128)(2,1)S(1)}, bf16[96,1280]{1,0:T(8,128)(2,1)S(1)}, u32[]{:S(2)}, u32[]{:S(2)}) collective-permute-start(bf16[96,1280]{1,0:T(8,128)(2,1)S(1)} %get-tuple-element.356), channel_id=1, source_target_pairs={{0,16},{8,24},{16,0},{24,8},{1,17},{9,25},{17,1},{25,9},{2,18},{10... | collective-permute-start | bytes 737288 | tf_op jit(solution)/shard_map/ppermute | solution.py:959
  52.5 26.6 %collective-permute-start.2 = (bf16[96,1280]{1,0:T(8,128)(2,1)S(1)}, bf16[96,1280]{1,0:T(8,128)(2,1)S(1)}, u32[]{:S(2)}, u32[]{:S(2)}) collective-permute-start(bf16[96,1280]{1,0:T(8,128)(2,1)S(1)} %get-tuple-element.357), channel_id=1, source_target_pairs={{0,8},{8,0},{16,24},{24,16},{1,9},{9,1},{17,25},{25,17},{2,10},{10... | collective-permute-start | bytes 737288 | tf_op jit(solution)/shard_map/ppermute | solution.py:959
  79.1 26.5 %collective-permute-start.4 = (bf16[2,96,1280]{2,1,0:T(8,128)(2,1)S(1)}, bf16[2,96,1280]{2,1,0:T(8,128)(2,1)S(1)}, u32[]{:S(2)}, u32[]{:S(2)}) collective-permute-start(bf16[2,96,1280]{2,1,0:T(8,128)(2,1)S(1)} %pad_maximum_fusion.12), channel_id=1, source_target_pairs={{0,16},{8,24},{16,0},{24,8},{1,17},{9,25},{17,1},{25,9},{2,18},{10... | collective-permute-start | bytes 1474568 | tf_op jit(solution)/shard_map/ppermute | solution.py:959
  79.5 26.1 %collective-permute-start.5 = (bf16[2,96,1280]{2,1,0:T(8,128)(2,1)S(1)}, bf16[2,96,1280]{2,1,0:T(8,128)(2,1)S(1)}, u32[]{:S(2)}, u32[]{:S(2)}) collective-permute-start(bf16[2,96,1280]{2,1,0:T(8,128)(2,1)S(1)} %pad_maximum_fusion.13), channel_id=1, source_target_pairs={{0,8},{8,0},{16,24},{24,16},{1,9},{9,1},{17,25},{25,17},{2,10},{10... | collective-permute-start | bytes 1474568 | tf_op jit(solution)/shard_map/ppermute | solution.py:959
  106.9 14.5 %collective-permute-start.12 = (bf16[96,3456]{1,0:T(8,128)(2,1)}, bf16[96,3456]{1,0:T(8,128)(2,1)}, u32[]{:S(2)}, u32[]{:S(2)}) collective-permute-start(bf16[96,3456]{1,0:T(8,128)(2,1)} %get-tuple-element.326), channel_id=1, source_target_pairs={{0,16},{8,24},{16,0},{24,8},{1,17},{9,25},{17,1},{25,9},{2,18},{10... | collective-permute-start | bytes 1990664 | tf_op jit(solution)/shard_map/ppermute | solution.py:959
  108.4 15.2 %collective-permute-start.11 = (bf16[96,3456]{1,0:T(8,128)(2,1)}, bf16[96,3456]{1,0:T(8,128)(2,1)}, u32[]{:S(2)}, u32[]{:S(2)}) collective-permute-start(bf16[96,3456]{1,0:T(8,128)(2,1)} %get-tuple-element.327), channel_id=1, source_target_pairs={{0,8},{8,0},{16,24},{24,16},{1,9},{9,1},{17,25},{25,17},{2,10},{10... | collective-permute-start | bytes 1990664 | tf_op jit(solution)/shard_map/ppermute | solution.py:959
  177.4 61.4 %collective-permute-start.16 = (bf16[2,96,3456]{2,1,0:T(8,128)(2,1)}, bf16[2,96,3456]{2,1,0:T(8,128)(2,1)S(1)}, u32[]{:S(2)}, u32[]{:S(2)}) collective-permute-start(bf16[2,96,3456]{2,1,0:T(8,128)(2,1)} %pad_maximum_fusion.5.refs_12_), channel_id=1, source_target_pairs={{0,16},{8,24},{16,0},{24,8},{1,17},{9,25},{17,1},{25,9},{2,18},{10... | collective-permute-start | bytes 3981320 | tf_op jit(solution)/shard_map/ppermute | solution.py:959
  179.0 62.0 %collective-permute-start.17 = (bf16[2,96,3456]{2,1,0:T(8,128)(2,1)S(1)}, bf16[2,96,3456]{2,1,0:T(8,128)(2,1)S(1)}, u32[]{:S(2)}, u32[]{:S(2)}) collective-permute-start(bf16[2,96,3456]{2,1,0:T(8,128)(2,1)S(1)} %copy-done.15), channel_id=1, source_target_pairs={{0,8},{8,0},{16,24},{24,16},{1,9},{9,1},{17,25},{25,17},{2,10},{10... | collective-permute-start | bytes 3981320 | tf_op jit(solution)/shard_map/ppermute | solution.py:959
  233.0 12.0 %collective-permute-start.13 = (bf16[512,384]{1,0:T(8,128)(2,1)S(1)}, bf16[512,384]{1,0:T(8,128)(2,1)}, u32[]{:S(2)}, u32[]{:S(2)}) collective-permute-start(bf16[512,384]{1,0:T(8,128)(2,1)S(1)} %get-tuple-element.341), channel_id=1, source_target_pairs={{0,0},{1,3},{2,2},{3,1},{4,4},{5,7},{6,6},{7,5},{8,8},{9,11},{10,1... | collective-permute-start | bytes 1179656 | tf_op jit(solution)/shard_map/ppermute | solution.py:1234
  234.4 10.9 %collective-permute-start.14 = (bf16[512,384]{1,0:T(8,128)(2,1)S(1)}, bf16[512,384]{1,0:T(8,128)(2,1)}, u32[]{:S(2)}, u32[]{:S(2)}) collective-permute-start(bf16[512,384]{1,0:T(8,128)(2,1)S(1)} %get-tuple-element.340), channel_id=1, source_target_pairs={{0,3},{1,0},{2,1},{3,2},{4,7},{5,4},{6,5},{7,6},{8,11},{9,8},{10,9... | collective-permute-start | bytes 1179656 | tf_op jit(solution)/shard_map/ppermute | solution.py:1236
  234.5 11.3 %collective-permute-start.8 = (bf16[512,384]{1,0:T(8,128)(2,1)S(1)}, bf16[512,384]{1,0:T(8,128)(2,1)}, u32[]{:S(2)}, u32[]{:S(2)}) collective-permute-start(bf16[512,384]{1,0:T(8,128)(2,1)S(1)} %get-tuple-element.345), channel_id=1, source_target_pairs={{0,0},{1,3},{2,2},{3,1},{4,4},{5,7},{6,6},{7,5},{8,8},{9,11},{10,1... | collective-permute-start | bytes 1179656 | tf_op jit(solution)/shard_map/ppermute | solution.py:1234
  244.5 57.2 %collective-permute-start.21 = (bf16[2,96,3456]{2,1,0:T(8,128)(2,1)}, bf16[2,96,3456]{2,1,0:T(8,128)(2,1)S(1)}, u32[]{:S(2)}, u32[]{:S(2)}) collective-permute-start(bf16[2,96,3456]{2,1,0:T(8,128)(2,1)} %pad_maximum_fusion.5.refs_12_), channel_id=1, source_target_pairs={{0,1},{1,0},{2,3},{3,2},{4,5},{5,4},{6,7},{7,6},{8,9},{9,8},{10,11... | collective-permute-start | bytes 3981320 | tf_op jit(solution)/shard_map/ppermute | solution.py:959
  244.5 60.8 %collective-permute-start.23 = (bf16[2,96,3456]{2,1,0:T(8,128)(2,1)S(1)}, bf16[2,96,3456]{2,1,0:T(8,128)(2,1)S(1)}, u32[]{:S(2)}, u32[]{:S(2)}) collective-permute-start(bf16[2,96,3456]{2,1,0:T(8,128)(2,1)S(1)} %copy-done.15), channel_id=1, source_target_pairs={{0,1},{1,0},{2,3},{3,2},{4,5},{5,4},{6,7},{7,6},{8,9},{9,8},{10,11... | collective-permute-start | bytes 3981320 | tf_op jit(solution)/shard_map/ppermute | solution.py:959
  245.0 55.2 %collective-permute-start.9 = (bf16[512,384]{1,0:T(8,128)(2,1)S(1)}, bf16[512,384]{1,0:T(8,128)(2,1)S(1)}, u32[]{:S(2)}, u32[]{:S(2)}) collective-permute-start(bf16[512,384]{1,0:T(8,128)(2,1)S(1)} %get-tuple-element.344), channel_id=1, source_target_pairs={{0,3},{1,0},{2,1},{3,2},{4,7},{5,4},{6,5},{7,6},{8,11},{9,8},{10,9... | collective-permute-start | bytes 1179656 | tf_op jit(solution)/shard_map/ppermute | solution.py:1236
  245.3 66.1 %collective-permute-start.22 = (bf16[2,96,3456]{2,1,0:T(8,128)(2,1)}, bf16[2,96,3456]{2,1,0:T(8,128)(2,1)}, u32[]{:S(2)}, u32[]{:S(2)}) collective-permute-start(bf16[2,96,3456]{2,1,0:T(8,128)(2,1)} %copy-done.29), channel_id=1, source_target_pairs={{0,1},{1,0},{2,3},{3,2},{4,5},{5,4},{6,7},{7,6},{8,9},{9,8},{10,11... | collective-permute-start | bytes 3981320 | tf_op jit(solution)/shard_map/ppermute | solution.py:959
  245.8 65.6 %collective-permute-start.24 = (bf16[2,96,3456]{2,1,0:T(8,128)(2,1)}, bf16[2,96,3456]{2,1,0:T(8,128)(2,1)}, u32[]{:S(2)}, u32[]{:S(2)}) collective-permute-start(bf16[2,96,3456]{2,1,0:T(8,128)(2,1)} %copy-done.30), channel_id=1, source_target_pairs={{0,1},{1,0},{2,3},{3,2},{4,5},{5,4},{6,7},{7,6},{8,9},{9,8},{10,11... | collective-permute-start | bytes 3981320 | tf_op jit(solution)/shard_map/ppermute | solution.py:959
  300.2 7.6 collective-permute-start.18
  301.7 9.7 %collective-permute-start.19 = (bf16[512,384]{1,0:T(8,128)(2,1)S(1)}, bf16[512,384]{1,0:T(8,128)(2,1)}, u32[]{:S(2)}, u32[]{:S(2)}) collective-permute-start(bf16[512,384]{1,0:T(8,128)(2,1)S(1)} %get-tuple-element.330), channel_id=1, source_target_pairs={{0,3},{1,0},{2,1},{3,2},{4,7},{5,4},{6,5},{7,6},{8,11},{9,8},{10,9... | collective-permute-start | bytes 1179656 | tf_op jit(solution)/shard_map/ppermute | solution.py:1236
  426.0 6.5 collective-permute-start.25
  426.9 13.9 %collective-permute-start.26 = (bf16[512,384]{1,0:T(8,128)(2,1)S(1)}, bf16[512,384]{1,0:T(8,128)(2,1)S(1)}, u32[]{:S(2)}, u32[]{:S(2)}) collective-permute-start(bf16[512,384]{1,0:T(8,128)(2,1)S(1)} %get-tuple-element.315), channel_id=1, source_target_pairs={{3,0},{0,1},{1,2},{2,3},{7,4},{4,5},{5,6},{6,7},{11,8},{8,9},{9,10... | collective-permute-start | bytes 1179656 | tf_op jit(solution)/shard_map/ppermute | solution.py:1244
  441.6 186.0 %reduce-scatter.12.cloned.1.call-start = ((), (), s32[]{:S(2)}) async-start(), calls=%async_computation.8 | async-start | bytes 2654208 | tf_op jit(solution)/shard_map/reduce_scatter | solution.py:1358
  441.7 90.1 %collective-permute-start.28 = (bf16[512,384]{1,0:T(8,128)(2,1)S(1)}, bf16[512,384]{1,0:T(8,128)(2,1)}, u32[]{:S(2)}, u32[]{:S(2)}) collective-permute-start(bf16[512,384]{1,0:T(8,128)(2,1)S(1)} %get-tuple-element.320), channel_id=1, source_target_pairs={{0,0},{3,1},{2,2},{1,3},{4,4},{7,5},{6,6},{5,7},{8,8},{11,9},{10,1... | collective-permute-start | bytes 1179656 | tf_op jit(solution)/shard_map/ppermute | solution.py:1242
  443.1 88.8 %collective-permute-start.29 = (bf16[512,384]{1,0:T(8,128)(2,1)S(1)}, bf16[512,384]{1,0:T(8,128)(2,1)}, u32[]{:S(2)}, u32[]{:S(2)}) collective-permute-start(bf16[512,384]{1,0:T(8,128)(2,1)S(1)} %get-tuple-element.314), channel_id=1, source_target_pairs={{3,0},{0,1},{1,2},{2,3},{7,4},{4,5},{5,6},{6,7},{11,8},{8,9},{9,10... | collective-permute-start | bytes 1179656 | tf_op jit(solution)/shard_map/ppermute | solution.py:1244
  443.1 88.7 %collective-permute-start.30 = (bf16[256,384]{1,0:T(8,128)(2,1)S(1)}, bf16[256,384]{1,0:T(8,128)(2,1)}, u32[]{:S(2)}, u32[]{:S(2)}) collective-permute-start(bf16[256,384]{1,0:T(8,128)(2,1)S(1)} %get-tuple-element.311), channel_id=1, source_target_pairs={{0,1},{1,0},{2,3},{3,2},{4,5},{5,4},{6,7},{7,6},{8,9},{9,8},{10,11... | collective-permute-start | bytes 589832 | tf_op jit(solution)/shard_map/ppermute | solution.py:959
  443.9 290.8 %reduce-scatter.6.cloned.1.call-start = ((), (), s32[]{:S(2)}) async-start(), calls=%async_computation.5 | async-start | bytes 7077888 | tf_op jit(solution)/shard_map/reduce_scatter | solution.py:1371
  531.9 202.9 %reduce-scatter.10.cloned.1.call-start = ((), (), s32[]{:S(2)}) async-start(), calls=%async_computation.7 | async-start | bytes 7077888 | tf_op jit(solution)/shard_map/reduce_scatter | solution.py:1371
  531.9 90.8 %collective-permute-start.31 = (bf16[512,384]{1,0:T(8,128)(2,1)S(1)}, bf16[512,384]{1,0:T(8,128)(2,1)S(1)}, u32[]{:S(2)}, u32[]{:S(2)}) collective-permute-start(bf16[512,384]{1,0:T(8,128)(2,1)S(1)} %get-tuple-element.319), channel_id=1, source_target_pairs={{0,0},{3,1},{2,2},{1,3},{4,4},{7,5},{6,6},{5,7},{8,8},{11,9},{10,1... | collective-permute-start | bytes 1179656 | tf_op jit(solution)/shard_map/ppermute | solution.py:1242
  532.6 90.1 %collective-permute-start.32 = (bf16[512,384]{1,0:T(8,128)(2,1)S(1)}, bf16[512,384]{1,0:T(8,128)(2,1)S(1)}, u32[]{:S(2)}, u32[]{:S(2)}) collective-permute-start(bf16[512,384]{1,0:T(8,128)(2,1)S(1)} %get-tuple-element.313), channel_id=1, source_target_pairs={{3,0},{0,1},{1,2},{2,3},{7,4},{4,5},{5,6},{6,7},{11,8},{8,9},{9,10... | collective-permute-start | bytes 1179656 | tf_op jit(solution)/shard_map/ppermute | solution.py:1244
  535.0 87.7 %collective-permute-start.33 = (bf16[256,384]{1,0:T(8,128)(2,1)S(1)}, bf16[256,384]{1,0:T(8,128)(2,1)S(1)}, u32[]{:S(2)}, u32[]{:S(2)}) collective-permute-start(bf16[256,384]{1,0:T(8,128)(2,1)S(1)} %get-tuple-element.310), channel_id=1, source_target_pairs={{0,1},{1,0},{2,3},{3,2},{4,5},{5,4},{6,7},{7,6},{8,9},{9,8},{10,11... | collective-permute-start | bytes 589832 | tf_op jit(solution)/shard_map/ppermute | solution.py:959
  623.7 189.1 %reduce-scatter.14.cloned.1.call-start = ((), (), s32[]{:S(2)}) async-start(), calls=%async_computation.9 | async-start | bytes 7077888 | tf_op jit(solution)/shard_map/reduce_scatter | solution.py:1386
  627.3 95.5 %collective-permute-start.34 = (bf16[256,768]{1,0:T(8,128)(2,1)}, bf16[256,768]{1,0:T(8,128)(2,1)}, u32[]{:S(2)}, u32[]{:S(2)}) collective-permute-start(bf16[256,768]{1,0:T(8,128)(2,1)} %slice.475), channel_id=1, source_target_pairs={{0,1},{1,0},{2,3},{3,2},{4,5},{5,4},{6,7},{7,6},{8,9},{9,8},{10,11... | collective-permute-start | bytes 1179656 | tf_op jit(solution)/shard_map/ppermute | solution.py:959
  721.2 13.3 %collective-permute-start.37 = (bf16[2,96,1280]{2,1,0:T(8,128)(2,1)S(1)}, bf16[2,96,1280]{2,1,0:T(8,128)(2,1)S(1)}, u32[]{:S(2)}, u32[]{:S(2)}) collective-permute-start(bf16[2,96,1280]{2,1,0:T(8,128)(2,1)S(1)} %dynamic-slice_bitcast_fusion.1), channel_id=1, source_target_pairs={{0,8},{8,0},{16,24},{24,16},{1,9},{9,1},{17,25},{25,17},{2,10},{10... | collective-permute-start | bytes 1474568 | tf_op jit(solution)/shard_map/ppermute | solution.py:959
  722.8 13.2 %collective-permute-start.39 = (bf16[2,96,1280]{2,1,0:T(8,128)(2,1)}, bf16[2,96,1280]{2,1,0:T(8,128)(2,1)}, u32[]{:S(2)}, u32[]{:S(2)}) collective-permute-start(bf16[2,96,1280]{2,1,0:T(8,128)(2,1)} %dynamic-slice_bitcast_fusion), channel_id=1, source_target_pairs={{0,16},{8,24},{16,0},{24,8},{1,17},{9,25},{17,1},{25,9},{2,18},{10... | collective-permute-start | bytes 1474568 | tf_op jit(solution)/shard_map/ppermute | solution.py:959
  734.8 7.3 collective-permute-start.38
  737.2 6.8 collective-permute-start.40
  744.3 18.4 %collective-permute-start.44 = (bf16[2,24,3456]{2,1,0:T(8,128)(2,1)S(1)}, bf16[2,24,3456]{2,1,0:T(8,128)(2,1)S(1)}, u32[]{:S(2)}, u32[]{:S(2)}) collective-permute-start(bf16[2,24,3456]{2,1,0:T(8,128)(2,1)S(1)} %dynamic-slice_bitcast_fusion.7), channel_id=1, source_target_pairs={{0,8},{8,0},{16,24},{24,16},{1,9},{9,1},{17,25},{25,17},{2,10},{10... | collective-permute-start | bytes 995336 | tf_op jit(solution)/shard_map/ppermute | solution.py:959
  746.0 13.4 %collective-permute-start.41 = (bf16[2,48,1280]{2,1,0:T(8,128)(2,1)S(1)}, bf16[2,48,1280]{2,1,0:T(8,128)(2,1)S(1)}, u32[]{:S(2)}, u32[]{:S(2)}) collective-permute-start(bf16[2,48,1280]{2,1,0:T(8,128)(2,1)S(1)} %dynamic-slice_bitcast_fusion.8), channel_id=1, source_target_pairs={{0,2},{1,3},{2,0},{3,1},{4,6},{5,7},{6,4},{7,5},{8,10},{9,11},{10,... | collective-permute-start | bytes 737288 | tf_op jit(solution)/shard_map/ppermute | solution.py:959
  746.7 17.3 %collective-permute-start.46 = (bf16[2,24,3456]{2,1,0:T(8,128)(2,1)S(1)}, bf16[2,24,3456]{2,1,0:T(8,128)(2,1)S(1)}, u32[]{:S(2)}, u32[]{:S(2)}) collective-permute-start(bf16[2,24,3456]{2,1,0:T(8,128)(2,1)S(1)} %dynamic-slice_bitcast_fusion.6), channel_id=1, source_target_pairs={{0,16},{8,24},{16,0},{24,8},{1,17},{9,25},{17,1},{25,9},{2,18},{10... | collective-permute-start | bytes 995336 | tf_op jit(solution)/shard_map/ppermute | solution.py:959
  759.4 13.0 %collective-permute-start.42 = (bf16[48,1280]{1,0:T(8,128)(2,1)S(1)}, bf16[48,1280]{1,0:T(8,128)(2,1)S(1)}, u32[]{:S(2)}, u32[]{:S(2)}) collective-permute-start(bf16[48,1280]{1,0:T(8,128)(2,1)S(1)} %dynamic-slice_bitcast_fusion.13), channel_id=1, source_target_pairs={{0,4},{1,5},{2,6},{3,7},{4,0},{5,1},{6,2},{7,3},{8,12},{9,13},{10,... | collective-permute-start | bytes 368648 | tf_op jit(solution)/shard_map/ppermute | solution.py:959
  762.8 14.5 %collective-permute-start.45 = (bf16[24,3456]{1,0:T(8,128)(2,1)S(1)}, bf16[24,3456]{1,0:T(8,128)(2,1)S(1)}, u32[]{:S(2)}, u32[]{:S(2)}) collective-permute-start(bf16[24,3456]{1,0:T(8,128)(2,1)S(1)} %dynamic-slice_bitcast_fusion.12), channel_id=1, source_target_pairs={{0,16},{8,24},{16,0},{24,8},{1,17},{9,25},{17,1},{25,9},{2,18},{10... | collective-permute-start | bytes 497672 | tf_op jit(solution)/shard_map/ppermute | solution.py:959
  772.6 6.7 collective-permute-start.47
  (58 other events, 313.2 us)
Sparse Core Ops, SparseCore 0:
  10.4 95.0 all-gather.6
  107.8 63.5 all-gather.8
  173.6 63.5 all-gather.10
  441.7 90.0 reduce-scatter.7
  534.1 38.2 reduce-scatter.11
  574.6 69.8 reduce-scatter.5
  646.9 68.1 reduce-scatter.9
  734.9 77.9 reduce-scatter.13

commit v5 on v4

--- a/solution.py
+++ b/solution.py
@@ -1410,10 +1410,8 @@
         [sums_high, sums_low, jnp.zeros((SMALL_COLS - 2 * count, D), BF)], axis=0
     ).T
     late = jnp.concatenate([g_heads.astype(BF), sums], axis=1)
-    for index, step in enumerate(reduce_steps()):
+    for step in reduce_steps():
         late = step(late)
-        if square and index == 1:
-            late, g_rest, g_more = pin(late, g_rest, g_more)
     early = jnp.concatenate([g_rest, g_more], axis=-1)
     for step in square_steps(core) if square else ():
         early = step(early)

time: 838 us -> 834 us (level)
  waiting for transfers between devices: 73.2 us -> 63.3 us
  transfers between devices with their start and end apart: 56 -> 56, of which waited for: 12 -> 12; matrix products, arithmetic and copies ran while one was open for 8% -> 9% of each run, Pallas kernels for 50% -> 51%
where the time goes in v5:
time: 834 us; the launch traced here: 824 us
  Pallas kernels  535 us (64%)
  blocking collectives  73 us (9%)
  waiting for transfers between devices  63.3 us (8%)
  local copies, waits for them, and re-layouts  59.4 us (7%)
  starting transfers between devices  46.6 us (6%)
  other arithmetic  26.6 us (3%)
  between operations  20.2 us (2%)
    pallas_call x3, Pallas kernels, attend_backward(): pl.pallas_call(functools.partial(attend_backward_kernel, totals is not No...  263 us
    pallas_call x3, Pallas kernels, attend_forward(): pl.pallas_call(attend_forward_kernel, grid_spec=pltpu.PrefetchScalarGridS...  154 us
    pallas_call x1, Pallas kernels, feed_forward(): pl.pallas_call(functools.partial(feed_forward_kernel, prompt_parts, clen,...  113 us
    all_gather x3, blocking collectives, gather_zone(): lax.all_gather(packed, 'fsdp', axis=0, tiled=True, axis_index_groups=groups)  73 us
    ppermute x36, starting transfers between devices, neighbour(): return lax.ppermute(value, axis, pairs)  30.7 us
    ppermute x36, waiting for transfers between devices, neighbour(): return lax.ppermute(value, axis, pairs)  30 us
    reduce_scatter x3, waiting for transfers between devices, body(): lax.psum_scatter(tables[-1], 'fsdp', scatter_dimension=0, tiled=True)  20.6 us
  transfers between devices with their start and end apart: 56, of which 12 were waited for; matrix products, arithmetic and copies ran while one was open for 9% of the time, Pallas kernels for 51%

profile of v5, /device:TPU:0, one launch (start us, length us, event | category | flops | bytes accessed | tf_op | source)
XLA Modules:
  0.0 823.9 jit_solution(4814133647350750179)
XLA Ops:
  7.2 3.1 fusion.57
  26.5 23.5 %all_gather.18 = bf16[192,1280]{1,0:T(8,128)(2,1)S(1)} all-gather(bf16[48,1280]{1,0:T(8,128)(2,1)S(1)} %maximum_select_fusion.1), channel_id=1, replica_groups={{0,2,4,6},{1,3,5,7},{8,10,12,14},{9,11,13,15},{16,18,20,22},{17,19,21,2..., dimensions={0}, use_global_device_ids=true | all-gather | bytes 614400 | tf_op jit(solution)/shard_map/all_gather | solution.py:996
  50.2 1.6 collective-permute-start.3
  52.4 1.6 collective-permute-start.2
  54.0 24.9 %all_gather.19 = bf16[192,1664]{1,0:T(8,128)(2,1)S(1)} all-gather(bf16[48,1664]{1,0:T(8,128)(2,1)S(1)} %slice.511), channel_id=1, replica_groups={{0,2,4,6},{1,3,5,7},{8,10,12,14},{9,11,13,15},{16,18,20,22},{17,19,21,2..., dimensions={0}, use_global_device_ids=true | all-gather | bytes 798720 | tf_op jit(solution)/shard_map/all_gather | solution.py:996
  81.0 24.6 %all_gather.20 = bf16[192,1792]{1,0:T(8,128)(2,1)S(1)} all-gather(bf16[48,1792]{1,0:T(8,128)(2,1)S(1)} %slice-done), channel_id=1, replica_groups={{0,2,4,6},{1,3,5,7},{8,10,12,14},{9,11,13,15},{16,18,20,22},{17,19,21,2..., dimensions={0}, use_global_device_ids=true | all-gather | bytes 860160 | tf_op jit(solution)/shard_map/all_gather | solution.py:996
  106.9 1.6 collective-permute-start.12
  108.4 1.5 collective-permute-start.11
  114.6 1.6 slice_bitcast_fusion
  118.4 3.0 collective-permute-done.12
  121.4 2.3 pad_maximum_fusion.6.refs_14_
  123.7 2.3 pad_maximum_fusion.5.refs_12_
  126.0 51.4 %attend_forward.3 = (bf16[1536,384]{1,0:T(8,128)(2,1)}, f32[6,8,256]{2,1,0:T(8,128)}, bf16[1536,384]{1,0:T(8,128)(2,1)}, bf16[4608,768]{1,0:T(8,128)(2,1)}) custom-call(s32[6,5]{1,0:T(8,128)} %fusion.48.info, s32[6,5]{1,0:T(8,128)} %stack.331.spot, bf16[4096,768]{1,0:T(8,128)(2,1)} %bitcast.312, bf16[512,768]{1,0:T(8,128)(2,1)} %pad_maximum_fusion.9.xc_hbm.xqc_ref, ...), custom_call_target="tpu_custom_call" | custom-call | flops 24763170816 | bytes 20971520 | tf_op jit(solution)/shard_map/attend_forward/pallas_call | solution.py:244
  177.5 1.5 collective-permute-start.16
  179.0 1.5 collective-permute-start.17
  180.5 51.1 %attend_forward.4 = (bf16[1536,384]{1,0:T(8,128)(2,1)}, f32[6,8,256]{2,1,0:T(8,128)}, bf16[1536,384]{1,0:T(8,128)(2,1)}, bf16[4608,768]{1,0:T(8,128)(2,1)}) custom-call(s32[6,5]{1,0:T(8,128)} %get-tuple-element.371.info, s32[6,5]{1,0:T(8,128)} %stack.331.spot, bf16[4096,768]{1,0:T(8,128)(2,1)} %bitcast.308, ...), custom_call_target="tpu_custom_call" | custom-call | flops 24763170816 | bytes 20971520 | tf_op jit(solution)/shard_map/attend_forward/pallas_call | solution.py:244
  234.5 1.8 collective-permute-start.8
  236.3 1.8 fusion.62
  238.8 2.2 collective-permute-start.15
  245.8 2.2 collective-permute-start.24
  248.0 51.0 %attend_forward.5 = (bf16[1536,384]{1,0:T(8,128)(2,1)}, f32[6,8,256]{2,1,0:T(8,128)}, bf16[1536,384]{1,0:T(8,128)(2,1)}, bf16[4608,768]{1,0:T(8,128)(2,1)}) custom-call(s32[6,5]{1,0:T(8,128)} %get-tuple-element.370.info, s32[6,5]{1,0:T(8,128)} %stack.331.spot, bf16[4096,768]{1,0:T(8,128)(2,1)} %bitcast.304, ...), custom_call_target="tpu_custom_call" | custom-call | flops 24763170816 | bytes 20971520 | tf_op jit(solution)/shard_map/attend_forward/pallas_call | solution.py:244
  300.2 1.4 collective-permute-start.18
  301.7 1.9 collective-permute-start.19
  303.6 1.7 fusion.60
  307.8 3.5 collective-permute-done.19.refs_10_
  311.3 113.3 %feed_forward.1 = (bf16[3,512,768]{2,1,0:T(8,128)(2,1)}, bf16[3,256,768]{2,1,0:T(8,128)(2,1)}, bf16[3,512,768]{2,1,0:T(8,128)(2,1)}, bf16[3,256,768]{2,1,0:T(8,1...) custom-call(s32[3,1]{1,0:T(4,128)} %copy.200.lens, ...), custom_call_target="tpu_custom_call" | custom-call | flops 73383542784 | bytes 52428800 | tf_op jit(solution)/shard_map/feed_forward/pallas_call | solution.py:856
  424.7 1.5 slice_bitcast_fusion.5
  427.0 3.5 collective-permute-start.26
  430.7 1.9 slice_bitcast_fusion.22
  432.6 8.3 %collective-permute-done.26.refs_2_ = bf16[512,384]{1,0:T(8,128)(2,1)S(1)} collective-permute-done((bf16[512,384]{1,0:T(8,128)(2,1)S(1)}, bf16[512,384]{1,0:T(8,128)(2,1)S(1)}, u32[]{:S(2)}, u32[]{:S(2)}) %collective-permute-start.26) | collective-permute-done | bytes 393248 | tf_op jit(solution)/shard_map/ppermute | solution.py:1244
  441.8 1.4 collective-permute-start.28
  444.1 87.9 %attend_backward.3 = (bf16[4096,768]{1,0:T(8,128)(2,1)}, bf16[512,768]{1,0:T(8,128)(2,1)}, f32[768,1152]{1,0:T(8,128)}, f32[8,768]{1,0:T(8,128)}, f32[8,1152]{1,0:T(8,128)}) custom-call(s32[6,5]{1,0:T(8,128)} %fusion.48.info, s32[6,5]{1,0:T(8,128)} %stack.331.spot, bf16[4096,768]{1,0:T(8,128)(2,1)} %bitcast.314, ...), custom_call_target="tpu_custom_call" | custom-call | flops 59190018048 | bytes 31457280 | tf_op jit(solution)/shard_map/attend_backward/pallas_call | solution.py:539
  532.7 2.4 collective-permute-start.32
  535.3 87.6 %attend_backward.4 = (bf16[4096,768]{1,0:T(8,128)(2,1)}, bf16[512,768]{1,0:T(8,128)(2,1)}, f32[768,1152]{1,0:T(8,128)}, f32[8,768]{1,0:T(8,128)}, f32[8,1152]{1,0:T(8,128)}) custom-call(s32[6,5]{1,0:T(8,128)} %get-tuple-element.371.info, s32[6,5]{1,0:T(8,128)} %stack.331.spot, bf16[4096,768]{1,0:T(8,128)(2,1)} %bitcast.310, ...), custom_call_target="tpu_custom_call" | custom-call | flops 59190018048 | bytes 31457280 | tf_op jit(solution)/shard_map/attend_backward/pallas_call | solution.py:539
  627.9 87.9 %attend_backward.5 = (bf16[4096,768]{1,0:T(8,128)(2,1)}, bf16[512,768]{1,0:T(8,128)(2,1)}, f32[768,1152]{1,0:T(8,128)}, f32[8,768]{1,0:T(8,128)}, f32[8,1152]{1,0:T(8,128)}) custom-call(s32[6,5]{1,0:T(8,128)} %get-tuple-element.370.info, s32[6,5]{1,0:T(8,128)} %stack.331.spot, bf16[4096,768]{1,0:T(8,128)(2,1)} %bitcast.306, ...), custom_call_target="tpu_custom_call" | custom-call | flops 59190018048 | bytes 31457280 | tf_op jit(solution)/shard_map/attend_backward/pallas_call | solution.py:539
  724.1 2.0 collective-permute-start.37
  735.9 2.2 fusion.34
  738.6 1.7 fusion.42
  743.1 1.5 collective-permute-start.38
  746.7 4.3 collective-permute-done.38
  751.1 2.1 collective-permute-done.40
  753.8 13.5 %collective-permute-done.41 = bf16[2,48,1280]{2,1,0:T(8,128)(2,1)S(1)} collective-permute-done((bf16[2,48,1280]{2,1,0:T(8,128)(2,1)S(1)}, bf16[2,48,1280]{2,1,0:T(8,128)(2,1)S(1)}, u32[]{:S(2)}, u32[]{:S(2)}) %collective-permute-start.41) | collective-permute-done | bytes 245792 | tf_op jit(solution)/shard_map/ppermute | solution.py:959
  768.1 2.5 collective-permute-start.42
  773.8 2.6 reshape.625
  777.0 4.6 collective-permute-done.42
  787.5 20.6 %reduce-scatter.14.cloned.1.call-done.refs_2_ = bf16[512,768]{1,0:T(8,128)(2,1)} async-done(((bf16[4096,768]{1,0:T(8,128)(2,1)}), bf16[512,768]{1,0:T(8,128)(2,1)}) %reduce-scatter.14.cloned.1.call-update) | async-done | bytes 786448 | tf_op jit(solution)/shard_map/reduce_scatter | solution.py:1386
  808.2 1.7 copy-done.1
  812.1 4.5 input_grads.1
  (406 shorter events, 79.6 us)
Async XLA Ops:
  7.2 118.9 %all-gather.7.cloned.1.call-start = ((), (), s32[]{:S(2)}) async-start(), calls=%async_computation.10 | async-start | bytes 7077888 | tf_op jit(solution)/shard_map/all_gather | solution.py:1153
  10.3 167.2 %all-gather.9.cloned.1.call-start = ((), (), s32[]{:S(2)}) async-start(), calls=%async_computation.11 | async-start | bytes 7077888 | tf_op jit(solution)/shard_map/all_gather | solution.py:1153
  11.1 233.4 %all-gather.11.cloned.1.call-start = ((), (), s32[]{:S(2)}) async-start(), calls=%async_computation.12 | async-start | bytes 7077888 | tf_op jit(solution)/shard_map/all_gather | solution.py:1153
  14.3 35.7 %collective-permute-start = (bf16[24,3456]{1,0:T(8,128)(2,1)S(1)}, bf16[24,3456]{1,0:T(8,128)(2,1)S(1)}, u32[]{:S(2)}, u32[]{:S(2)}) collective-permute-start(bf16[24,3456]{1,0:T(8,128)(2,1)S(1)} %get-tuple-element.363), channel_id=1, source_target_pairs={{0,1},{1,0},{2,3},{3,2},{4,5},{5,4},{6,7},{7,6},{8,9},{9,8},{10,11... | collective-permute-start | bytes 497672 | tf_op jit(solution)/shard_map/ppermute | solution.py:959
  16.9 9.6 %collective-permute-start.1 = (bf16[24,1280]{1,0:T(8,128)(2,1)S(1)}, bf16[24,1280]{1,0:T(8,128)(2,1)S(1)}, u32[]{:S(2)}, u32[]{:S(2)}) collective-permute-start(bf16[24,1280]{1,0:T(8,128)(2,1)S(1)} %pad_maximum_fusion.17), channel_id=1, source_target_pairs={{0,1},{1,0},{2,3},{3,2},{4,5},{5,4},{6,7},{7,6},{8,9},{9,8},{10,11... | collective-permute-start | bytes 184328 | tf_op jit(solution)/shard_map/ppermute | solution.py:959
  17.5 97.1 %collective-permute-start.7 = (bf16[3,256,768]{2,1,0:T(8,128)(2,1)S(1)}, bf16[3,256,768]{2,1,0:T(8,128)(2,1)}, u32[]{:S(2)}, u32[]{:S(2)}) collective-permute-start(bf16[3,256,768]{2,1,0:T(8,128)(2,1)S(1)} %copy-done.6), channel_id=1, source_target_pairs={{0,1},{1,0},{2,3},{3,2},{4,5},{5,4},{6,7},{7,6},{8,9},{9,8},{10,11... | collective-permute-start | bytes 3538952 | tf_op jit(solution)/shard_map/ppermute | solution.py:959
  17.6 517.6 %reduce-scatter.8.cloned.1.call-start = ((), (), s32[]{:S(2)}) async-start(), calls=%async_computation.6 | async-start | bytes 9289728 | tf_op jit(solution)/shard_map/reduce_scatter | solution.py:1358
  50.2 28.7 %collective-permute-start.3 = (bf16[96,1280]{1,0:T(8,128)(2,1)S(1)}, bf16[96,1280]{1,0:T(8,128)(2,1)S(1)}, u32[]{:S(2)}, u32[]{:S(2)}) collective-permute-start(bf16[96,1280]{1,0:T(8,128)(2,1)S(1)} %get-tuple-element.350), channel_id=1, source_target_pairs={{0,16},{8,24},{16,0},{24,8},{1,17},{9,25},{17,1},{25,9},{2,18},{10... | collective-permute-start | bytes 737288 | tf_op jit(solution)/shard_map/ppermute | solution.py:959
  52.4 26.6 %collective-permute-start.2 = (bf16[96,1280]{1,0:T(8,128)(2,1)S(1)}, bf16[96,1280]{1,0:T(8,128)(2,1)S(1)}, u32[]{:S(2)}, u32[]{:S(2)}) collective-permute-start(bf16[96,1280]{1,0:T(8,128)(2,1)S(1)} %get-tuple-element.351), channel_id=1, source_target_pairs={{0,8},{8,0},{16,24},{24,16},{1,9},{9,1},{17,25},{25,17},{2,10},{10... | collective-permute-start | bytes 737288 | tf_op jit(solution)/shard_map/ppermute | solution.py:959
  79.1 26.5 %collective-permute-start.4 = (bf16[2,96,1280]{2,1,0:T(8,128)(2,1)S(1)}, bf16[2,96,1280]{2,1,0:T(8,128)(2,1)S(1)}, u32[]{:S(2)}, u32[]{:S(2)}) collective-permute-start(bf16[2,96,1280]{2,1,0:T(8,128)(2,1)S(1)} %pad_maximum_fusion.12), channel_id=1, source_target_pairs={{0,16},{8,24},{16,0},{24,8},{1,17},{9,25},{17,1},{25,9},{2,18},{10... | collective-permute-start | bytes 1474568 | tf_op jit(solution)/shard_map/ppermute | solution.py:959
  79.5 26.1 %collective-permute-start.5 = (bf16[2,96,1280]{2,1,0:T(8,128)(2,1)S(1)}, bf16[2,96,1280]{2,1,0:T(8,128)(2,1)S(1)}, u32[]{:S(2)}, u32[]{:S(2)}) collective-permute-start(bf16[2,96,1280]{2,1,0:T(8,128)(2,1)S(1)} %pad_maximum_fusion.13), channel_id=1, source_target_pairs={{0,8},{8,0},{16,24},{24,16},{1,9},{9,1},{17,25},{25,17},{2,10},{10... | collective-permute-start | bytes 1474568 | tf_op jit(solution)/shard_map/ppermute | solution.py:959
  106.9 14.5 %collective-permute-start.12 = (bf16[96,3456]{1,0:T(8,128)(2,1)}, bf16[96,3456]{1,0:T(8,128)(2,1)}, u32[]{:S(2)}, u32[]{:S(2)}) collective-permute-start(bf16[96,3456]{1,0:T(8,128)(2,1)} %get-tuple-element.320), channel_id=1, source_target_pairs={{0,16},{8,24},{16,0},{24,8},{1,17},{9,25},{17,1},{25,9},{2,18},{10... | collective-permute-start | bytes 1990664 | tf_op jit(solution)/shard_map/ppermute | solution.py:959
  108.4 15.3 %collective-permute-start.11 = (bf16[96,3456]{1,0:T(8,128)(2,1)}, bf16[96,3456]{1,0:T(8,128)(2,1)}, u32[]{:S(2)}, u32[]{:S(2)}) collective-permute-start(bf16[96,3456]{1,0:T(8,128)(2,1)} %get-tuple-element.321), channel_id=1, source_target_pairs={{0,8},{8,0},{16,24},{24,16},{1,9},{9,1},{17,25},{25,17},{2,10},{10... | collective-permute-start | bytes 1990664 | tf_op jit(solution)/shard_map/ppermute | solution.py:959
  177.5 61.3 %collective-permute-start.16 = (bf16[2,96,3456]{2,1,0:T(8,128)(2,1)}, bf16[2,96,3456]{2,1,0:T(8,128)(2,1)S(1)}, u32[]{:S(2)}, u32[]{:S(2)}) collective-permute-start(bf16[2,96,3456]{2,1,0:T(8,128)(2,1)} %pad_maximum_fusion.5.refs_12_), channel_id=1, source_target_pairs={{0,16},{8,24},{16,0},{24,8},{1,17},{9,25},{17,1},{25,9},{2,18},{10... | collective-permute-start | bytes 3981320 | tf_op jit(solution)/shard_map/ppermute | solution.py:959
  179.0 61.9 %collective-permute-start.17 = (bf16[2,96,3456]{2,1,0:T(8,128)(2,1)S(1)}, bf16[2,96,3456]{2,1,0:T(8,128)(2,1)S(1)}, u32[]{:S(2)}, u32[]{:S(2)}) collective-permute-start(bf16[2,96,3456]{2,1,0:T(8,128)(2,1)S(1)} %copy-done.22), channel_id=1, source_target_pairs={{0,8},{8,0},{16,24},{24,16},{1,9},{9,1},{17,25},{25,17},{2,10},{10... | collective-permute-start | bytes 3981320 | tf_op jit(solution)/shard_map/ppermute | solution.py:959
  233.0 12.0 %collective-permute-start.13 = (bf16[512,384]{1,0:T(8,128)(2,1)S(1)}, bf16[512,384]{1,0:T(8,128)(2,1)}, u32[]{:S(2)}, u32[]{:S(2)}) collective-permute-start(bf16[512,384]{1,0:T(8,128)(2,1)S(1)} %get-tuple-element.335), channel_id=1, source_target_pairs={{0,0},{1,3},{2,2},{3,1},{4,4},{5,7},{6,6},{7,5},{8,8},{9,11},{10,1... | collective-permute-start | bytes 1179656 | tf_op jit(solution)/shard_map/ppermute | solution.py:1234
  234.4 10.8 %collective-permute-start.14 = (bf16[512,384]{1,0:T(8,128)(2,1)S(1)}, bf16[512,384]{1,0:T(8,128)(2,1)}, u32[]{:S(2)}, u32[]{:S(2)}) collective-permute-start(bf16[512,384]{1,0:T(8,128)(2,1)S(1)} %get-tuple-element.334), channel_id=1, source_target_pairs={{0,3},{1,0},{2,1},{3,2},{4,7},{5,4},{6,5},{7,6},{8,11},{9,8},{10,9... | collective-permute-start | bytes 1179656 | tf_op jit(solution)/shard_map/ppermute | solution.py:1236
  234.5 11.3 %collective-permute-start.8 = (bf16[512,384]{1,0:T(8,128)(2,1)S(1)}, bf16[512,384]{1,0:T(8,128)(2,1)}, u32[]{:S(2)}, u32[]{:S(2)}) collective-permute-start(bf16[512,384]{1,0:T(8,128)(2,1)S(1)} %get-tuple-element.339), channel_id=1, source_target_pairs={{0,0},{1,3},{2,2},{3,1},{4,4},{5,7},{6,6},{7,5},{8,8},{9,11},{10,1... | collective-permute-start | bytes 1179656 | tf_op jit(solution)/shard_map/ppermute | solution.py:1234
  244.4 57.2 %collective-permute-start.21 = (bf16[2,96,3456]{2,1,0:T(8,128)(2,1)}, bf16[2,96,3456]{2,1,0:T(8,128)(2,1)S(1)}, u32[]{:S(2)}, u32[]{:S(2)}) collective-permute-start(bf16[2,96,3456]{2,1,0:T(8,128)(2,1)} %pad_maximum_fusion.5.refs_12_), channel_id=1, source_target_pairs={{0,1},{1,0},{2,3},{3,2},{4,5},{5,4},{6,7},{7,6},{8,9},{9,8},{10,11... | collective-permute-start | bytes 3981320 | tf_op jit(solution)/shard_map/ppermute | solution.py:959
  244.4 60.9 %collective-permute-start.23 = (bf16[2,96,3456]{2,1,0:T(8,128)(2,1)S(1)}, bf16[2,96,3456]{2,1,0:T(8,128)(2,1)S(1)}, u32[]{:S(2)}, u32[]{:S(2)}) collective-permute-start(bf16[2,96,3456]{2,1,0:T(8,128)(2,1)S(1)} %copy-done.22), channel_id=1, source_target_pairs={{0,1},{1,0},{2,3},{3,2},{4,5},{5,4},{6,7},{7,6},{8,9},{9,8},{10,11... | collective-permute-start | bytes 3981320 | tf_op jit(solution)/shard_map/ppermute | solution.py:959
  244.9 55.3 %collective-permute-start.9 = (bf16[512,384]{1,0:T(8,128)(2,1)S(1)}, bf16[512,384]{1,0:T(8,128)(2,1)S(1)}, u32[]{:S(2)}, u32[]{:S(2)}) collective-permute-start(bf16[512,384]{1,0:T(8,128)(2,1)S(1)} %get-tuple-element.338), channel_id=1, source_target_pairs={{0,3},{1,0},{2,1},{3,2},{4,7},{5,4},{6,5},{7,6},{8,11},{9,8},{10,9... | collective-permute-start | bytes 1179656 | tf_op jit(solution)/shard_map/ppermute | solution.py:1236
  245.2 66.1 %collective-permute-start.22 = (bf16[2,96,3456]{2,1,0:T(8,128)(2,1)}, bf16[2,96,3456]{2,1,0:T(8,128)(2,1)}, u32[]{:S(2)}, u32[]{:S(2)}) collective-permute-start(bf16[2,96,3456]{2,1,0:T(8,128)(2,1)} %copy-done.37), channel_id=1, source_target_pairs={{0,1},{1,0},{2,3},{3,2},{4,5},{5,4},{6,7},{7,6},{8,9},{9,8},{10,11... | collective-permute-start | bytes 3981320 | tf_op jit(solution)/shard_map/ppermute | solution.py:959
  245.8 65.6 %collective-permute-start.24 = (bf16[2,96,3456]{2,1,0:T(8,128)(2,1)}, bf16[2,96,3456]{2,1,0:T(8,128)(2,1)}, u32[]{:S(2)}, u32[]{:S(2)}) collective-permute-start(bf16[2,96,3456]{2,1,0:T(8,128)(2,1)} %copy-done.38), channel_id=1, source_target_pairs={{0,1},{1,0},{2,3},{3,2},{4,5},{5,4},{6,7},{7,6},{8,9},{9,8},{10,11... | collective-permute-start | bytes 3981320 | tf_op jit(solution)/shard_map/ppermute | solution.py:959
  300.2 7.6 collective-permute-start.18
  301.7 9.7 %collective-permute-start.19 = (bf16[512,384]{1,0:T(8,128)(2,1)S(1)}, bf16[512,384]{1,0:T(8,128)(2,1)}, u32[]{:S(2)}, u32[]{:S(2)}) collective-permute-start(bf16[512,384]{1,0:T(8,128)(2,1)S(1)} %get-tuple-element.324), channel_id=1, source_target_pairs={{0,3},{1,0},{2,1},{3,2},{4,7},{5,4},{6,5},{7,6},{8,11},{9,8},{10,9... | collective-permute-start | bytes 1179656 | tf_op jit(solution)/shard_map/ppermute | solution.py:1236
  426.2 6.5 collective-permute-start.25
  427.0 14.0 %collective-permute-start.26 = (bf16[512,384]{1,0:T(8,128)(2,1)S(1)}, bf16[512,384]{1,0:T(8,128)(2,1)S(1)}, u32[]{:S(2)}, u32[]{:S(2)}) collective-permute-start(bf16[512,384]{1,0:T(8,128)(2,1)S(1)} %get-tuple-element.309), channel_id=1, source_target_pairs={{3,0},{0,1},{1,2},{2,3},{7,4},{4,5},{5,6},{6,7},{11,8},{8,9},{9,10... | collective-permute-start | bytes 1179656 | tf_op jit(solution)/shard_map/ppermute | solution.py:1244
  441.7 186.2 %reduce-scatter.12.cloned.1.call-start = ((), (), s32[]{:S(2)}) async-start(), calls=%async_computation.8 | async-start | bytes 2654208 | tf_op jit(solution)/shard_map/reduce_scatter | solution.py:1358
  441.8 90.2 %collective-permute-start.28 = (bf16[512,384]{1,0:T(8,128)(2,1)S(1)}, bf16[512,384]{1,0:T(8,128)(2,1)}, u32[]{:S(2)}, u32[]{:S(2)}) collective-permute-start(bf16[512,384]{1,0:T(8,128)(2,1)S(1)} %get-tuple-element.314), channel_id=1, source_target_pairs={{0,0},{3,1},{2,2},{1,3},{4,4},{7,5},{6,6},{5,7},{8,8},{11,9},{10,1... | collective-permute-start | bytes 1179656 | tf_op jit(solution)/shard_map/ppermute | solution.py:1242
  443.2 88.8 %collective-permute-start.29 = (bf16[512,384]{1,0:T(8,128)(2,1)S(1)}, bf16[512,384]{1,0:T(8,128)(2,1)}, u32[]{:S(2)}, u32[]{:S(2)}) collective-permute-start(bf16[512,384]{1,0:T(8,128)(2,1)S(1)} %get-tuple-element.308), channel_id=1, source_target_pairs={{3,0},{0,1},{1,2},{2,3},{7,4},{4,5},{5,6},{6,7},{11,8},{8,9},{9,10... | collective-permute-start | bytes 1179656 | tf_op jit(solution)/shard_map/ppermute | solution.py:1244
  443.2 88.7 %collective-permute-start.30 = (bf16[256,384]{1,0:T(8,128)(2,1)S(1)}, bf16[256,384]{1,0:T(8,128)(2,1)}, u32[]{:S(2)}, u32[]{:S(2)}) collective-permute-start(bf16[256,384]{1,0:T(8,128)(2,1)S(1)} %get-tuple-element.305), channel_id=1, source_target_pairs={{0,1},{1,0},{2,3},{3,2},{4,5},{5,4},{6,7},{7,6},{8,9},{9,8},{10,11... | collective-permute-start | bytes 589832 | tf_op jit(solution)/shard_map/ppermute | solution.py:959
  444.0 285.8 %reduce-scatter.6.cloned.1.call-start = ((), (), s32[]{:S(2)}) async-start(), calls=%async_computation.5 | async-start | bytes 7077888 | tf_op jit(solution)/shard_map/reduce_scatter | solution.py:1371
  532.0 197.8 %reduce-scatter.10.cloned.1.call-start = ((), (), s32[]{:S(2)}) async-start(), calls=%async_computation.7 | async-start | bytes 7077888 | tf_op jit(solution)/shard_map/reduce_scatter | solution.py:1371
  532.0 90.8 %collective-permute-start.31 = (bf16[512,384]{1,0:T(8,128)(2,1)S(1)}, bf16[512,384]{1,0:T(8,128)(2,1)S(1)}, u32[]{:S(2)}, u32[]{:S(2)}) collective-permute-start(bf16[512,384]{1,0:T(8,128)(2,1)S(1)} %get-tuple-element.313), channel_id=1, source_target_pairs={{0,0},{3,1},{2,2},{1,3},{4,4},{7,5},{6,6},{5,7},{8,8},{11,9},{10,1... | collective-permute-start | bytes 1179656 | tf_op jit(solution)/shard_map/ppermute | solution.py:1242
  532.7 90.1 %collective-permute-start.32 = (bf16[512,384]{1,0:T(8,128)(2,1)S(1)}, bf16[512,384]{1,0:T(8,128)(2,1)S(1)}, u32[]{:S(2)}, u32[]{:S(2)}) collective-permute-start(bf16[512,384]{1,0:T(8,128)(2,1)S(1)} %get-tuple-element.307), channel_id=1, source_target_pairs={{3,0},{0,1},{1,2},{2,3},{7,4},{4,5},{5,6},{6,7},{11,8},{8,9},{9,10... | collective-permute-start | bytes 1179656 | tf_op jit(solution)/shard_map/ppermute | solution.py:1244
  535.2 87.7 %collective-permute-start.33 = (bf16[256,384]{1,0:T(8,128)(2,1)S(1)}, bf16[256,384]{1,0:T(8,128)(2,1)S(1)}, u32[]{:S(2)}, u32[]{:S(2)}) collective-permute-start(bf16[256,384]{1,0:T(8,128)(2,1)S(1)} %get-tuple-element.304), channel_id=1, source_target_pairs={{0,1},{1,0},{2,3},{3,2},{4,5},{5,4},{6,7},{7,6},{8,9},{9,8},{10,11... | collective-permute-start | bytes 589832 | tf_op jit(solution)/shard_map/ppermute | solution.py:959
  623.9 184.3 %reduce-scatter.14.cloned.1.call-start = ((), (), s32[]{:S(2)}) async-start(), calls=%async_computation.9 | async-start | bytes 7077888 | tf_op jit(solution)/shard_map/reduce_scatter | solution.py:1386
  627.5 106.6 %collective-permute-start.34 = (bf16[256,768]{1,0:T(8,128)(2,1)}, bf16[256,768]{1,0:T(8,128)(2,1)}, u32[]{:S(2)}, u32[]{:S(2)}) collective-permute-start(bf16[256,768]{1,0:T(8,128)(2,1)} %slice.475), channel_id=1, source_target_pairs={{0,1},{1,0},{2,3},{3,2},{4,5},{5,4},{6,7},{7,6},{8,9},{9,8},{10,11... | collective-permute-start | bytes 1179656 | tf_op jit(solution)/shard_map/ppermute | solution.py:959
  720.2 11.0 %collective-permute-start.44 = (bf16[2,24,3456]{2,1,0:T(8,128)(2,1)}, bf16[2,24,3456]{2,1,0:T(8,128)(2,1)}, u32[]{:S(2)}, u32[]{:S(2)}) collective-permute-start(bf16[2,24,3456]{2,1,0:T(8,128)(2,1)} %dynamic-slice_bitcast_fusion.7), channel_id=1, source_target_pairs={{0,8},{8,0},{16,24},{24,16},{1,9},{9,1},{17,25},{25,17},{2,10},{10... | collective-permute-start | bytes 995336 | tf_op jit(solution)/shard_map/ppermute | solution.py:959
  721.6 11.0 %collective-permute-start.46 = (bf16[2,24,3456]{2,1,0:T(8,128)(2,1)}, bf16[2,24,3456]{2,1,0:T(8,128)(2,1)}, u32[]{:S(2)}, u32[]{:S(2)}) collective-permute-start(bf16[2,24,3456]{2,1,0:T(8,128)(2,1)} %dynamic-slice_bitcast_fusion.6), channel_id=1, source_target_pairs={{0,16},{8,24},{16,0},{24,8},{1,17},{9,25},{17,1},{25,9},{2,18},{10... | collective-permute-start | bytes 995336 | tf_op jit(solution)/shard_map/ppermute | solution.py:959
  724.1 17.6 %collective-permute-start.37 = (bf16[2,96,1280]{2,1,0:T(8,128)(2,1)}, bf16[2,96,1280]{2,1,0:T(8,128)(2,1)}, u32[]{:S(2)}, u32[]{:S(2)}) collective-permute-start(bf16[2,96,1280]{2,1,0:T(8,128)(2,1)} %dynamic-slice_bitcast_fusion.1), channel_id=1, source_target_pairs={{0,8},{8,0},{16,24},{24,16},{1,9},{9,1},{17,25},{25,17},{2,10},{10... | collective-permute-start | bytes 1474568 | tf_op jit(solution)/shard_map/ppermute | solution.py:959
  726.9 17.7 %collective-permute-start.39 = (bf16[2,96,1280]{2,1,0:T(8,128)(2,1)}, bf16[2,96,1280]{2,1,0:T(8,128)(2,1)}, u32[]{:S(2)}, u32[]{:S(2)}) collective-permute-start(bf16[2,96,1280]{2,1,0:T(8,128)(2,1)} %dynamic-slice_bitcast_fusion), channel_id=1, source_target_pairs={{0,16},{8,24},{16,0},{24,8},{1,17},{9,25},{17,1},{25,9},{2,18},{10... | collective-permute-start | bytes 1474568 | tf_op jit(solution)/shard_map/ppermute | solution.py:959
  734.1 12.6 %collective-permute-start.45 = (bf16[24,3456]{1,0:T(8,128)(2,1)S(1)}, bf16[24,3456]{1,0:T(8,128)(2,1)S(1)}, u32[]{:S(2)}, u32[]{:S(2)}) collective-permute-start(bf16[24,3456]{1,0:T(8,128)(2,1)S(1)} %dynamic-slice_bitcast_fusion.12), channel_id=1, source_target_pairs={{0,16},{8,24},{16,0},{24,8},{1,17},{9,25},{17,1},{25,9},{2,18},{10... | collective-permute-start | bytes 497672 | tf_op jit(solution)/shard_map/ppermute | solution.py:959
  734.8 19.0 %collective-permute-start.47 = (bf16[24,3456]{1,0:T(8,128)(2,1)S(1)}, bf16[24,3456]{1,0:T(8,128)(2,1)S(1)}, u32[]{:S(2)}, u32[]{:S(2)}) collective-permute-start(bf16[24,3456]{1,0:T(8,128)(2,1)S(1)} %dynamic-slice_bitcast_fusion.11), channel_id=1, source_target_pairs={{0,8},{8,0},{16,24},{24,16},{1,9},{9,1},{17,25},{25,17},{2,10},{10... | collective-permute-start | bytes 497672 | tf_op jit(solution)/shard_map/ppermute | solution.py:959
  743.1 8.0 collective-permute-start.38
  745.8 7.5 collective-permute-start.40
  753.4 13.9 %collective-permute-start.41 = (bf16[2,48,1280]{2,1,0:T(8,128)(2,1)S(1)}, bf16[2,48,1280]{2,1,0:T(8,128)(2,1)S(1)}, u32[]{:S(2)}, u32[]{:S(2)}) collective-permute-start(bf16[2,48,1280]{2,1,0:T(8,128)(2,1)S(1)} %dynamic-slice_bitcast_fusion.8), channel_id=1, source_target_pairs={{0,2},{1,3},{2,0},{3,1},{4,6},{5,7},{6,4},{7,5},{8,10},{9,11},{10,... | collective-permute-start | bytes 737288 | tf_op jit(solution)/shard_map/ppermute | solution.py:959
  768.1 13.5 %collective-permute-start.42 = (bf16[48,1280]{1,0:T(8,128)(2,1)}, bf16[48,1280]{1,0:T(8,128)(2,1)}, u32[]{:S(2)}, u32[]{:S(2)}) collective-permute-start(bf16[48,1280]{1,0:T(8,128)(2,1)} %dynamic-slice_bitcast_fusion.13), channel_id=1, source_target_pairs={{0,4},{1,5},{2,6},{3,7},{4,0},{5,1},{6,2},{7,3},{8,12},{9,13},{10,... | collective-permute-start | bytes 368648 | tf_op jit(solution)/shard_map/ppermute | solution.py:959
  (66 other events, 439.0 us)
Sparse Core Ops, SparseCore 0:
  10.4 95.1 all-gather.6
  107.8 63.5 all-gather.8
  173.6 63.5 all-gather.10
  441.9 90.0 reduce-scatter.7
  534.2 38.2 reduce-scatter.11
  574.7 70.2 reduce-scatter.5
  647.5 68.1 reduce-scatter.9
  730.0 78.1 reduce-scatter.13
